TPU v7x, 512 devices: a whole 4x4x16 slice. The times are simulated.
512 devices in a mesh: frames: 32 (over z, core), phon: 4 (over y), chap: 4 (over x).
Axes of the slice: x: 4, y: 4, z: 16, core: 2. Of those that a mesh axis runs over, the one named last changes fastest.
Arguments:
- queries: bfloat16 [65536, 512], P(('chap', 'frames')), parts along dimension 0, may hold values from -80 to 80
- keys: bfloat16 [16384, 512], P(('chap', 'phon', 'frames')), parts along dimension 0, may hold values from -7 to 7
- values: bfloat16 [16384, 512], P(('chap', 'phon', 'frames')), parts along dimension 0, may hold values from -6 to 6
- band_first: int32 [128], P(('chap', 'frames')), parts along dimension 0, may hold values from 0 to 6, as said below
- cotangent: bfloat16 [65536, 512], P(('chap', 'frames')), parts along dimension 0, may hold values from -6 to 6
Outputs:
- aligned: bfloat16 [65536, 512], P(('chap', 'frames')), parts along dimension 0
- grad_query: bfloat16 [65536, 512], P(('chap', 'frames')), parts along dimension 0
- grad_key: float32 [16384, 512], P(('chap', 'phon', 'frames')), parts along dimension 0
- grad_value: float32 [16384, 512], P(('chap', 'phon', 'frames')), parts along dimension 0
There are 4 independent parts, one for each index of `chap`. A program takes and returns all parts, laid end to end along the dimension named above; each array names one. Nothing has to cross between parts.
Inputs may be any that keep to these rules, and one draw needn't show every extreme that they name: Query tile i attends the key tiles band_first[i] to band_first[i] + 1.
All inputs are finite; a program needn't handle non-finite values.
Results may differ from a plain program's by a relative error of at most 0.022.
Values may be sent and summed in bfloat16 or wider, within the bound.
No kernel may reach another device: no remote copies, remote signals or barrier semaphores. Data moves between devices by JAX's collectives and lax.ppermute only.
A program may use at most 64 MiB of HBM per device.

v0:
```python
import jax
import jax.numpy as jnp
from jax import lax
from jax.sharding import PartitionSpec as P

TILE = 512
NBAND = 2


NEG_FILL = -1e30


def in_one_piece(arrays, axis, dim, along):
    both = jnp.concatenate(arrays, axis=along)
    result, at, finished = (lax.all_gather(both, axis, axis=dim, tiled=True), 0, [])
    for a in arrays:
        finished.append(lax.slice_in_dim(result, at, at + a.shape[along], axis=along))
        at += a.shape[along]
    return tuple(finished)


def sent_to_all(value, axis):
    length = lax.axis_size(axis)
    return lax.all_to_all(
        jnp.broadcast_to(value[None], (length, *value.shape)), axis, 0, 0, tiled=True
    )


def of_everyone(value, axis):
    return sent_to_all(value, axis).max(axis=0)


def together(arrays, axis):
    ends = [0]
    for a in arrays:
        ends.append(ends[-1] + a.size)
    total = lax.psum(jnp.concatenate([a.ravel() for a in arrays]), axis)
    return tuple((total[b:e].reshape(a.shape) for a, b, e in zip(arrays, ends, ends[1:])))


def over_copies(value, axis):
    everything = sent_to_all(value, axis)
    return jnp.sum(everything.astype(jnp.float32), axis=0)


def side_by_side(arrays, axis, dim, along):
    ends, at = ([], 0)
    for a in arrays[:-1]:
        at += a.shape[along]
        ends.append(at)
    both = jnp.concatenate(arrays, axis=along)
    return tuple(
        jnp.split(lax.psum_scatter(both, axis, scatter_dimension=dim, tiled=True), ends, axis=along)
    )


def body(queries, keys, values, band_first, cotangent):
    width = queries.shape[1]
    scale = width ** (-0.5)
    block_keys, block_values = in_one_piece((keys, values), "frames", 0, 1)
    block = block_keys.shape[0]
    first_tile = lax.axis_index("phon") * (block // TILE)
    key_tile = first_tile + jnp.arange(block, dtype=jnp.int32) // TILE
    row_first = jnp.repeat(band_first, TILE)
    allowed = (key_tile[None, :] >= row_first[:, None]) & (
        key_tile[None, :] < row_first[:, None] + NBAND
    )
    key_float = block_keys.astype(jnp.float32)
    key_sq = jnp.sum(key_float * key_float, axis=1)
    raw = (
        jnp.dot(queries, block_keys.T, preferred_element_type=jnp.float32) - 0.5 * key_sq[None, :]
    ) * scale
    scores = jnp.where(allowed, raw, NEG_FILL)
    local_max = jnp.max(scores, axis=1)
    row_max = of_everyone(local_max, "phon")
    expd = jnp.where(allowed, jnp.exp(scores - row_max[:, None]), 0.0)
    part_total = jnp.sum(expd, axis=1)
    part_out = jnp.dot(expd.astype(jnp.bfloat16), block_values, preferred_element_type=jnp.float32)
    total, summed = together((part_total, part_out), "phon")
    aligned_f = summed / total[:, None]
    lse = row_max + jnp.log(total)
    back_keys, back_values = (block_keys, block_values)
    probs = jnp.where(allowed, jnp.exp(scores - lse[:, None]), 0.0)
    d_probs = jnp.dot(cotangent, back_values.T, preferred_element_type=jnp.float32)
    delta = jnp.sum(cotangent.astype(jnp.float32) * aligned_f, axis=1)
    d_scores = probs * (d_probs - delta[:, None])
    ds_low = d_scores.astype(jnp.bfloat16)
    part_query = jnp.dot(ds_low, back_keys, preferred_element_type=jnp.float32) * scale
    grad_query = (
        over_copies(part_query.astype(jnp.bfloat16), "phon")
        .astype(jnp.float32)
        .astype(jnp.bfloat16)
    )
    column_sum = jnp.sum(d_scores, axis=0)
    part_key = (
        jnp.einsum("qk,qd->kd", ds_low, queries, preferred_element_type=jnp.float32)
        - column_sum[:, None] * back_keys.astype(jnp.float32)
    ) * scale
    part_value = jnp.einsum(
        "qk,qd->kd", probs.astype(jnp.bfloat16), cotangent, preferred_element_type=jnp.float32
    )
    grad_key, grad_value = tuple(
        (
            part.astype(jnp.float32)
            for part in side_by_side(
                (part_key.astype(jnp.bfloat16), part_value.astype(jnp.bfloat16)), "frames", 0, 1
            )
        )
    )
    return (aligned_f.astype(jnp.bfloat16), grad_query, grad_key, grad_value)


def solution(mesh):
    in_specs = (
        P(("chap", "frames"), None),
        P(("chap", "phon", "frames"), None),
        P(("chap", "phon", "frames"), None),
        P(("chap", "frames")),
        P(("chap", "frames"), None),
    )
    out_specs = (
        P(("chap", "frames"), None),
        P(("chap", "frames"), None),
        P(("chap", "phon", "frames"), None),
        P(("chap", "phon", "frames"), None),
    )
    return jax.shard_map(body, mesh=mesh, in_specs=in_specs, out_specs=out_specs, check_vma=False)
```

profile of v0, /device:TPU:6, one launch (start us, length us, event | category | flops | bytes accessed | tf_op | source)
XLA Modules:
  0.0 291.0 jit_solution(5057413454272372290)
XLA Ops:
  7.2 0.0 copy-start
  7.2 0.0 all-gather.2.cloned.1.call-start
  7.2 1.5 pad_maximum_fusion.2
  8.7 0.0 all-gather.2.cloned.1.call-update
  8.7 0.0 all-reduce.2.cloned.1.call-start
  9.4 77.1 %all-gather.2.cloned.1.call-done = bf16[1024,1024]{1,0:T(8,128)(2,1)} async-done(((bf16[32,1024]{1,0:T(8,128)(2,1)}), bf16[1024,1024]{1,0:T(8,128)(2,1)}) %all-gather.2.cloned.1.call-update) | async-done | bytes 2097168 | tf_op jit(solution)/shard_map/all_gather | solution.py:15
  86.6 1.5 fusion
  88.1 0.0 copy-done
  88.1 2.0 fusion.32
  90.1 0.0 copy-start.1
  90.1 9.4 %all_to_all.11 = f32[4,1,512]{2,1,0:T(1,128)S(1)} all-to-all(f32[4,1,512]{2,1,0:T(1,128)S(1)} %broadcast_in_dim.13), channel_id=1, replica_groups=mesh['frames'=32,'phon'=4,'chap'=4] {'phon'}, dimensions={0} | all-to-all | bytes 16384 | tf_op jit(solution)/shard_map/all_to_all | solution.py:24
  99.6 0.0 copy-start.3
  99.6 0.4 fusion.4
  100.0 1.2 copy-done.3
  101.1 0.9 convolution_bitcast_fusion
  102.0 0.0 copy-done.1
  102.0 0.3 copy.23
  102.3 1.1 pad_maximum_fusion.1
  103.4 0.0 all-reduce.2.cloned.1.call-update
  103.4 0.0 copy-start.6
  103.4 0.0 reduce-scatter.2.cloned.1.call-start
  103.5 57.0 %all-reduce.2.cloned.1.call-done = f32[262656]{0:T(1024)} async-done(((f32[262656]{0:T(1024)}), f32[262656]{0:T(1024)}) %all-reduce.2.cloned.1.call-update) | async-done | bytes 1050640 | tf_op jit(solution)/shard_map/psum | solution.py:37
  160.5 1.3 slice.29
  161.8 0.2 slice.25
  162.0 0.7 log_add_fusion
  162.7 0.0 copy-done.6
  162.7 0.0 copy-start.4
  162.7 2.5 convolution_convert_fusion
  165.2 0.0 copy-start.2
  165.2 1.0 multiply_reduce_fusion
  166.2 0.0 copy-done.4
  166.2 0.7 copy-done.2
  167.0 1.1 fusion.33
  168.0 0.0 copy-start.7
  168.0 0.7 fusion.3
  168.7 0.2 copy-done.7
  169.0 1.6 pad_maximum_fusion
  170.6 0.0 copy-start.5
  170.6 0.0 reduce-scatter.2.cloned.1.call-update
  170.6 1.6 copy-done.5
  172.1 2.0 fusion.7
  174.1 0.2 broadcast_in_dim.15
  174.3 27.8 %all_to_all.12 = bf16[4,512,512]{2,1,0:T(8,128)(2,1)S(1)} all-to-all(bf16[4,512,512]{2,1,0:T(8,128)(2,1)S(1)} %broadcast_in_dim.15), channel_id=1, replica_groups=mesh['frames'=32,'phon'=4,'chap'=4] {'phon'}, dimensions={0} | all-to-all | bytes 4194304 | tf_op jit(solution)/shard_map/all_to_all | solution.py:24
  202.1 1.2 reduce_sum.51
  203.3 79.7 %reduce-scatter.2.cloned.1.call-done = bf16[32,1024]{1,0:T(8,128)(2,1)} async-done(((bf16[1024,1024]{1,0:T(8,128)(2,1)}), bf16[32,1024]{1,0:T(8,128)(2,1)}) %reduce-scatter.2.cloned.1.call-update) | async-done | bytes 65552 | tf_op jit(solution)/shard_map/reduce_scatter | solution.py:53
  283.0 1.4 slice_convert_fusion
  (4 shorter events, 0.0 us)
Async XLA Ops:
  7.2 80.9 %copy-start = (bf16[512,512]{1,0:T(8,128)(2,1)S(1)}, bf16[512,512]{1,0:T(8,128)(2,1)}, u32[]{:S(2)}) copy-start(bf16[512,512]{1,0:T(8,128)(2,1)} %param.5) | copy-start | bytes 1572868
  7.2 79.4 %all-gather.2.cloned.1.call-start = ((), (), s32[]{:S(2)}) async-start(), calls=%async_computation.3 | async-start | bytes 2162688 | tf_op jit(solution)/shard_map/all_gather | solution.py:15
  8.7 151.8 %all-reduce.2.cloned.1.call-start = ((), (), s32[]{:S(2)}) async-start(), calls=%async_computation.4 | async-start | bytes 2105344 | tf_op jit(solution)/shard_map/psum | solution.py:37
  90.1 11.9 %copy-start.1 = (f32[1024,512]{1,0:T(8,128)}, f32[1024,512]{1,0:T(8,128)S(1)}, u32[]{:S(2)}) copy-start(f32[1024,512]{1,0:T(8,128)S(1)} %get-tuple-element.11) | copy-start | bytes 6291460
  99.6 1.6 copy-start.3
  103.4 59.2 %copy-start.6 = (bf16[512,512]{1,0:T(8,128)(2,1)S(1)}, bf16[512,512]{1,0:T(8,128)(2,1)}, u32[]{:S(2)}) copy-start(bf16[512,512]{1,0:T(8,128)(2,1)} %param.9) | copy-start | bytes 1572868
  103.4 179.6 %reduce-scatter.2.cloned.1.call-start = ((), (), s32[]{:S(2)}) async-start(), calls=%async_computation.5 | async-start | bytes 2162688 | tf_op jit(solution)/shard_map/reduce_scatter | solution.py:53
  162.7 3.5 %copy-start.4 = (bf16[1024,1024]{1,0:T(8,128)(2,1)S(1)}, bf16[1024,1024]{1,0:T(8,128)(2,1)}, u32[]{:S(2)}) copy-start(bf16[1024,1024]{1,0:T(8,128)(2,1)} %all-gather.2.cloned.1.call-done) | copy-start | bytes 6291460
  165.2 1.8 copy-start.2
  168.0 1.0 copy-start.7
  170.6 1.6 copy-start.5
Sparse Core Ops, SparseCore 0:
  10.7 75.8 all-gather.1
  103.5 56.9 all-reduce.1
  170.7 112.2 reduce-scatter.1
where the time goes:
time: 292 us; the launch traced here: 291 us
  waiting for transfers between devices  214 us (73%)
  blocking collectives  37.2 us (13%)
  between operations  14.5 us (5%)
  other arithmetic  10.4 us (4%)
  matrix products  9.12 us (3%)
  local copies, waits for them, and re-layouts  5.67 us (2%)
    reduce_scatter x1, waiting for transfers between devices, side_by_side(): lax.psum_scatter(both, axis, scatter_dimension=dim, tiled=True)  79.7 us
    all_gather x1, waiting for transfers between devices, in_one_piece(): lax.all_gather(both, axis, axis=dim, tiled=True)  77.1 us
    psum x1, waiting for transfers between devices, together(): total = lax.psum(jnp.concatenate([a.ravel() for a in arrays]), axis)  57 us
    all_to_all x2, blocking collectives, sent_to_all(): lax.all_to_all(jnp.broadcast_to(value[None], (length, *value.shape)), axi...  37.2 us
  transfers between devices with their start and end apart: 3, of which 3 were waited for; matrix products, arithmetic and copies ran while one was open for 1% of the time, Pallas kernels for 0%

commit v1 on v0

v1 whole, which is shorter than its diff:
```python
import jax
import jax.numpy as jnp
import numpy as np
from jax import lax
from jax.sharding import PartitionSpec as P

TILE = 512
NBAND = 2
NEG_FILL = -1e30
LIFT = 4096.0


def chip_order(offset):
    return [[(4 * g + (k + g) % 4 + offset) % 16 for g in range(4)] for k in range(4)]


ORDERS = [chip_order(0), chip_order(2)]
QUADS = [[2 * ORDERS[c][k][g] + c for k in range(4)] for c in range(2) for g in range(4)]
CROSSES = [[2 * ORDERS[c][k][g] + c for g in range(4)] for c in range(2) for k in range(4)]


def gathered(keys, values):
    both = jnp.concatenate([keys, values], axis=1).astype(jnp.float32) * LIFT
    every = lax.all_gather(both.astype(jnp.float16), "frames", axis=0, tiled=True)
    every = (every.astype(jnp.float32) * (1.0 / LIFT)).astype(jnp.bfloat16)
    width = keys.shape[1]
    return every[:, :width], every[:, width:]


def to_all_phon(value):
    n = lax.axis_size("phon")
    return lax.all_to_all(
        jnp.broadcast_to(value[None], (n, *value.shape)), "phon", 0, 0, tiled=True
    )


def shifted(value, axis, d):
    n = lax.axis_size(axis)
    return lax.ppermute(value, axis, [(i, (i + d) % n) for i in range(n)])


def f32_sum(parts):
    total = parts[0].astype(jnp.float32)
    for part in parts[1:]:
        total = total + part.astype(jnp.float32)
    return total


def body(queries, keys, values, band_first, cotangent):
    f32, bf16 = jnp.float32, jnp.bfloat16
    rows, width = queries.shape
    own = keys.shape[0]
    scale = width ** (-0.5)
    phon = lax.axis_index("phon")
    frame = lax.axis_index("frames")
    core = frame % 2
    block_keys, block_values = gathered(keys, values)
    block = block_keys.shape[0]
    key_tile = phon * (block // TILE) + jnp.arange(block, dtype=jnp.int32) // TILE
    allowed = (key_tile >= band_first[0]) & (key_tile < band_first[0] + NBAND)
    allowed = allowed[None, :]
    key_float = block_keys.astype(f32)
    key_sq = jnp.sum(key_float * key_float, axis=1)
    raw = (
        jnp.dot(queries, block_keys.T, preferred_element_type=f32) - 0.5 * key_sq[None, :]
    ) * scale
    scores = jnp.where(allowed, raw, NEG_FILL)
    local_max = jnp.max(scores, axis=1)
    expd = jnp.where(allowed, jnp.exp(scores - local_max[:, None]), 0.0)
    d_probs = jnp.dot(cotangent, block_values.T, preferred_element_type=f32)
    part_total = jnp.sum(expd, axis=1)
    part_delta = jnp.sum(expd * d_probs, axis=1)
    stats = to_all_phon(jnp.stack([local_max, part_total, part_delta]))
    row_max = jnp.max(stats[:, 0], axis=0)
    weight = jnp.exp(stats[:, 0] - row_max[None, :])
    total = jnp.sum(weight * stats[:, 1], axis=0)
    delta = jnp.sum(weight * stats[:, 2], axis=0) / total
    share = jnp.exp(local_max - row_max) / total
    probs = expd * share[:, None]
    probs_low = probs.astype(bf16)
    part_out = jnp.dot(probs_low, block_values, preferred_element_type=f32)
    d_scores = probs * (d_probs - delta[:, None])
    ds_low = d_scores.astype(bf16)
    part_query = jnp.dot(ds_low, block_keys, preferred_element_type=f32) * scale
    column_sum = jnp.sum(d_scores, axis=0)
    part_key = (
        jnp.einsum("qk,qd->kd", ds_low, queries, preferred_element_type=f32)
        - column_sum[:, None] * key_float
    ) * scale
    part_value = jnp.einsum("qk,qd->kd", probs_low, cotangent, preferred_element_type=f32)

    outs = jnp.concatenate([part_out.astype(bf16), part_query.astype(bf16)], axis=1)
    quarter = rows // 4
    outs = outs.reshape(4, quarter, 2 * width)
    pieces = [outs[phon]] + [shifted(outs[(phon + d) % 4], "phon", d) for d in (1, 3, 2)]

    grads = jnp.concatenate([part_key.astype(bf16), part_value.astype(bf16)], axis=1)
    grads = grads.reshape(block // own, own, 2 * width)
    table = jnp.asarray(np.asarray(ORDERS, np.int32).reshape(2, 16) * 2 + np.arange(2)[:, None], jnp.int32)
    keep = jnp.take(grads, table[core], axis=0)
    send = jnp.take(grads, table[1 - core], axis=0)
    n = lax.axis_size("frames")
    came = lax.ppermute(send, "frames", [(i, i ^ 1) for i in range(n)])
    first = f32_sum([keep, came]).astype(bf16).reshape(4, 4, own, 2 * width)
    first = lax.all_to_all(first, "frames", 0, 0, tiled=True, axis_index_groups=QUADS)
    mine = f32_sum(pieces).astype(bf16)
    spread = [mine] + [shifted(mine, "phon", d) for d in (1, 2, 3)]
    second = jnp.sum(first.astype(f32), axis=0).astype(bf16)
    second = lax.all_to_all(second, "frames", 0, 0, tiled=True, axis_index_groups=CROSSES)
    grad = jnp.sum(second.astype(f32), axis=0)
    everything = jnp.take(
        jnp.stack(spread), (phon - jnp.arange(4, dtype=jnp.int32)) % 4, axis=0
    ).reshape(rows, 2 * width)
    return (everything[:, :width], everything[:, width:], grad[:, :width], grad[:, width:])


def solution(mesh):
    in_specs = (
        P(("chap", "frames"), None),
        P(("chap", "phon", "frames"), None),
        P(("chap", "phon", "frames"), None),
        P(("chap", "frames")),
        P(("chap", "frames"), None),
    )
    out_specs = (
        P(("chap", "frames"), None),
        P(("chap", "frames"), None),
        P(("chap", "phon", "frames"), None),
        P(("chap", "phon", "frames"), None),
    )
    return jax.shard_map(body, mesh=mesh, in_specs=in_specs, out_specs=out_specs, check_vma=False)
```

time: 292 us -> 140 us (0.48)
  waiting for transfers between devices: 214 us -> 33.4 us
  starting transfers between devices: 0.12 us -> 32.1 us
  between operations: 14.5 us -> 1.73 us
  blocking collectives: 37.2 us -> 42.1 us
    reduce_scatter x1 -> x0, waiting for transfers between devices: 79.7 us -> none  [side_by_side(): lax.psum_scatter(both, axis, scatter_dimension=dim, tiled=True)]
    all_gather x1 -> x0, waiting for transfers between devices: 77.1 us -> none  [in_one_piece(): lax.all_gather(both, axis, axis=dim, tiled=True)]
    psum x1 -> x0, waiting for transfers between devices: 57 us -> none  [together(): total = lax.psum(jnp.concatenate([a.ravel() for a in arrays]), axis)]
    all_gather x0 -> x1, blocking collectives: none -> 42.1 us  [gathered(): lax.all_gather(both.astype(jnp.float16), 'frames', axis=0, tiled=True)]
    all_to_all x2 -> x0, blocking collectives: 37.2 us -> none  [sent_to_all(): lax.all_to_all(jnp.broadcast_to(value[None], (length, *value.shape)), axi...]
    ppermute x0 -> x7, starting transfers between devices: none -> 18.7 us  [the longest x6 16.8 us: shifted(): return lax.ppermute(value, axis, [(i, (i + d) % n) for i in range(n)])]
    all_to_all x0 -> x3, waiting for transfers between devices: none -> 18.5 us  [the longest x1 13 us: body(): lax.all_to_all(second, 'frames', 0, 0, tiled=True, axis_index_groups=CROS...]
    ppermute x0 -> x7, waiting for transfers between devices: none -> 14.9 us  [the longest x6 13.6 us: shifted(): return lax.ppermute(value, axis, [(i, (i + d) % n) for i in range(n)])]
  transfers between devices with their start and end apart: 3 -> 10, of which waited for: 3 -> 8; matrix products, arithmetic and copies ran while one was open for 1% -> 7% of each run, Pallas kernels for 0% -> 0%
where the time goes in v1:
time: 140 us; the launch traced here: 139 us
  blocking collectives  42.1 us (30%)
  waiting for transfers between devices  33.4 us (24%)
  starting transfers between devices  32.1 us (23%)
  other arithmetic  12 us (9%)
  matrix products  10 us (7%)
  local copies, waits for them, and re-layouts  7.98 us (6%)
  between operations  1.73 us (1%)
    all_gather x1, blocking collectives, gathered(): lax.all_gather(both.astype(jnp.float16), 'frames', axis=0, tiled=True)  42.1 us
    ppermute x6, starting transfers between devices, shifted(): return lax.ppermute(value, axis, [(i, (i + d) % n) for i in range(n)])  16.8 us
    ppermute x6, waiting for transfers between devices, shifted(): return lax.ppermute(value, axis, [(i, (i + d) % n) for i in range(n)])  13.6 us
    all_to_all x1, waiting for transfers between devices, body(): lax.all_to_all(second, 'frames', 0, 0, tiled=True, axis_index_groups=CROS...  13 us
    all_to_all x1, waiting for transfers between devices, to_all_phon(): lax.all_to_all(jnp.broadcast_to(value[None], (n, *value.shape)), 'phon',...  5.42 us
    all_to_all x1, starting transfers between devices, body(): lax.all_to_all(second, 'frames', 0, 0, tiled=True, axis_index_groups=CROS...  4.71 us
    all_to_all x1, starting transfers between devices, to_all_phon(): lax.all_to_all(jnp.broadcast_to(value[None], (n, *value.shape)), 'phon',...  4.46 us
    all_to_all x1, starting transfers between devices, body(): lax.all_to_all(first, 'frames', 0, 0, tiled=True, axis_index_groups=QUADS)  4.23 us
  transfers between devices with their start and end apart: 10, of which 8 were waited for; matrix products, arithmetic and copies ran while one was open for 7% of the time, Pallas kernels for 0%

profile of v1, /device:TPU:6, one launch (start us, length us, event | category | flops | bytes accessed | tf_op | source)
XLA Modules:
  0.0 139.3 jit_solution(7639880336110400139)
XLA Ops:
  0.6 0.0 copy-start
  0.7 0.9 multiply_convert_fusion.4
  1.5 42.1 %all-gather.1 = f16[1024,1024]{1,0:T(8,128)(2,1)S(1)} all-gather(f16[32,1024]{1,0:T(8,128)(2,1)S(1)} %multiply_convert_fusion.4), channel_id=1, replica_groups=mesh['frames'=32,'phon'=4,'chap'=4] {'frames'}, dimensions={0}, use_global_device_ids=true | all-gather | bytes 2162688 | tf_op jit(solution)/shard_map/all_gather | solution.py:24
  43.6 0.6 multiply_convert_fusion
  44.2 0.0 copy-start.1
  44.3 0.3 fusion
  45.3 0.0 copy-done.9
  45.3 0.8 fusion.4
  46.1 0.0 copy-start.3
  46.1 0.0 copy-done
  46.1 0.0 copy-start.8
  46.1 2.5 %fusion.34 = (f32[512]{0:T(512)S(1)}, f32[512]{0:T(512)S(1)}, f32[1024,512]{1,0:T(8,128)}) fusion(f32[512]{0:T(512)S(1)} %get-tuple-element.30, f32[1024,512]{1,0:T(8,128)S(1)} %get-tuple-element.31, f32[1024]{0:T(1024)S(1)} %broadcast_multiply_fusion, pred[1024]{0:T(1024)(128)(4,1)S(1)} %fusion.27, bf16[512,512]{1,0:T(8,128)(2,1)S(1)} %copy-done, ...), kind=kOutput, calls=%fused_computation.90 | convolution fusion | flops 541064192 | bytes 5778432 | tf_op jit(solution)/shard_map/dot_general | solution.py:70
  48.6 0.0 copy-done.3
  48.6 0.6 broadcast_in_dim.63
  49.2 4.5 %all-to-all-start = ((f32[4,3,512]{2,1,0:T(4,128)}), f32[4,3,512]{2,1,0:T(4,128)S(1)}, u32[]{:S(2)}, u32[]{:S(2)}) async-start(f32[4,3,512]{2,1,0:T(4,128)} %broadcast_in_dim.63), calls=%async_computation | async-start | bytes 65536 | tf_op jit(solution)/shard_map/all_to_all | solution.py:32
  53.7 0.0 copy-done.8
  53.7 5.4 %all-to-all-done = f32[4,3,512]{2,1,0:T(4,128)S(1)} async-done(((f32[4,3,512]{2,1,0:T(4,128)}), f32[4,3,512]{2,1,0:T(4,128)S(1)}, u32[]{:S(2)}, u32[]{:S(2)}) %all-to-all-start) | async-done | bytes 24608 | tf_op jit(solution)/shard_map/all_to_all | solution.py:32
  59.2 0.0 copy-start.4
  59.2 0.0 copy-start.6
  59.2 2.7 %convolution_convert_fusion = bf16[1024,512]{1,0:T(8,128)(2,1)S(1)} fusion(bf16[512,512]{1,0:T(8,128)(2,1)S(1)} %copy-done, f32[512]{0:T(512)S(1)} %get-tuple-element.26, f32[1024,512]{1,0:T(8,128)} %copy-done.3, f32[512]{0:T(512)S(1)} %get-tuple-element.30, f32[1024]{0:T(1024)S(1)} %broadcast_multiply_fusion, pred[1024]{0:T(1024)(128)(4,1)S(1)} %fusion.27), kind=kOutput, calls=%fused_computation.18 | convolution fusion | flops 541065216 | bytes 3679232 | tf_op jit(solution)/shard_map/qk,qd->kd/dot_general | solution.py:90
  61.9 0.0 copy-done.4
  61.9 0.1 copy-done.6
  62.1 1.4 %fusion.12 = (f32[1024]{0:T(1024)S(1)}, bf16[1024,512]{1,0:T(8,128)(2,1)S(1)}) fusion(f32[1024,512]{1,0:T(8,128)S(1)} %copy-done.6, f32[512]{0:T(512)S(1)} %get-tuple-element.27, f32[512]{0:T(512)S(1)} %get-tuple-element.26, f32[512]{0:T(512)S(1)} %get-tuple-element.30, f32[1024,512]{1,0:T(8,128)S(1)} %copy-done.4, f32[1024]{0:T(1024)S(1)} %broadcast_multiply_fusion, ...), kind=kLoop, calls=%fused_computation.32 | loop fusion | flops 5241856 | bytes 5258240 | tf_op jit(solution)/shard_map/reduce_sum | solution.py:85
  63.5 0.0 copy-start.7
  63.5 0.0 copy-done.1
  63.5 1.0 copy-done.7
  64.4 0.7 fusion.3
  65.2 0.3 pad_maximum_fusion
  65.4 1.6 %gather_fusion.2 = bf16[16,32,1024]{2,1,0:T(8,128)(2,1)} fusion(bf16[32,32,1024]{2,1,0:T(8,128)(2,1)S(1)} %bitcast.64, s32[1024]{0:T(1024)S(1)} %pad_clamp_fusion), kind=kCustom, calls=%fused_computation.1.clone | custom fusion | bytes 2097216 | tf_op jit(solution)/shard_map/jit(_take)/gather | solution.py:101
  67.0 2.4 %broadcast_select_fusion = bf16[16,32,1024]{2,1,0:T(8,128)(2,1)} fusion(bf16[16,32,1024]{2,1,0:T(8,128)(2,1)} %gather_fusion.2, pred[16]{0:T(512)(128)(4,1)S(1)} %get-tuple-element.28), kind=kLoop, calls=%fused_computation.25 | loop fusion | flops 524288 | bytes 2097168 | tf_op jit(solution)/shard_map/jit(_take)/select_n | solution.py:101
  69.4 1.9 %collective-permute-start.6 = (bf16[16,32,1024]{2,1,0:T(8,128)(2,1)}, bf16[16,32,1024]{2,1,0:T(8,128)(2,1)}, u32[]{:S(2)}, u32[]{:S(2)}) collective-permute-start(bf16[16,32,1024]{2,1,0:T(8,128)(2,1)} %broadcast_select_fusion), channel_id=1, source_target_pairs={{0,16},{16,0},{32,48},{48,32},{64,80},{80,64},{96,112},{112,96},{1... | collective-permute-start | bytes 3145736 | tf_op jit(solution)/shard_map/ppermute | solution.py:103
  71.4 1.6 %gather_fusion.1 = bf16[16,32,1024]{2,1,0:T(8,128)(2,1)} fusion(bf16[32,32,1024]{2,1,0:T(8,128)(2,1)S(1)} %bitcast.65, s32[1024]{0:T(1024)S(1)} %pad_clamp_fusion.1), kind=kCustom, calls=%fused_computation.clone | custom fusion | bytes 2097216 | tf_op jit(solution)/shard_map/jit(_take)/gather | solution.py:100
  73.0 1.3 collective-permute-done.6
  74.3 3.3 %add_convert_fusion = bf16[16,32,1024]{2,1,0:T(8,128)(2,1)} fusion(bf16[16,32,1024]{2,1,0:T(8,128)(2,1)} %collective-permute-done.6, bf16[16,32,1024]{2,1,0:T(8,128)(2,1)} %gather_fusion.1, pred[16]{0:T(512)(128)(4,1)S(1)} %get-tuple-element.9), kind=kLoop, calls=%fused_computation.14 | loop fusion | flops 2621440 | bytes 3145744 | tf_op jit(solution)/shard_map/convert_element_type | solution.py:104
  77.6 4.2 %all-to-all-start.1 = ((bf16[4,4,32,1024]{3,2,1,0:T(8,128)(2,1)}), bf16[4,4,32,1024]{3,2,1,0:T(8,128)(2,1)}, u32[]{:S(2)}, u32[]{:S(2)}) async-start(bf16[4,4,32,1024]{3,2,1,0:T(8,128)(2,1)} %bitcast.68), calls=%async_computation.1 | async-start | bytes 2097152 | tf_op jit(solution)/shard_map/all_to_all | solution.py:105
  81.9 0.0 copy-done.2
  81.9 2.1 %fusion.5 = bf16[512,512]{0,1:T(8,128)(2,1)S(1)} fusion(bf16[1024,512]{1,0:T(8,128)(2,1)} %copy-done.7, bf16[1024,1024]{1,0:T(8,128)(2,1)S(1)} %copy-done.2), kind=kOutput, calls=%fused_computation.20 | convolution fusion | flops 537395200 | bytes 2621440 | tf_op jit(solution)/shard_map/dot_general | solution.py:84
  84.0 1.2 convolution_convert_fusion.1
  85.3 0.1 pad_maximum_fusion.1
  85.4 0.5 copy.39
  85.9 0.1 dynamic-slice_bitcast_fusion.2
  86.0 3.0 %collective-permute-start.2 = (bf16[128,1024]{1,0:T(8,128)(2,1)S(1)}, bf16[128,1024]{1,0:T(8,128)(2,1)S(1)}, u32[]{:S(2)}, u32[]{:S(2)}) collective-permute-start(bf16[128,1024]{1,0:T(8,128)(2,1)S(1)} %get-tuple-element.18), channel_id=1, source_target_pairs={{0,8},{4,12},{8,0},{12,4},{1,9},{5,13},{9,1},{13,5},{2,10},{6,14},... | collective-permute-start | bytes 786440 | tf_op jit(solution)/shard_map/ppermute | solution.py:39
  89.0 4.1 %collective-permute-start.1 = (bf16[128,1024]{1,0:T(8,128)(2,1)S(1)}, bf16[128,1024]{1,0:T(8,128)(2,1)S(1)}, u32[]{:S(2)}, u32[]{:S(2)}) collective-permute-start(bf16[128,1024]{1,0:T(8,128)(2,1)S(1)} %get-tuple-element.19), channel_id=1, source_target_pairs={{0,12},{4,0},{8,4},{12,8},{1,13},{5,1},{9,5},{13,9},{2,14},{6,2},{... | collective-permute-start | bytes 786440 | tf_op jit(solution)/shard_map/ppermute | solution.py:39
  93.1 1.9 %collective-permute-start = (bf16[128,1024]{1,0:T(8,128)(2,1)S(1)}, bf16[128,1024]{1,0:T(8,128)(2,1)S(1)}, u32[]{:S(2)}, u32[]{:S(2)}) collective-permute-start(bf16[128,1024]{1,0:T(8,128)(2,1)S(1)} %get-tuple-element.17), channel_id=1, source_target_pairs={{0,4},{4,8},{8,12},{12,0},{1,5},{5,9},{9,13},{13,1},{2,6},{6,10},{... | collective-permute-start | bytes 786440 | tf_op jit(solution)/shard_map/ppermute | solution.py:39
  95.0 3.0 %collective-permute-done.2 = bf16[128,1024]{1,0:T(8,128)(2,1)S(1)} collective-permute-done((bf16[128,1024]{1,0:T(8,128)(2,1)S(1)}, bf16[128,1024]{1,0:T(8,128)(2,1)S(1)}, u32[]{:S(2)}, u32[]{:S(2)}) %collective-permute-start.2) | collective-permute-done | bytes 262176 | tf_op jit(solution)/shard_map/ppermute | solution.py:39
  98.0 3.8 %collective-permute-done.1 = bf16[128,1024]{1,0:T(8,128)(2,1)S(1)} collective-permute-done((bf16[128,1024]{1,0:T(8,128)(2,1)S(1)}, bf16[128,1024]{1,0:T(8,128)(2,1)S(1)}, u32[]{:S(2)}, u32[]{:S(2)}) %collective-permute-start.1) | collective-permute-done | bytes 262176 | tf_op jit(solution)/shard_map/ppermute | solution.py:39
  101.8 2.1 %collective-permute-done = bf16[128,1024]{1,0:T(8,128)(2,1)S(1)} collective-permute-done((bf16[128,1024]{1,0:T(8,128)(2,1)S(1)}, bf16[128,1024]{1,0:T(8,128)(2,1)S(1)}, u32[]{:S(2)}, u32[]{:S(2)}) %collective-permute-start) | collective-permute-done | bytes 262176 | tf_op jit(solution)/shard_map/ppermute | solution.py:39
  103.9 0.2 fusion.16
  104.1 2.5 %collective-permute-start.5 = (bf16[128,1024]{1,0:T(8,128)(2,1)S(1)}, bf16[128,1024]{1,0:T(8,128)(2,1)S(1)}, u32[]{:S(2)}, u32[]{:S(2)}) collective-permute-start(bf16[128,1024]{1,0:T(8,128)(2,1)S(1)} %fusion.16), channel_id=1, source_target_pairs={{0,12},{4,0},{8,4},{12,8},{1,13},{5,1},{9,5},{13,9},{2,14},{6,2},{... | collective-permute-start | bytes 786440 | tf_op jit(solution)/shard_map/ppermute | solution.py:39
  106.6 3.4 %collective-permute-start.4 = (bf16[128,1024]{1,0:T(8,128)(2,1)S(1)}, bf16[128,1024]{1,0:T(8,128)(2,1)S(1)}, u32[]{:S(2)}, u32[]{:S(2)}) collective-permute-start(bf16[128,1024]{1,0:T(8,128)(2,1)S(1)} %fusion.16), channel_id=1, source_target_pairs={{0,8},{4,12},{8,0},{12,4},{1,9},{5,13},{9,1},{13,5},{2,10},{6,14},... | collective-permute-start | bytes 786440 | tf_op jit(solution)/shard_map/ppermute | solution.py:39
  110.0 1.9 %collective-permute-start.3 = (bf16[128,1024]{1,0:T(8,128)(2,1)S(1)}, bf16[128,1024]{1,0:T(8,128)(2,1)S(1)}, u32[]{:S(2)}, u32[]{:S(2)}) collective-permute-start(bf16[128,1024]{1,0:T(8,128)(2,1)S(1)} %fusion.16), channel_id=1, source_target_pairs={{0,4},{4,8},{8,12},{12,0},{1,5},{5,9},{9,13},{13,1},{2,6},{6,10},{... | collective-permute-start | bytes 786440 | tf_op jit(solution)/shard_map/ppermute | solution.py:39
  111.9 0.1 broadcast_bitcast_fusion
  112.0 0.0 all-to-all-done.1
  112.0 2.2 %reduce_sum.81 = bf16[4,32,1024]{2,1,0:T(8,128)(2,1)} reduce(bf16[4,4,32,1024]{3,2,1,0:T(8,128)(2,1)} %all-to-all-done.1, bf16[]{:T(256)} %constant.114.clone.1), dimensions={0}, to_apply=%region_8.10 | reduce | flops 393216 | bytes 1310722 | tf_op jit(solution)/shard_map/reduce_sum | solution.py:108
  114.2 4.7 %all-to-all-start.2 = ((bf16[4,32,1024]{2,1,0:T(8,128)(2,1)}), bf16[4,32,1024]{2,1,0:T(8,128)(2,1)S(1)}, u32[]{:S(2)}, u32[]{:S(2)}) async-start(bf16[4,32,1024]{2,1,0:T(8,128)(2,1)} %reduce_sum.81), calls=%async_computation.2 | async-start | bytes 524288 | tf_op jit(solution)/shard_map/all_to_all | solution.py:109
  118.9 0.0 collective-permute-done.5
  118.9 0.3 collective-permute-done.4
  119.2 4.4 %collective-permute-done.3 = bf16[128,1024]{1,0:T(8,128)(2,1)S(1)} collective-permute-done((bf16[128,1024]{1,0:T(8,128)(2,1)S(1)}, bf16[128,1024]{1,0:T(8,128)(2,1)S(1)}, u32[]{:S(2)}, u32[]{:S(2)}) %collective-permute-start.3) | collective-permute-done | bytes 262176 | tf_op jit(solution)/shard_map/ppermute | solution.py:39
  123.6 0.1 pad_maximum_fusion.2
  123.7 0.6 gather_fusion
  124.3 0.2 bitcast_select_fusion
  124.6 1.0 fusion.35
  125.6 13.0 %all-to-all-done.2 = bf16[4,32,1024]{2,1,0:T(8,128)(2,1)S(1)} async-done(((bf16[4,32,1024]{2,1,0:T(8,128)(2,1)}), bf16[4,32,1024]{2,1,0:T(8,128)(2,1)S(1)}, u32[]{:S(2)}, u32[]{:S(2)}) %all-to-all-start.2) | async-done | bytes 262176 | tf_op jit(solution)/shard_map/all_to_all | solution.py:109
  138.7 0.7 fusion.36
  (17 shorter events, 0.2 us)
Async XLA Ops:
  0.6 45.5 %copy-start = (bf16[512,512]{1,0:T(8,128)(2,1)S(1)}, bf16[512,512]{1,0:T(8,128)(2,1)}, u32[]{:S(2)}) copy-start(bf16[512,512]{1,0:T(8,128)(2,1)} %param.12) | copy-start | bytes 1572868
  43.6 1.6 %copy-start.9 = (bf16[512,512]{1,0:T(8,128)(2,1)S(1)}, bf16[512,512]{1,0:T(8,128)(2,1)}, u32[]{:S(2)}) copy-start(bf16[512,512]{1,0:T(8,128)(2,1)} %param.8) | copy-start | bytes 1572868
  44.2 19.2 %copy-start.1 = (bf16[1024,1024]{1,0:T(8,128)(2,1)}, bf16[1024,1024]{1,0:T(8,128)(2,1)S(1)}, u32[]{:S(2)}) copy-start(bf16[1024,1024]{1,0:T(8,128)(2,1)S(1)} %multiply_convert_fusion) | copy-start | bytes 6291460
  46.1 2.5 %copy-start.3 = (f32[1024,512]{1,0:T(8,128)}, f32[1024,512]{1,0:T(8,128)S(1)}, u32[]{:S(2)}) copy-start(f32[1024,512]{1,0:T(8,128)S(1)} %get-tuple-element.31) | copy-start | bytes 6291460
  46.1 7.6 %copy-start.8 = (s32[2,16]{1,0:T(2,128)S(1)}, s32[2,16]{1,0:T(2,128)}, u32[]{:S(2)}) copy-start(s32[2,16]{1,0:T(2,128)} %constant.115.clone) | copy-start | bytes 388
  49.2 9.9 %all-to-all-start = ((f32[4,3,512]{2,1,0:T(4,128)}), f32[4,3,512]{2,1,0:T(4,128)S(1)}, u32[]{:S(2)}, u32[]{:S(2)}) async-start(f32[4,3,512]{2,1,0:T(4,128)} %broadcast_in_dim.63), calls=%async_computation | async-start | bytes 65536 | tf_op jit(solution)/shard_map/all_to_all | solution.py:32
  59.2 2.7 %copy-start.4 = (f32[1024,512]{1,0:T(8,128)S(1)}, f32[1024,512]{1,0:T(8,128)}, u32[]{:S(2)}) copy-start(f32[1024,512]{1,0:T(8,128)} %copy-done.3) | copy-start | bytes 6291460
  59.2 2.8 %copy-start.6 = (f32[1024,512]{1,0:T(8,128)S(1)}, f32[1024,512]{1,0:T(8,128)}, u32[]{:S(2)}) copy-start(f32[1024,512]{1,0:T(8,128)} %get-tuple-element.32) | copy-start | bytes 6291460
  63.5 1.0 copy-start.7
  69.4 4.9 %collective-permute-start.6 = (bf16[16,32,1024]{2,1,0:T(8,128)(2,1)}, bf16[16,32,1024]{2,1,0:T(8,128)(2,1)}, u32[]{:S(2)}, u32[]{:S(2)}) collective-permute-start(bf16[16,32,1024]{2,1,0:T(8,128)(2,1)} %broadcast_select_fusion), channel_id=1, source_target_pairs={{0,16},{16,0},{32,48},{48,32},{64,80},{80,64},{96,112},{112,96},{1... | collective-permute-start | bytes 3145736 | tf_op jit(solution)/shard_map/ppermute | solution.py:103
  74.3 7.6 %copy-start.2 = (bf16[1024,1024]{1,0:T(8,128)(2,1)S(1)}, bf16[1024,1024]{1,0:T(8,128)(2,1)}, u32[]{:S(2)}) copy-start(bf16[1024,1024]{1,0:T(8,128)(2,1)} %copy-done.1) | copy-start | bytes 6291460
  77.6 34.4 %all-to-all-start.1 = ((bf16[4,4,32,1024]{3,2,1,0:T(8,128)(2,1)}), bf16[4,4,32,1024]{3,2,1,0:T(8,128)(2,1)}, u32[]{:S(2)}, u32[]{:S(2)}) async-start(bf16[4,4,32,1024]{3,2,1,0:T(8,128)(2,1)} %bitcast.68), calls=%async_computation.1 | async-start | bytes 2097152 | tf_op jit(solution)/shard_map/all_to_all | solution.py:105
  81.9 2.1 %copy-start.5 = (f32[1024,512]{1,0:T(8,128)S(1)}, f32[1024,512]{1,0:T(8,128)}, u32[]{:S(2)}) copy-start(f32[1024,512]{1,0:T(8,128)} %copy-done.3) | copy-start | bytes 6291460
  86.0 12.1 %collective-permute-start.2 = (bf16[128,1024]{1,0:T(8,128)(2,1)S(1)}, bf16[128,1024]{1,0:T(8,128)(2,1)S(1)}, u32[]{:S(2)}, u32[]{:S(2)}) collective-permute-start(bf16[128,1024]{1,0:T(8,128)(2,1)S(1)} %get-tuple-element.18), channel_id=1, source_target_pairs={{0,8},{4,12},{8,0},{12,4},{1,9},{5,13},{9,1},{13,5},{2,10},{6,14},... | collective-permute-start | bytes 786440 | tf_op jit(solution)/shard_map/ppermute | solution.py:39
  89.0 12.9 %collective-permute-start.1 = (bf16[128,1024]{1,0:T(8,128)(2,1)S(1)}, bf16[128,1024]{1,0:T(8,128)(2,1)S(1)}, u32[]{:S(2)}, u32[]{:S(2)}) collective-permute-start(bf16[128,1024]{1,0:T(8,128)(2,1)S(1)} %get-tuple-element.19), channel_id=1, source_target_pairs={{0,12},{4,0},{8,4},{12,8},{1,13},{5,1},{9,5},{13,9},{2,14},{6,2},{... | collective-permute-start | bytes 786440 | tf_op jit(solution)/shard_map/ppermute | solution.py:39
  93.1 10.9 %collective-permute-start = (bf16[128,1024]{1,0:T(8,128)(2,1)S(1)}, bf16[128,1024]{1,0:T(8,128)(2,1)S(1)}, u32[]{:S(2)}, u32[]{:S(2)}) collective-permute-start(bf16[128,1024]{1,0:T(8,128)(2,1)S(1)} %get-tuple-element.17), channel_id=1, source_target_pairs={{0,4},{4,8},{8,12},{12,0},{1,5},{5,9},{9,13},{13,1},{2,6},{6,10},{... | collective-permute-start | bytes 786440 | tf_op jit(solution)/shard_map/ppermute | solution.py:39
  104.1 14.8 %collective-permute-start.5 = (bf16[128,1024]{1,0:T(8,128)(2,1)S(1)}, bf16[128,1024]{1,0:T(8,128)(2,1)S(1)}, u32[]{:S(2)}, u32[]{:S(2)}) collective-permute-start(bf16[128,1024]{1,0:T(8,128)(2,1)S(1)} %fusion.16), channel_id=1, source_target_pairs={{0,12},{4,0},{8,4},{12,8},{1,13},{5,1},{9,5},{13,9},{2,14},{6,2},{... | collective-permute-start | bytes 786440 | tf_op jit(solution)/shard_map/ppermute | solution.py:39
  106.6 12.6 %collective-permute-start.4 = (bf16[128,1024]{1,0:T(8,128)(2,1)S(1)}, bf16[128,1024]{1,0:T(8,128)(2,1)S(1)}, u32[]{:S(2)}, u32[]{:S(2)}) collective-permute-start(bf16[128,1024]{1,0:T(8,128)(2,1)S(1)} %fusion.16), channel_id=1, source_target_pairs={{0,8},{4,12},{8,0},{12,4},{1,9},{5,13},{9,1},{13,5},{2,10},{6,14},... | collective-permute-start | bytes 786440 | tf_op jit(solution)/shard_map/ppermute | solution.py:39
  110.0 13.6 %collective-permute-start.3 = (bf16[128,1024]{1,0:T(8,128)(2,1)S(1)}, bf16[128,1024]{1,0:T(8,128)(2,1)S(1)}, u32[]{:S(2)}, u32[]{:S(2)}) collective-permute-start(bf16[128,1024]{1,0:T(8,128)(2,1)S(1)} %fusion.16), channel_id=1, source_target_pairs={{0,4},{4,8},{8,12},{12,0},{1,5},{5,9},{9,13},{13,1},{2,6},{6,10},{... | collective-permute-start | bytes 786440 | tf_op jit(solution)/shard_map/ppermute | solution.py:39
  114.2 24.4 %all-to-all-start.2 = ((bf16[4,32,1024]{2,1,0:T(8,128)(2,1)}), bf16[4,32,1024]{2,1,0:T(8,128)(2,1)S(1)}, u32[]{:S(2)}, u32[]{:S(2)}) async-start(bf16[4,32,1024]{2,1,0:T(8,128)(2,1)} %reduce_sum.81), calls=%async_computation.2 | async-start | bytes 524288 | tf_op jit(solution)/shard_map/all_to_all | solution.py:109

commit v2 on v1

v2 whole, which is shorter than its diff:
```python
import jax
import jax.numpy as jnp
import numpy as np
from jax import lax
from jax.experimental import pallas as pl
from jax.experimental.pallas import tpu as pltpu
from jax.sharding import PartitionSpec as P


TILE = 512
NBAND = 2
NEG_FILL = -1e30
FLOOR = -1e29
LIFT = 4096.0
CHUNK = 128
NT = (((1,), (1,)), ((), ()))
F32, BF16 = jnp.float32, jnp.bfloat16


def chip_order(offset):
    return [[(4 * g + (k + g) % 4 + offset) % 16 for g in range(4)] for k in range(4)]


ORDERS = [chip_order(0), chip_order(2)]
QUADS = [[2 * ORDERS[c][k][g] + c for k in range(4)] for c in range(2) for g in range(4)]
CROSSES = [[2 * ORDERS[c][k][g] + c for g in range(4)] for c in range(2) for k in range(4)]
BLOCKS = [2 * ORDERS[c][k][g] + c for c in range(2) for k in range(4) for g in range(4)]


def vmem_call(kernel, out_shape, scalars, arrays, flops):
    spec = pl.BlockSpec(memory_space=pltpu.VMEM)
    size = sum(a.size * a.dtype.itemsize for a in arrays)
    size += sum(int(np.prod(o.shape)) * o.dtype.itemsize for o in out_shape)
    return pl.pallas_call(
        kernel,
        out_shape=out_shape,
        in_specs=[pl.BlockSpec(memory_space=pltpu.SMEM)] * len(scalars) + [spec] * len(arrays),
        out_specs=[spec] * len(out_shape),
        cost_estimate=pl.CostEstimate(flops=flops, bytes_accessed=size, transcendentals=0),
        compiler_params=pltpu.CompilerParams(vmem_limit_bytes=16 << 20),
    )(*scalars, *arrays)


def forward_kernel(flags, every, queries, cotangent, keys, values, expd, d_probs, stats):
    block, width = keys.shape
    own = block // len(BLOCKS)
    scale = width ** (-0.5)
    peak = jnp.full((1, queries.shape[0]), FLOOR, F32)
    for at in range(0, block, CHUNK):
        for i in range(at // own, (at + CHUNK) // own):
            piece = every[own * BLOCKS[i] : own * (BLOCKS[i] + 1), :]
            keys[own * i : own * (i + 1), :] = piece[:, :width]
            values[own * i : own * (i + 1), :] = piece[:, width:]
        here = slice(at, at + CHUNK)
        key = keys[here, :].astype(F32)
        offset = jnp.sum(key * key, axis=1, keepdims=True) * (-0.5 * scale)
        raw = lax.dot_general(keys[here, :], queries[...], NT, preferred_element_type=F32)
        scores = raw * scale + offset
        parts = [
            jnp.where(
                flags[own * BLOCKS[at // own + j] // TILE] > 0,
                scores[own * j : own * (j + 1)],
                NEG_FILL,
            )
            for j in range(CHUNK // own)
        ]
        scores = jnp.concatenate(parts, axis=0)
        expd[here, :] = scores
        peak = jnp.maximum(peak, jnp.max(scores, axis=0, keepdims=True))
    total = jnp.zeros_like(peak)
    delta = jnp.zeros_like(peak)
    for at in range(0, block, CHUNK):
        here = slice(at, at + CHUNK)
        e = jnp.exp(expd[here, :] - peak)
        expd[here, :] = e
        dp = lax.dot_general(values[here, :], cotangent[...], NT, preferred_element_type=F32)
        d_probs[here, :] = dp
        total += jnp.sum(e, axis=0, keepdims=True)
        delta += jnp.sum(e * dp, axis=0, keepdims=True)
    for i in range(stats.shape[0]):
        stats[i, 0:1, :] = peak
        stats[i, 1:2, :] = total
        stats[i, 2:3, :] = delta


def backward_kernel(
    start, stats, mine, expd, d_probs, keys, queries, cotangent, grads, probs_low, ds_low
):
    half, width = grads.shape[0], keys.shape[1]
    scale = width ** (-0.5)
    peaks = [stats[i, 0:1, :] for i in range(stats.shape[0])]
    peak = peaks[0]
    for p in peaks[1:]:
        peak = jnp.maximum(peak, p)
    total = jnp.zeros_like(peak)
    delta = jnp.zeros_like(peak)
    for i, p in enumerate(peaks):
        weight = jnp.exp(p - peak)
        total += weight * stats[i, 1:2, :]
        delta += weight * stats[i, 2:3, :]
    delta = delta / total
    share = jnp.exp(mine[0, 0:1, :] - peak) / total
    for at in range(0, half, CHUNK):
        there = pl.ds(pl.multiple_of(start[0] + at, CHUNK), CHUNK)
        here = slice(at, at + CHUNK)
        probs = expd[there, :] * share
        low = probs.astype(BF16)
        probs_low[here, :] = low
        value = jnp.dot(low, cotangent[...], preferred_element_type=F32)
        grads[here, width:] = value.astype(BF16)
        ds = probs * (d_probs[there, :] - delta)
        low = ds.astype(BF16)
        ds_low[here, :] = low
        column = jnp.sum(ds, axis=1, keepdims=True)
        key = jnp.dot(low, queries[...], preferred_element_type=F32)
        key = (key - column * keys[there, :].astype(F32)) * scale
        grads[here, :width] = key.astype(BF16)


def shifted(value, axis, d):
    n = lax.axis_size(axis)
    return lax.ppermute(value, axis, [(i, (i + d) % n) for i in range(n)])


def f32_sum(parts):
    total = parts[0].astype(F32)
    for part in parts[1:]:
        total = total + part.astype(F32)
    return total


def step(queries, keys, values, band_first, cotangent):
    rows, width = queries.shape
    own = keys.shape[0]
    scale = width ** (-0.5)
    phon = lax.axis_index("phon")
    core = lax.axis_index("frames") & 1
    n = lax.axis_size("frames")
    block = own * n
    half = block // 2
    tall = lambda dtype, r=block, w=width: jax.ShapeDtypeStruct((r, w), dtype)

    both = jnp.concatenate([keys, values], axis=1).astype(F32) * LIFT
    every = lax.all_gather(both.astype(jnp.float16), "frames", axis=0, tiled=True)
    every = (every.astype(F32) * (1.0 / LIFT)).astype(BF16)
    tiles = phon * (block // TILE) + jnp.arange(block // TILE, dtype=jnp.int32)
    flags = ((tiles >= band_first[0]) & (tiles < band_first[0] + NBAND)).astype(jnp.int32)
    work = 2 * block * rows * width
    block_keys, block_values, expd, d_probs, stats = vmem_call(
        forward_kernel,
        [tall(BF16), tall(BF16), tall(F32), tall(F32), jax.ShapeDtypeStruct((4, 3, rows), F32)],
        [flags],
        [every, queries, cotangent],
        2 * work,
    )
    all_stats = lax.all_to_all(stats, "phon", 0, 0, tiled=True)

    def backward(start):
        return vmem_call(
            backward_kernel,
            [tall(BF16, half, 2 * width), tall(BF16, half), tall(BF16, half)],
            [jnp.reshape(start, (1,)).astype(jnp.int32)],
            [all_stats, stats, expd, d_probs, block_keys, queries, cotangent],
            work,
        )

    send, send_probs, send_ds = backward((1 - core) * half)
    came = lax.ppermute(send, "frames", [(i, i ^ 1) for i in range(n)])
    keep, keep_probs, keep_ds = backward(core * half)
    first = f32_sum([keep, came]).astype(BF16).reshape(4, half // 4, 2 * width)
    first = lax.all_to_all(first, "frames", 0, 0, tiled=True, axis_index_groups=QUADS)

    def part(low_keep, low_send, right):
        one = lax.dynamic_slice_in_dim(right, core * half, half, axis=0)
        two = lax.dynamic_slice_in_dim(right, (1 - core) * half, half, axis=0)
        dims = (((0,), (0,)), ((), ()))
        return lax.dot_general(low_keep, one, dims, preferred_element_type=F32) + lax.dot_general(
            low_send, two, dims, preferred_element_type=F32
        )

    out = part(keep_probs, send_probs, block_values).astype(BF16)
    query = (part(keep_ds, send_ds, block_keys) * scale).astype(BF16)
    outs = jnp.concatenate([out, query], axis=1).reshape(4, rows // 4, 2 * width)
    pieces = [lax.dynamic_index_in_dim(outs, phon, 0, False)] + [
        shifted(lax.dynamic_index_in_dim(outs, (phon + d) & 3, 0, False), "phon", d)
        for d in (1, 2, 3)
    ]

    second = f32_sum([first[i] for i in range(4)]).astype(BF16).reshape(4, own, 2 * width)
    second, *pieces = lax.optimization_barrier((second, *pieces))
    mine = f32_sum(pieces).astype(BF16)
    second = lax.all_to_all(second, "frames", 0, 0, tiled=True, axis_index_groups=CROSSES)
    spread = [mine] + [shifted(mine, "phon", d) for d in (1, 2, 3)]
    everything = jnp.zeros((4, rows // 4, 2 * width), BF16)
    for d in range(4):
        everything = lax.dynamic_update_index_in_dim(everything, spread[d], (phon - d) & 3, 0)
    everything = everything.reshape(rows, 2 * width)
    grad = f32_sum([second[i] for i in range(4)])
    return (everything[:, :width], everything[:, width:], grad[:, :width], grad[:, width:])


def solution(mesh):
    in_specs = (
        P(("chap", "frames"), None),
        P(("chap", "phon", "frames"), None),
        P(("chap", "phon", "frames"), None),
        P(("chap", "frames")),
        P(("chap", "frames"), None),
    )
    out_specs = (
        P(("chap", "frames"), None),
        P(("chap", "frames"), None),
        P(("chap", "phon", "frames"), None),
        P(("chap", "phon", "frames"), None),
    )
    return jax.shard_map(step, mesh=mesh, in_specs=in_specs, out_specs=out_specs, check_vma=False)
```

time: 140 us -> 144 us (1.029)
  Pallas kernels: 0 us -> 8.59 us
  matrix products: 10 us -> 1.96 us
  local copies, waits for them, and re-layouts: 7.98 us -> 14.4 us
  other arithmetic: 12 us -> 6.72 us
  starting transfers between devices: 32.1 us -> 35.1 us
  waiting for transfers between devices: 33.4 us -> 31.9 us
    unnamed x20 -> x38, local copies, waits for them, and re-layouts: 1.14 us -> 11.9 us
    pallas_call x0 -> x3, Pallas kernels: none -> 8.59 us  [vmem_call(): pl.pallas_call(kernel, out_shape=out_shape, in_specs=[pl.BlockSpec(memory...]
    dot_general x6 -> x4, matrix products: 10 us -> 1.96 us  [the longest x2 0.98 us: part(): lax.dot_general(low_send, two, dims, preferred_element_type=F32)]
    ppermute x6, waiting for transfers between devices: 13.6 us -> 7.65 us  [shifted(): return lax.ppermute(value, axis, [(i, (i + d) % n) for i in range(n)])]
    all_to_all x3, waiting for transfers between devices: 18.5 us -> 24.2 us  [the longest x1 13.1 us: step(): lax.all_to_all(second, 'frames', 0, 0, tiled=True, axis_index_groups=CROS...]
    reduce_sum x5 -> x0, other arithmetic: 3.92 us -> none  [the longest x1 2.18 us: body(): second = jnp.sum(first.astype(f32), axis=0).astype(bf16)]
    gather x3 -> x0, local copies, waits for them, and re-layouts: 3.85 us -> none  [the longest x1 1.62 us: body(): send = jnp.take(grads, table[1 - core], axis=0)]
    select_n x3 -> x0, other arithmetic: 2.6 us -> none  [the longest x1 2.38 us: body(): send = jnp.take(grads, table[1 - core], axis=0)]
  transfers between devices with their start and end apart: 10 -> 10, of which waited for: 8 -> 7; matrix products, arithmetic and copies ran while one was open for 7% -> 4% of each run, Pallas kernels for 0% -> 1%
where the time goes in v2:
time: 144 us; the launch traced here: 142 us
  blocking collectives  42.1 us (29%)
  starting transfers between devices  35.1 us (24%)
  waiting for transfers between devices  31.9 us (22%)
  local copies, waits for them, and re-layouts  14.4 us (10%)
  Pallas kernels  8.59 us (6%)
  other arithmetic  6.72 us (5%)
  matrix products  1.96 us (1%)
  between operations  1.59 us (1%)
    all_gather x1, blocking collectives, step(): lax.all_gather(both.astype(jnp.float16), 'frames', axis=0, tiled=True)  42.1 us
    ppermute x6, starting transfers between devices, shifted(): return lax.ppermute(value, axis, [(i, (i + d) % n) for i in range(n)])  19.3 us
    all_to_all x1, waiting for transfers between devices, step(): lax.all_to_all(second, 'frames', 0, 0, tiled=True, axis_index_groups=CROS...  13.1 us
    unnamed x38, local copies, waits for them, and re-layouts  11.9 us
    pallas_call x3, Pallas kernels, vmem_call(): pl.pallas_call(kernel, out_shape=out_shape, in_specs=[pl.BlockSpec(memory...  8.59 us
    ppermute x6, waiting for transfers between devices, shifted(): return lax.ppermute(value, axis, [(i, (i + d) % n) for i in range(n)])  7.65 us
    all_to_all x1, waiting for transfers between devices, step(): lax.all_to_all(first, 'frames', 0, 0, tiled=True, axis_index_groups=QUADS)  5.71 us
    all_to_all x1, waiting for transfers between devices, step(): all_stats = lax.all_to_all(stats, 'phon', 0, 0, tiled=True)  5.45 us
  transfers between devices with their start and end apart: 10, of which 7 were waited for; matrix products, arithmetic and copies ran while one was open for 4% of the time, Pallas kernels for 1%

profile of v2, /device:TPU:6, one launch (start us, length us, event | category | flops | bytes accessed | tf_op | source)
XLA Modules:
  0.0 142.4 jit_solution(2666726093590984899)
XLA Ops:
  1.3 0.8 multiply_convert_fusion.1
  2.1 42.1 %all-gather.1 = f16[1024,1024]{1,0:T(8,128)(2,1)S(1)} all-gather(f16[32,1024]{1,0:T(8,128)(2,1)S(1)} %multiply_convert_fusion.1), channel_id=1, replica_groups=mesh['frames'=32,'phon'=4,'chap'=4] {'frames'}, dimensions={0}, use_global_device_ids=true | all-gather | bytes 2162688 | tf_op jit(solution)/shard_map/all_gather | solution.py:144
  44.2 0.6 multiply_convert_fusion.every
  44.9 0.4 copy-done.3
  45.3 0.2 copy-done.6
  45.4 4.4 %shard_map.84 = (bf16[1024,512]{1,0:T(8,128)(2,1)S(1)}, bf16[1024,512]{1,0:T(8,128)(2,1)S(1)}, f32[1024,512]{1,0:T(8,128)S(1)}, f32[1024,512]{1,0:T(8,128)S(1)}, f32[4,3,512]{2,1,0:T(4,128)}) custom-call(s32[2]{0:T(128)S(1)} %and_convert_fusion.flags, bf16[1024,1024]{1,0:T(8,128)(2,1)S(1)} %multiply_convert_fusion.every, bf16[512,512]{1,0:T(8,128)(2,1)S(1)} %copy-done.3, ...), custom_call_target="tpu_custom_call" | custom-call | flops 1073741824 | bytes 9461760 | tf_op jit(solution)/shard_map/pallas_call | solution.py:34
  49.8 1.4 copy-done
  51.2 1.0 copy-done.9
  52.2 4.5 %all-to-all-start = ((f32[4,3,512]{2,1,0:T(4,128)}), f32[4,3,512]{2,1,0:T(4,128)S(1)}, u32[]{:S(2)}, u32[]{:S(2)}) async-start(f32[4,3,512]{2,1,0:T(4,128)} %get-tuple-element.20.mine), calls=%async_computation | async-start | bytes 65536 | tf_op jit(solution)/shard_map/all_to_all | solution.py:156
  56.6 5.5 %all-to-all-done.stats = f32[4,3,512]{2,1,0:T(4,128)S(1)} async-done(((f32[4,3,512]{2,1,0:T(4,128)}), f32[4,3,512]{2,1,0:T(4,128)S(1)}, u32[]{:S(2)}, u32[]{:S(2)}) %all-to-all-start) | async-done | bytes 24608 | tf_op jit(solution)/shard_map/all_to_all | solution.py:156
  62.1 1.6 %copy-done.1 = f32[1024,512]{1,0:T(8,128)S(1)} copy-done((f32[1024,512]{1,0:T(8,128)S(1)}, f32[1024,512]{1,0:T(8,128)}, u32[]{:S(2)}) %copy-start.1) | copy-done | bytes 2097176
  63.7 1.0 copy-done.4
  64.7 1.0 copy-done.7
  65.8 2.5 %shard_map.86 = (bf16[512,1024]{1,0:T(8,128)(2,1)}, bf16[512,512]{1,0:T(8,128)(2,1)S(1)}, bf16[512,512]{1,0:T(8,128)(2,1)S(1)}) custom-call(s32[1]{0:T(128)} %bitcast.2.start, f32[4,3,512]{2,1,0:T(4,128)S(1)} %all-to-all-done.stats, f32[4,3,512]{2,1,0:T(4,128)} %get-tuple-element.20.mine, f32[1024,512]{1,0:T(8,128)S(1)} %get-tuple-element.21.expd, ...), custom_call_target="tpu_custom_call" | custom-call | flops 536870912 | bytes 8437760 | tf_op jit(solution)/shard_map/pallas_call | solution.py:34
  68.3 0.8 copy-done.15
  69.1 0.8 copy-done.17
  69.9 1.9 %collective-permute-start = (bf16[512,1024]{1,0:T(8,128)(2,1)}, bf16[512,1024]{1,0:T(8,128)(2,1)}, u32[]{:S(2)}, u32[]{:S(2)}) collective-permute-start(bf16[512,1024]{1,0:T(8,128)(2,1)} %get-tuple-element.25), channel_id=1, source_target_pairs={{0,16},{16,0},{32,48},{48,32},{64,80},{80,64},{96,112},{112,96},{1... | collective-permute-start | bytes 3145736 | tf_op jit(solution)/shard_map/ppermute | solution.py:168
  71.8 0.0 copy-start.2
  71.8 1.6 %copy-done.2 = f32[1024,512]{1,0:T(8,128)S(1)} copy-done((f32[1024,512]{1,0:T(8,128)S(1)}, f32[1024,512]{1,0:T(8,128)}, u32[]{:S(2)}) %copy-start.2) | copy-done | bytes 2097176
  73.4 1.0 copy-done.5
  74.4 1.0 copy-done.8
  75.5 1.7 %shard_map.85 = (bf16[512,1024]{1,0:T(8,128)(2,1)S(1)}, bf16[512,512]{1,0:T(8,128)(2,1)S(1)}, bf16[512,512]{1,0:T(8,128)(2,1)S(1)}) custom-call(s32[1]{0:T(128)} %bitcast.start, f32[4,3,512]{2,1,0:T(4,128)S(1)} %all-to-all-done.stats, f32[4,3,512]{2,1,0:T(4,128)} %get-tuple-element.20.mine, f32[1024,512]{1,0:T(8,128)S(1)} %get-tuple-element.21.expd, ...), custom_call_target="tpu_custom_call" | custom-call | flops 536870912 | bytes 8437760 | tf_op jit(solution)/shard_map/pallas_call | solution.py:34
  77.1 0.0 copy-start.11
  77.2 0.0 copy-start.13
  77.2 0.0 collective-permute-done
  77.2 3.0 %add_convert_fusion = bf16[512,1024]{1,0:T(8,128)(2,1)} fusion(bf16[512,1024]{1,0:T(8,128)(2,1)} %collective-permute-done, bf16[512,1024]{1,0:T(8,128)(2,1)S(1)} %get-tuple-element.24), kind=kLoop, calls=%fused_computation.1 | loop fusion | flops 2097152 | bytes 3145728 | tf_op jit(solution)/shard_map/convert_element_type | solution.py:170
  80.2 0.0 copy-done.11
  80.2 0.0 copy-done.13
  80.2 0.0 copy-start.12
  80.2 4.4 %all-to-all-start.1 = ((bf16[4,128,1024]{2,1,0:T(8,128)(2,1)}), bf16[4,128,1024]{2,1,0:T(8,128)(2,1)}, u32[]{:S(2)}, u32[]{:S(2)}) async-start(bf16[4,128,1024]{2,1,0:T(8,128)(2,1)} %bitcast.31), calls=%async_computation.1 | async-start | bytes 2097152 | tf_op jit(solution)/shard_map/all_to_all | solution.py:171
  84.6 0.0 copy-done.14
  84.6 0.0 copy-start.18
  84.6 0.5 fusion.4
  85.1 0.0 copy-done.10
  85.1 0.0 copy-done.12
  85.1 0.0 copy-start.16
  85.1 0.5 fusion.7
  85.6 0.0 copy-done.18
  85.6 0.5 fusion.2
  86.1 0.1 copy-done.16
  86.2 0.5 fusion.1
  86.7 0.1 pad_maximum_fusion
  86.8 0.5 copy.13
  87.3 0.1 dynamic-slice_bitcast_fusion
  87.4 2.5 %collective-permute-start.1 = (bf16[128,1024]{1,0:T(8,128)(2,1)S(1)}, bf16[128,1024]{1,0:T(8,128)(2,1)S(1)}, u32[]{:S(2)}, u32[]{:S(2)}) collective-permute-start(bf16[128,1024]{1,0:T(8,128)(2,1)S(1)} %get-tuple-element.42), channel_id=1, source_target_pairs={{0,4},{4,8},{8,12},{12,0},{1,5},{5,9},{9,13},{13,1},{2,6},{6,10},{... | collective-permute-start | bytes 786440 | tf_op jit(solution)/shard_map/ppermute | solution.py:122
  89.9 4.0 %collective-permute-start.2 = (bf16[128,1024]{1,0:T(8,128)(2,1)S(1)}, bf16[128,1024]{1,0:T(8,128)(2,1)S(1)}, u32[]{:S(2)}, u32[]{:S(2)}) collective-permute-start(bf16[128,1024]{1,0:T(8,128)(2,1)S(1)} %get-tuple-element.41), channel_id=1, source_target_pairs={{0,8},{4,12},{8,0},{12,4},{1,9},{5,13},{9,1},{13,5},{2,10},{6,14},... | collective-permute-start | bytes 786440 | tf_op jit(solution)/shard_map/ppermute | solution.py:122
  93.9 3.0 %collective-permute-start.3 = (bf16[128,1024]{1,0:T(8,128)(2,1)S(1)}, bf16[128,1024]{1,0:T(8,128)(2,1)S(1)}, u32[]{:S(2)}, u32[]{:S(2)}) collective-permute-start(bf16[128,1024]{1,0:T(8,128)(2,1)S(1)} %get-tuple-element.40), channel_id=1, source_target_pairs={{0,12},{4,0},{8,4},{12,8},{1,13},{5,1},{9,5},{13,9},{2,14},{6,2},{... | collective-permute-start | bytes 786440 | tf_op jit(solution)/shard_map/ppermute | solution.py:122
  96.9 5.7 %all-to-all-done.1 = bf16[4,128,1024]{2,1,0:T(8,128)(2,1)} async-done(((bf16[4,128,1024]{2,1,0:T(8,128)(2,1)}), bf16[4,128,1024]{2,1,0:T(8,128)(2,1)}, u32[]{:S(2)}, u32[]{:S(2)}) %all-to-all-start.1) | async-done | bytes 1048608 | tf_op jit(solution)/shard_map/all_to_all | solution.py:171
  102.6 2.0 %add_convert_fusion.2 = bf16[1,128,1024]{2,1,0:T(8,128)(2,1)} fusion(bf16[4,128,1024]{2,1,0:T(8,128)(2,1)} %all-to-all-done.1), kind=kLoop, calls=%fused_computation.15 | loop fusion | flops 1048576 | bytes 1310720 | tf_op jit(solution)/shard_map/convert
  104.6 0.2 collective-permute-done.1
  104.8 0.0 collective-permute-done.2
  104.8 2.5 %collective-permute-done.3 = bf16[128,1024]{1,0:T(8,128)(2,1)S(1)} collective-permute-done((bf16[128,1024]{1,0:T(8,128)(2,1)S(1)}, bf16[128,1024]{1,0:T(8,128)(2,1)S(1)}, u32[]{:S(2)}, u32[]{:S(2)}) %collective-permute-start.3) | collective-permute-done | bytes 262176 | tf_op jit(solution)/shard_map/ppermute | solution.py:122
  107.4 0.1 broadcast_in_dim.16
  107.5 0.2 bitcast_dynamic-update-slice_fusion.3
  107.7 2.3 %collective-permute-start.4 = (bf16[128,1024]{1,0:T(8,128)(2,1)S(1)}, bf16[128,1024]{1,0:T(8,128)(2,1)S(1)}, u32[]{:S(2)}, u32[]{:S(2)}) collective-permute-start(bf16[128,1024]{1,0:T(8,128)(2,1)S(1)} %get-tuple-element.37), channel_id=1, source_target_pairs={{0,4},{4,8},{8,12},{12,0},{1,5},{5,9},{9,13},{13,1},{2,6},{6,10},{... | collective-permute-start | bytes 786440 | tf_op jit(solution)/shard_map/ppermute | solution.py:122
  110.0 5.6 %collective-permute-start.5 = (bf16[128,1024]{1,0:T(8,128)(2,1)S(1)}, bf16[128,1024]{1,0:T(8,128)(2,1)S(1)}, u32[]{:S(2)}, u32[]{:S(2)}) collective-permute-start(bf16[128,1024]{1,0:T(8,128)(2,1)S(1)} %get-tuple-element.37), channel_id=1, source_target_pairs={{0,8},{4,12},{8,0},{12,4},{1,9},{5,13},{9,1},{13,5},{2,10},{6,14},... | collective-permute-start | bytes 786440 | tf_op jit(solution)/shard_map/ppermute | solution.py:122
  115.6 1.9 %collective-permute-start.6 = (bf16[128,1024]{1,0:T(8,128)(2,1)S(1)}, bf16[128,1024]{1,0:T(8,128)(2,1)S(1)}, u32[]{:S(2)}, u32[]{:S(2)}) collective-permute-start(bf16[128,1024]{1,0:T(8,128)(2,1)S(1)} %get-tuple-element.37), channel_id=1, source_target_pairs={{0,12},{4,0},{8,4},{12,8},{1,13},{5,1},{9,5},{13,9},{2,14},{6,2},{... | collective-permute-start | bytes 786440 | tf_op jit(solution)/shard_map/ppermute | solution.py:122
  117.5 5.0 %all-to-all-start.2 = ((bf16[4,32,1024]{2,1,0:T(8,128)(2,1)}), bf16[4,32,1024]{2,1,0:T(8,128)(2,1)S(1)}, u32[]{:S(2)}, u32[]{:S(2)}) async-start(bf16[4,32,1024]{2,1,0:T(8,128)(2,1)} %bitcast.4), calls=%async_computation.2 | async-start | bytes 524288 | tf_op jit(solution)/shard_map/all_to_all | solution.py:192
  122.6 0.0 collective-permute-done.4
  122.6 2.9 %collective-permute-done.5 = bf16[128,1024]{1,0:T(8,128)(2,1)S(1)} collective-permute-done((bf16[128,1024]{1,0:T(8,128)(2,1)S(1)}, bf16[128,1024]{1,0:T(8,128)(2,1)S(1)}, u32[]{:S(2)}, u32[]{:S(2)}) %collective-permute-start.5) | collective-permute-done | bytes 262176 | tf_op jit(solution)/shard_map/ppermute | solution.py:122
  125.5 2.0 %collective-permute-done.6 = bf16[128,1024]{1,0:T(8,128)(2,1)S(1)} collective-permute-done((bf16[128,1024]{1,0:T(8,128)(2,1)S(1)}, bf16[128,1024]{1,0:T(8,128)(2,1)S(1)}, u32[]{:S(2)}, u32[]{:S(2)}) %collective-permute-start.6) | collective-permute-done | bytes 262176 | tf_op jit(solution)/shard_map/ppermute | solution.py:122
  127.6 1.0 fusion.13
  128.6 13.1 %all-to-all-done.2 = bf16[4,32,1024]{2,1,0:T(8,128)(2,1)S(1)} async-done(((bf16[4,32,1024]{2,1,0:T(8,128)(2,1)}), bf16[4,32,1024]{2,1,0:T(8,128)(2,1)S(1)}, u32[]{:S(2)}, u32[]{:S(2)}) %all-to-all-start.2) | async-done | bytes 262176 | tf_op jit(solution)/shard_map/all_to_all | solution.py:192
  141.7 0.7 fusion.14
  (18 shorter events, 0.1 us)
Async XLA Ops:
  44.2 1.0 copy-start.3
  44.2 1.2 copy-start.6
  49.8 1.4 copy-start
  51.2 1.0 copy-start.9
  52.2 9.9 %all-to-all-start = ((f32[4,3,512]{2,1,0:T(4,128)}), f32[4,3,512]{2,1,0:T(4,128)S(1)}, u32[]{:S(2)}, u32[]{:S(2)}) async-start(f32[4,3,512]{2,1,0:T(4,128)} %get-tuple-element.20.mine), calls=%async_computation | async-start | bytes 65536 | tf_op jit(solution)/shard_map/all_to_all | solution.py:156
  62.1 1.6 %copy-start.1 = (f32[1024,512]{1,0:T(8,128)S(1)}, f32[1024,512]{1,0:T(8,128)}, u32[]{:S(2)}) copy-start(f32[1024,512]{1,0:T(8,128)} %copy-done) | copy-start | bytes 6291460
  63.7 1.0 copy-start.4
  64.7 1.0 copy-start.7
  68.3 0.8 copy-start.15
  69.1 0.8 copy-start.17
  69.9 7.3 %collective-permute-start = (bf16[512,1024]{1,0:T(8,128)(2,1)}, bf16[512,1024]{1,0:T(8,128)(2,1)}, u32[]{:S(2)}, u32[]{:S(2)}) collective-permute-start(bf16[512,1024]{1,0:T(8,128)(2,1)} %get-tuple-element.25), channel_id=1, source_target_pairs={{0,16},{16,0},{32,48},{48,32},{64,80},{80,64},{96,112},{112,96},{1... | collective-permute-start | bytes 3145736 | tf_op jit(solution)/shard_map/ppermute | solution.py:168
  71.8 1.6 %copy-start.2 = (f32[1024,512]{1,0:T(8,128)S(1)}, f32[1024,512]{1,0:T(8,128)}, u32[]{:S(2)}) copy-start(f32[1024,512]{1,0:T(8,128)} %copy-done) | copy-start | bytes 6291460
  73.4 1.0 copy-start.5
  74.4 1.0 copy-start.8
  77.1 3.0 %copy-start.11 = (bf16[512,512]{1,0:T(8,128)(2,1)}, bf16[512,512]{1,0:T(8,128)(2,1)S(1)}, u32[]{:S(2)}) copy-start(bf16[512,512]{1,0:T(8,128)(2,1)S(1)} %get-tuple-element.26) | copy-start | bytes 1572868
  77.2 3.0 %copy-start.13 = (bf16[512,512]{1,0:T(8,128)(2,1)}, bf16[512,512]{1,0:T(8,128)(2,1)S(1)}, u32[]{:S(2)}) copy-start(bf16[512,512]{1,0:T(8,128)(2,1)S(1)} %get-tuple-element.29) | copy-start | bytes 1572868
  80.2 4.4 %copy-start.14 = (bf16[512,512]{1,0:T(8,128)(2,1)S(1)}, bf16[512,512]{1,0:T(8,128)(2,1)}, u32[]{:S(2)}) copy-start(bf16[512,512]{1,0:T(8,128)(2,1)} %copy-done.13) | copy-start | bytes 1572868
  80.2 4.9 %copy-start.10 = (bf16[1024,512]{1,0:T(8,128)(2,1)S(1)}, bf16[1024,512]{1,0:T(8,128)(2,1)}, u32[]{:S(2)}) copy-start(bf16[1024,512]{1,0:T(8,128)(2,1)} %copy-done.9) | copy-start | bytes 3145732
  80.2 4.9 %copy-start.12 = (bf16[512,512]{1,0:T(8,128)(2,1)S(1)}, bf16[512,512]{1,0:T(8,128)(2,1)}, u32[]{:S(2)}) copy-start(bf16[512,512]{1,0:T(8,128)(2,1)} %copy-done.11) | copy-start | bytes 1572868
  80.2 22.4 %all-to-all-start.1 = ((bf16[4,128,1024]{2,1,0:T(8,128)(2,1)}), bf16[4,128,1024]{2,1,0:T(8,128)(2,1)}, u32[]{:S(2)}, u32[]{:S(2)}) async-start(bf16[4,128,1024]{2,1,0:T(8,128)(2,1)} %bitcast.31), calls=%async_computation.1 | async-start | bytes 2097152 | tf_op jit(solution)/shard_map/all_to_all | solution.py:171
  84.6 1.0 copy-start.18
  85.1 1.1 copy-start.16
  87.4 17.4 %collective-permute-start.1 = (bf16[128,1024]{1,0:T(8,128)(2,1)S(1)}, bf16[128,1024]{1,0:T(8,128)(2,1)S(1)}, u32[]{:S(2)}, u32[]{:S(2)}) collective-permute-start(bf16[128,1024]{1,0:T(8,128)(2,1)S(1)} %get-tuple-element.42), channel_id=1, source_target_pairs={{0,4},{4,8},{8,12},{12,0},{1,5},{5,9},{9,13},{13,1},{2,6},{6,10},{... | collective-permute-start | bytes 786440 | tf_op jit(solution)/shard_map/ppermute | solution.py:122
  89.9 14.9 %collective-permute-start.2 = (bf16[128,1024]{1,0:T(8,128)(2,1)S(1)}, bf16[128,1024]{1,0:T(8,128)(2,1)S(1)}, u32[]{:S(2)}, u32[]{:S(2)}) collective-permute-start(bf16[128,1024]{1,0:T(8,128)(2,1)S(1)} %get-tuple-element.41), channel_id=1, source_target_pairs={{0,8},{4,12},{8,0},{12,4},{1,9},{5,13},{9,1},{13,5},{2,10},{6,14},... | collective-permute-start | bytes 786440 | tf_op jit(solution)/shard_map/ppermute | solution.py:122
  93.9 13.5 %collective-permute-start.3 = (bf16[128,1024]{1,0:T(8,128)(2,1)S(1)}, bf16[128,1024]{1,0:T(8,128)(2,1)S(1)}, u32[]{:S(2)}, u32[]{:S(2)}) collective-permute-start(bf16[128,1024]{1,0:T(8,128)(2,1)S(1)} %get-tuple-element.40), channel_id=1, source_target_pairs={{0,12},{4,0},{8,4},{12,8},{1,13},{5,1},{9,5},{13,9},{2,14},{6,2},{... | collective-permute-start | bytes 786440 | tf_op jit(solution)/shard_map/ppermute | solution.py:122
  107.7 14.9 %collective-permute-start.4 = (bf16[128,1024]{1,0:T(8,128)(2,1)S(1)}, bf16[128,1024]{1,0:T(8,128)(2,1)S(1)}, u32[]{:S(2)}, u32[]{:S(2)}) collective-permute-start(bf16[128,1024]{1,0:T(8,128)(2,1)S(1)} %get-tuple-element.37), channel_id=1, source_target_pairs={{0,4},{4,8},{8,12},{12,0},{1,5},{5,9},{9,13},{13,1},{2,6},{6,10},{... | collective-permute-start | bytes 786440 | tf_op jit(solution)/shard_map/ppermute | solution.py:122
  110.0 15.5 %collective-permute-start.5 = (bf16[128,1024]{1,0:T(8,128)(2,1)S(1)}, bf16[128,1024]{1,0:T(8,128)(2,1)S(1)}, u32[]{:S(2)}, u32[]{:S(2)}) collective-permute-start(bf16[128,1024]{1,0:T(8,128)(2,1)S(1)} %get-tuple-element.37), channel_id=1, source_target_pairs={{0,8},{4,12},{8,0},{12,4},{1,9},{5,13},{9,1},{13,5},{2,10},{6,14},... | collective-permute-start | bytes 786440 | tf_op jit(solution)/shard_map/ppermute | solution.py:122
  115.6 11.9 %collective-permute-start.6 = (bf16[128,1024]{1,0:T(8,128)(2,1)S(1)}, bf16[128,1024]{1,0:T(8,128)(2,1)S(1)}, u32[]{:S(2)}, u32[]{:S(2)}) collective-permute-start(bf16[128,1024]{1,0:T(8,128)(2,1)S(1)} %get-tuple-element.37), channel_id=1, source_target_pairs={{0,12},{4,0},{8,4},{12,8},{1,13},{5,1},{9,5},{13,9},{2,14},{6,2},{... | collective-permute-start | bytes 786440 | tf_op jit(solution)/shard_map/ppermute | solution.py:122
  117.5 24.2 %all-to-all-start.2 = ((bf16[4,32,1024]{2,1,0:T(8,128)(2,1)}), bf16[4,32,1024]{2,1,0:T(8,128)(2,1)S(1)}, u32[]{:S(2)}, u32[]{:S(2)}) async-start(bf16[4,32,1024]{2,1,0:T(8,128)(2,1)} %bitcast.4), calls=%async_computation.2 | async-start | bytes 524288 | tf_op jit(solution)/shard_map/all_to_all | solution.py:192

commit v3 on v2

v3 whole, which is shorter than its diff:
```python
import jax
import jax.numpy as jnp
import numpy as np
from jax import lax
from jax.experimental import pallas as pl
from jax.experimental.pallas import tpu as pltpu
from jax.sharding import PartitionSpec as P


TILE = 512
NBAND = 2
NEG_FILL = -1e30
FLOOR = -1e29
LIFT = 4096.0
CHUNK = 128
NT = (((1,), (1,)), ((), ()))
TN = (((0,), (0,)), ((), ()))
F32, BF16 = jnp.float32, jnp.bfloat16


def chip_order(offset):
    return [[(4 * g + (k + g) % 4 + offset) % 16 for g in range(4)] for k in range(4)]


ORDERS = [chip_order(0), chip_order(2)]
QUADS = [[2 * ORDERS[c][k][g] + c for k in range(4)] for c in range(2) for g in range(4)]
CROSSES = [[2 * ORDERS[c][k][g] + c for g in range(4)] for c in range(2) for k in range(4)]
BLOCKS = [2 * ORDERS[c][k][g] + c for c in range(2) for k in range(4) for g in range(4)]


VMEM, HBM, SMEM = pltpu.VMEM, pltpu.HBM, pltpu.SMEM


def call(kernel, outs, args, scratch=(), flops=0):
    shapes = [
        HBM(shape, dtype) if space == HBM else jax.ShapeDtypeStruct(shape, dtype)
        for shape, dtype, space in outs
    ]
    size = sum(a.size * a.dtype.itemsize for a, _ in args)
    size += sum(int(np.prod(o.shape)) * o.dtype.itemsize for o in shapes)
    return pl.pallas_call(
        kernel,
        out_shape=shapes,
        in_specs=[pl.BlockSpec(memory_space=space) for _, space in args],
        out_specs=[pl.BlockSpec(memory_space=space) for _, _, space in outs],
        scratch_shapes=list(scratch),
        cost_estimate=pl.CostEstimate(flops=flops, bytes_accessed=size, transcendentals=0),
        compiler_params=pltpu.CompilerParams(vmem_limit_bytes=16 << 20),
    )(*[pltpu.with_memory_space_constraint(a, HBM) if space == HBM else a for a, space in args])


def pieces_of(x):
    hi = x.astype(BF16)
    rest = x - hi.astype(F32)
    mid = rest.astype(BF16)
    low = (rest - mid.astype(F32)).astype(BF16)
    return [hi, mid, low]


def joined(block, at):
    rows = [block[3 * at + j : 3 * at + j + 1, :].astype(F32) for j in range(3)]
    return rows[0] + (rows[1] + rows[2])


def masked(scores, flags, first, own):
    return jnp.concatenate(
        [
            jnp.where(flags[first + j] > 0, scores[own * j : own * (j + 1)], NEG_FILL)
            for j in range(scores.shape[0] // own)
        ],
        axis=0,
    )


def forward_kernel(
    flags, every, queries_far, cotangent_far, keys_far, values_far, parcel,
    scores_at, expd, keys, values, queries, cotangent, sems,
):
    block, width = keys.shape
    own = block // len(BLOCKS)
    scale = width ** (-0.5)
    rows = queries.shape[0]
    fetch_q = pltpu.make_async_copy(queries_far, queries, sems.at[0])
    fetch_g = pltpu.make_async_copy(cotangent_far, cotangent, sems.at[1])
    fetch_q.start()
    fetch_g.start()
    peak = jnp.full((1, rows), FLOOR, F32)
    for at in range(0, block, CHUNK):
        for i in range(at // own, (at + CHUNK) // own):
            piece = every[own * BLOCKS[i] : own * (BLOCKS[i] + 1), :]
            keys[own * i : own * (i + 1), :] = piece[:, :width]
            values[own * i : own * (i + 1), :] = piece[:, width:]
        if at == 0:
            fetch_q.wait()
        here = slice(at, at + CHUNK)
        key = keys[here, :].astype(F32)
        offset = jnp.sum(key * key, axis=1, keepdims=True) * (-0.5 * scale)
        raw = lax.dot_general(keys[here, :], queries[...], NT, preferred_element_type=F32)
        scores = masked(raw * scale + offset, flags, at // own, own)
        scores_at[here, :] = scores
        peak = jnp.maximum(peak, jnp.max(scores, axis=0, keepdims=True))
    store_k = pltpu.make_async_copy(keys, keys_far, sems.at[2])
    store_v = pltpu.make_async_copy(values, values_far, sems.at[3])
    store_k.start()
    store_v.start()
    total = jnp.zeros_like(peak)
    for at in range(0, block, CHUNK):
        here = slice(at, at + CHUNK)
        e = jnp.exp(scores_at[here, :] - peak)
        expd[here, :] = e.astype(BF16)
        total += jnp.sum(e, axis=0, keepdims=True)
    fetch_g.wait()
    ranks, deep = parcel.shape[0], parcel.shape[1]
    quarter = rows // ranks
    deltas = []
    for r in range(ranks):
        part = slice(quarter * r, quarter * (r + 1))
        out = lax.dot_general(expd[:, part], values[...], TN, preferred_element_type=F32)
        parcel[r, :quarter, :] = out.astype(BF16)
        delta = jnp.sum(cotangent[part, :].astype(F32) * out, axis=1, keepdims=True)
        deltas.append(jnp.transpose(jnp.broadcast_to(delta, (quarter, 128)))[0:1, :])
    delta = jnp.concatenate(deltas, axis=1)
    lines = pieces_of(peak) + pieces_of(total) + pieces_of(delta)
    lines += [jnp.zeros((1, rows), BF16)] * (deep - quarter - len(lines))
    lines = jnp.concatenate([x.astype(F32) for x in lines], axis=0).astype(BF16)
    for r in range(ranks):
        parcel[r, quarter:, :] = lines
    store_k.wait()
    store_v.wait()


def merged(blocks):
    peaks = [joined(b, 0) for b in blocks]
    peak = peaks[0]
    for p in peaks[1:]:
        peak = jnp.maximum(peak, p)
    weights = [jnp.exp(p - peak) for p in peaks]
    total = sum(w * joined(b, 1) for w, b in zip(weights, blocks))
    return peak, total, weights


def backward_kernel(
    start, flags, parcels, keys_far, values_far, queries_far, cotangent_far, grads, ds_far,
    keys, values, queries, cotangent, ds_low, sems, key_sems, value_sems, store_sems,
):
    half, width = keys.shape
    scale = width ** (-0.5)
    rows = queries.shape[0]
    own = 2 * half // len(BLOCKS)
    spots = range(0, half, CHUNK)
    there = [pl.ds(pl.multiple_of(start[0] + at, CHUNK), CHUNK) for at in spots]
    here = [pl.ds(at, CHUNK) for at in spots]
    fetch_q = pltpu.make_async_copy(queries_far, queries, sems.at[0])
    fetch_g = pltpu.make_async_copy(cotangent_far, cotangent, sems.at[1])
    fetch_k = [
        pltpu.make_async_copy(keys_far.at[t], keys.at[h], key_sems.at[i])
        for i, (t, h) in enumerate(zip(there, here))
    ]
    fetch_v = [
        pltpu.make_async_copy(values_far.at[t], values.at[h], value_sems.at[i])
        for i, (t, h) in enumerate(zip(there, here))
    ]
    fetch_k[0].start()
    fetch_q.start()
    fetch_g.start()
    fetch_v[0].start()
    for k, v in zip(fetch_k[1:], fetch_v[1:]):
        k.start()
        v.start()
    quarter = rows // parcels.shape[0]
    blocks = [parcels[i, quarter:, :] for i in range(parcels.shape[0])]
    peak, total, weights = merged(blocks)
    delta = sum(w * joined(b, 2) for w, b in zip(weights, blocks)) / total
    lse = peak + jnp.log(total)
    fetch_k[0].wait()
    fetch_q.wait()
    stores = []
    for i, spot in enumerate(here):
        if i > 0:
            fetch_k[i].wait()
        low_key = keys[spot, :]
        key = low_key.astype(F32)
        offset = jnp.sum(key * key, axis=1, keepdims=True) * (-0.5 * scale)
        raw = lax.dot_general(low_key, queries[...], NT, preferred_element_type=F32)
        scores = masked(raw * scale + offset, flags, start[0] // own + i * CHUNK // own, own)
        probs = jnp.exp(scores - lse)
        if i == 0:
            fetch_g.wait()
        value = jnp.dot(probs.astype(BF16), cotangent[...], preferred_element_type=F32)
        grads[spot, width:] = value.astype(BF16)
        fetch_v[i].wait()
        dp = lax.dot_general(values[spot, :], cotangent[...], NT, preferred_element_type=F32)
        ds = probs * (dp - delta)
        low = ds.astype(BF16)
        ds_low[spot, :] = low
        stores.append(pltpu.make_async_copy(ds_low.at[spot], ds_far.at[spot], store_sems.at[i]))
        stores[-1].start()
        column = jnp.sum(ds, axis=1, keepdims=True)
        grad = jnp.dot(low, queries[...], preferred_element_type=F32)
        grads[spot, :width] = ((grad - column * key) * scale).astype(BF16)
    for store in stores:
        store.wait()


def outputs_kernel(
    place, parcels, keys_far, keep_far, send_far, out, own_query, *rest
):
    moved, (keys, low, sems) = rest[:3], rest[3:]
    quarter, width = out.shape
    half = low.shape[1]
    phon, keep_at = place[0], place[1]
    fetch_k = pltpu.make_async_copy(keys_far, keys, sems.at[0])
    fetch_keep = pltpu.make_async_copy(keep_far, low.at[0], sems.at[1])
    fetch_send = pltpu.make_async_copy(send_far, low.at[1], sems.at[2])
    for f in (fetch_k, fetch_keep, fetch_send):
        f.start()
    mine = pl.ds(pl.multiple_of(phon * quarter, quarter), quarter)
    blocks = [parcels[i, quarter:, mine] for i in range(parcels.shape[0])]
    _, total, weights = merged(blocks)
    result = jnp.zeros((quarter, width), F32)
    for i, w in enumerate(weights):
        w = jnp.transpose(jnp.broadcast_to(w / total, (quarter, quarter)))
        w = jnp.concatenate([w] * (width // quarter), axis=1)
        result += w * parcels[i, :quarter, :].astype(F32)
    result = result.astype(BF16)
    out[...] = result
    for f in (fetch_k, fetch_keep, fetch_send):
        f.wait()
    for d in range(4):
        part = pl.ds(pl.multiple_of(((phon + d) & 3) * quarter, quarter), quarter)
        query = jnp.zeros((quarter, width), F32)
        for i, at in enumerate((keep_at, half - keep_at)):
            right = keys[pl.ds(pl.multiple_of(at, half), half), :]
            query += lax.dot_general(low[i, :, part], right, TN, preferred_element_type=F32)
        query = (query * width ** (-0.5)).astype(BF16)
        if d == 0:
            own_query[...] = query
        else:
            moved[d - 1][:, :width] = query
            moved[d - 1][:, width:] = result


def add_kernel(keep, came, out, made, sems):
    n = sems.shape[0]
    size = keep.shape[0] // n
    stores = []
    for i in range(n):
        part = pl.ds(size * i, size)
        made[part, :] = (keep[part, :].astype(F32) + came[part, :].astype(F32)).astype(BF16)
        stores.append(pltpu.make_async_copy(made.at[part], out.at[part], sems.at[i]))
        stores[-1].start()
    for store in stores:
        store.wait()


def sum_kernel(came, out):
    out[...] = f32_sum([came[j] for j in range(came.shape[0])]).astype(BF16)


def shifted(value, axis, d):
    n = lax.axis_size(axis)
    return lax.ppermute(value, axis, [(i, (i + d) % n) for i in range(n)])


def f32_sum(parts):
    total = parts[0].astype(F32)
    for part in parts[1:]:
        total = total + part.astype(F32)
    return total


def step(queries, keys, values, band_first, cotangent):
    rows, width = queries.shape
    own = keys.shape[0]
    phon = lax.axis_index("phon")
    core = lax.axis_index("frames") & 1
    n = lax.axis_size("frames")
    block = own * n
    half = block // 2
    ranks = lax.axis_size("phon")
    quarter = rows // ranks
    deep = quarter + 16
    dma = pltpu.SemaphoreType.DMA
    near = [pltpu.VMEM((rows, width), BF16)] * 2

    both = jnp.concatenate([keys, values], axis=1).astype(F32) * LIFT
    every = lax.all_gather(both.astype(jnp.float16), "frames", axis=0, tiled=True)
    every = (every.astype(F32) * (1.0 / LIFT)).astype(BF16)
    tiles = phon * (block // TILE) + jnp.asarray(np.asarray(BLOCKS, np.int32) * own // TILE)
    flags = ((tiles >= band_first[0]) & (tiles < band_first[0] + NBAND)).astype(jnp.int32)
    work = 2 * block * rows * width
    block_keys, block_values, parcel = call(
        forward_kernel,
        [((block, width), BF16, HBM)] * 2 + [((ranks, deep, width), BF16, VMEM)],
        [(flags, SMEM), (every, VMEM), (queries, HBM), (cotangent, HBM)],
        [
            pltpu.VMEM((block, rows), F32),
            pltpu.VMEM((block, rows), BF16),
            pltpu.VMEM((block, width), BF16),
            pltpu.VMEM((block, width), BF16),
            *near,
            dma((4,)),
        ],
        2 * work,
    )
    parcels = lax.all_to_all(parcel, "phon", 0, 0, tiled=True)

    def backward(start):
        return call(
            backward_kernel,
            [((half, 2 * width), BF16, VMEM), ((half, rows), BF16, HBM)],
            [
                (jnp.reshape(start, (1,)).astype(jnp.int32), SMEM),
                (flags, SMEM),
                (parcels, VMEM),
                (block_keys, HBM),
                (block_values, HBM),
                (queries, HBM),
                (cotangent, HBM),
            ],
            [pltpu.VMEM((half, width), BF16)] * 2
            + near
            + [pltpu.VMEM((half, rows), BF16), dma((2,))]
            + [dma((half // CHUNK,))] * 3,
            2 * work,
        )

    send, send_ds = backward((1 - core) * half)
    came = lax.ppermute(send, "frames", [(i, i ^ 1) for i in range(n)])
    keep, keep_ds = backward(core * half)
    (first,) = call(
        add_kernel,
        [((half, 2 * width), BF16, HBM)],
        [(keep, VMEM), (came, VMEM)],
        [pltpu.VMEM((half, 2 * width), BF16), dma((4,))],
    )
    first = lax.all_to_all(
        first.reshape(4, half // 4, 2 * width), "frames", 0, 0, tiled=True,
        axis_index_groups=QUADS,
    )

    place = jnp.stack([phon, core * half]).astype(jnp.int32)
    mine_out, own_query, *parts = call(
        outputs_kernel,
        [((quarter, width), BF16, VMEM)] * 2 + [((quarter, 2 * width), BF16, VMEM)] * 3,
        [
            (place, SMEM),
            (parcels, VMEM),
            (block_keys, HBM),
            (keep_ds, HBM),
            (send_ds, HBM),
        ],
        [pltpu.VMEM((block, width), BF16), pltpu.VMEM((2, half, rows), BF16), dma((3,))],
        work,
    )
    moved = [shifted(p, "phon", d) for d, p in zip((1, 2, 3), parts)]

    (second,) = call(sum_kernel, [((half // 4, 2 * width), BF16, VMEM)], [(first, VMEM)])
    second = lax.all_to_all(
        second.reshape(4, own, 2 * width), "frames", 0, 0, tiled=True,
        axis_index_groups=CROSSES,
    )
    mine_query = f32_sum([own_query] + [m[:, :width] for m in moved]).astype(BF16)
    spread = [mine_query] + [shifted(mine_query, "phon", d) for d in (1, 2, 3)]

    def placed(parts):
        whole = jnp.zeros((ranks, quarter, width), BF16)
        for d, p in enumerate(parts):
            whole = lax.dynamic_update_index_in_dim(whole, p, (phon - d) & 3, 0)
        return whole.reshape(rows, width)

    aligned = placed([mine_out] + [m[:, width:] for m in moved])
    grad_query = placed(spread)
    grad = f32_sum([second[i] for i in range(4)])
    return (aligned, grad_query, grad[:, :width], grad[:, width:])


def solution(mesh):
    in_specs = (
        P(("chap", "frames"), None),
        P(("chap", "phon", "frames"), None),
        P(("chap", "phon", "frames"), None),
        P(("chap", "frames")),
        P(("chap", "frames"), None),
    )
    out_specs = (
        P(("chap", "frames"), None),
        P(("chap", "frames"), None),
        P(("chap", "phon", "frames"), None),
        P(("chap", "phon", "frames"), None),
    )
    return jax.shard_map(step, mesh=mesh, in_specs=in_specs, out_specs=out_specs, check_vma=False)
```

time: 144 us -> 145 us (level)
  Pallas kernels: 8.59 us -> 20.5 us
  local copies, waits for them, and re-layouts: 14.4 us -> 4.21 us
  waiting for transfers between devices: 31.9 us -> 40.5 us
  other arithmetic: 6.72 us -> 1.61 us
  matrix products: 1.96 us -> 0 us
    unnamed x38 -> x8, local copies, waits for them, and re-layouts: 11.9 us -> 0.06 us
    pallas_call x3 -> x5, Pallas kernels: 8.59 us -> 20.5 us  [call(): pl.pallas_call(kernel, out_shape=shapes, in_specs=[pl.BlockSpec(memory_sp...]
    all_to_all x3, waiting for transfers between devices: 24.2 us -> 29.2 us  [the longest x1 18.5 us: step(): lax.all_to_all(second.reshape(4, own, 2 * width), 'frames', 0, 0, tiled=T...]
    ppermute x6, waiting for transfers between devices: 7.65 us -> 11.3 us  [shifted(): return lax.ppermute(value, axis, [(i, (i + d) % n) for i in range(n)])]
    pallas_call x0 -> x1, local copies, waits for them, and re-layouts: none -> 3.34 us  [call(): pl.pallas_call(kernel, out_shape=shapes, in_specs=[pl.BlockSpec(memory_sp...]
    convert_element_type x1 -> x0, other arithmetic: 2.97 us -> none  [step(): first = f32_sum([keep, came]).astype(BF16).reshape(4, half // 4, 2 * width)]
    another operation x1, other arithmetic: 2.05 us -> 0.08 us  [step(): place = jnp.stack([phon, core * half]).astype(jnp.int32)]
    dot_general x4 -> x0, matrix products: 1.96 us -> none  [the longest x2 0.98 us: part(): lax.dot_general(low_send, two, dims, preferred_element_type=F32)]
  transfers between devices with their start and end apart: 10 -> 10, of which waited for: 7 -> 4; matrix products, arithmetic and copies ran while one was open for 4% -> 3% of each run, Pallas kernels for 1% -> 5%
where the time goes in v3:
time: 145 us; the launch traced here: 144 us
  blocking collectives  42.1 us (29%)
  waiting for transfers between devices  40.5 us (28%)
  starting transfers between devices  33.8 us (23%)
  Pallas kernels  20.5 us (14%)
  local copies, waits for them, and re-layouts  4.21 us (3%)
  other arithmetic  1.61 us (1%)
  between operations  1.55 us (1%)
    all_gather x1, blocking collectives, step(): lax.all_gather(both.astype(jnp.float16), 'frames', axis=0, tiled=True)  42.1 us
    pallas_call x5, Pallas kernels, call(): pl.pallas_call(kernel, out_shape=shapes, in_specs=[pl.BlockSpec(memory_sp...  20.5 us
    ppermute x6, starting transfers between devices, shifted(): return lax.ppermute(value, axis, [(i, (i + d) % n) for i in range(n)])  18.8 us
    all_to_all x1, waiting for transfers between devices, step(): lax.all_to_all(second.reshape(4, own, 2 * width), 'frames', 0, 0, tiled=T...  18.5 us
    ppermute x6, waiting for transfers between devices, shifted(): return lax.ppermute(value, axis, [(i, (i + d) % n) for i in range(n)])  11.3 us
    all_to_all x1, waiting for transfers between devices, step(): parcels = lax.all_to_all(parcel, 'phon', 0, 0, tiled=True)  10.7 us
    all_to_all x1, starting transfers between devices, step(): lax.all_to_all(second.reshape(4, own, 2 * width), 'frames', 0, 0, tiled=T...  4.99 us
    all_to_all x1, starting transfers between devices, step(): parcels = lax.all_to_all(parcel, 'phon', 0, 0, tiled=True)  4.47 us
  transfers between devices with their start and end apart: 10, of which 4 were waited for; matrix products, arithmetic and copies ran while one was open for 3% of the time, Pallas kernels for 5%

profile of v3, /device:TPU:6, one launch (start us, length us, event | category | flops | bytes accessed | tf_op | source)
XLA Modules:
  0.0 144.3 jit_solution(3676020181144076790)
XLA Ops:
  1.3 0.8 multiply_convert_fusion.1
  2.1 42.1 %all-gather.1 = f16[1024,1024]{1,0:T(8,128)(2,1)S(1)} all-gather(f16[32,1024]{1,0:T(8,128)(2,1)S(1)} %multiply_convert_fusion.1), channel_id=1, replica_groups=mesh['frames'=32,'phon'=4,'chap'=4] {'frames'}, dimensions={0}, use_global_device_ids=true | all-gather | bytes 2162688 | tf_op jit(solution)/shard_map/all_gather | solution.py:287
  44.2 0.0 copy-start.3
  44.2 0.6 multiply_convert_fusion.every
  44.8 0.0 copy-done.3
  44.9 5.4 %shard_map.93 = (bf16[1024,512]{1,0:T(8,128)(2,1)}, bf16[1024,512]{1,0:T(8,128)(2,1)}, bf16[4,144,512]{2,1,0:T(8,128)(2,1)}) custom-call(s32[32]{0:T(128)S(1)} %and_convert_fusion.flags, bf16[1024,1024]{1,0:T(8,128)(2,1)S(1)} %multiply_convert_fusion.every, bf16[512,512]{1,0:T(8,128)(2,1)} %queries_far.5, bf16[512,512]{1,0:T(8,128)(2,1)} %cotangent_far.5), custom_call_target="tpu_custom_call" | custom-call | flops 1073741824 | bytes 5832832 | tf_op jit(solution)/shard_map/pallas_call | solution.py:41
  50.3 4.5 %all-to-all-start = ((bf16[4,144,512]{2,1,0:T(8,128)(2,1)}), bf16[4,144,512]{2,1,0:T(8,128)(2,1)S(1)}, u32[]{:S(2)}, u32[]{:S(2)}) async-start(bf16[4,144,512]{2,1,0:T(8,128)(2,1)} %get-tuple-element.16), calls=%async_computation | async-start | bytes 1179648 | tf_op jit(solution)/shard_map/all_to_all | solution.py:306
  54.8 10.7 %all-to-all-done.parcels = bf16[4,144,512]{2,1,0:T(8,128)(2,1)S(1)} async-done(((bf16[4,144,512]{2,1,0:T(8,128)(2,1)}), bf16[4,144,512]{2,1,0:T(8,128)(2,1)S(1)}, u32[]{:S(2)}, u32[]{:S(2)}) %all-to-all-start) | async-done | bytes 589856 | tf_op jit(solution)/shard_map/all_to_all | solution.py:306
  65.5 6.6 %shard_map.95 = (bf16[512,1024]{1,0:T(8,128)(2,1)S(1)}, bf16[512,512]{1,0:T(8,128)(2,1)}) custom-call(s32[1]{0:T(128)} %bitcast.3.start, s32[32]{0:T(128)S(1)} %and_convert_fusion.flags, bf16[4,144,512]{2,1,0:T(8,128)(2,1)S(1)} %all-to-all-done.parcels, bf16[1024,512]{1,0:T(8,128)(2,1)} %get-tuple-element.17.keys_far, ...), custom_call_target="tpu_custom_call" | custom-call | flops 1073741824 | bytes 5308548 | tf_op jit(solution)/shard_map/pallas_call | solution.py:41
  72.0 1.9 %collective-permute-start.6 = (bf16[512,1024]{1,0:T(8,128)(2,1)S(1)}, bf16[512,1024]{1,0:T(8,128)(2,1)S(1)}, u32[]{:S(2)}, u32[]{:S(2)}) collective-permute-start(bf16[512,1024]{1,0:T(8,128)(2,1)S(1)} %get-tuple-element.27), channel_id=1, source_target_pairs={{0,16},{16,0},{32,48},{48,32},{64,80},{80,64},{96,112},{112,96},{1... | collective-permute-start | bytes 3145736 | tf_op jit(solution)/shard_map/ppermute | solution.py:329
  74.0 6.6 %shard_map.94 = (bf16[512,1024]{1,0:T(8,128)(2,1)S(1)}, bf16[512,512]{1,0:T(8,128)(2,1)}) custom-call(s32[1]{0:T(128)} %bitcast.1.start, s32[32]{0:T(128)S(1)} %and_convert_fusion.flags, bf16[4,144,512]{2,1,0:T(8,128)(2,1)S(1)} %all-to-all-done.parcels, bf16[1024,512]{1,0:T(8,128)(2,1)} %get-tuple-element.17.keys_far, ...), custom_call_target="tpu_custom_call" | custom-call | flops 1073741824 | bytes 5308548 | tf_op jit(solution)/shard_map/pallas_call | solution.py:41
  80.5 0.0 collective-permute-done.6.came
  80.6 1.1 shard_map.96
  81.7 0.0 copy-start
  81.7 3.7 %all-to-all-start.1 = ((bf16[4,128,1024]{2,1,0:T(8,128)(2,1)}), bf16[4,128,1024]{2,1,0:T(8,128)(2,1)S(1)}, u32[]{:S(2)}, u32[]{:S(2)}) async-start(bf16[4,128,1024]{2,1,0:T(8,128)(2,1)} %bitcast.34), calls=%async_computation.1 | async-start | bytes 2097152 | tf_op jit(solution)/shard_map/all_to_all | solution.py:337
  85.3 0.1 pad_add_fusion
  85.5 0.0 copy-done
  85.5 3.3 %shard_map.98 = (bf16[4,128,512]{2,1,0:T(8,128)(2,1)S(1)}, bf16[128,1024]{1,0:T(8,128)(2,1)}, bf16[128,1024]{1,0:T(8,128)(2,1)}, bf16[128,1024]{1,0:T(8,128)(2,1)}, bf16[128,512]{1,0:T(8,128)(2,1)S(1)}) fusion(bf16[4,128,512]{2,1,0:T(8,128)(2,1)S(1)} %broadcast.3.clone, s32[]{:T(128)S(6)} %select_n.17, s32[2]{0:T(128)S(1)} %pad_add_fusion, ...), kind=kCustom, calls=%fused_computation.12 | custom fusion | bytes 3736068 | tf_op jit(solution)/shard_map/pallas_call | solution.py:41
  88.8 2.5 %collective-permute-start = (bf16[128,1024]{1,0:T(8,128)(2,1)}, bf16[128,1024]{1,0:T(8,128)(2,1)S(1)}, u32[]{:S(2)}, u32[]{:S(2)}) collective-permute-start(bf16[128,1024]{1,0:T(8,128)(2,1)} %get-tuple-element.31), channel_id=1, source_target_pairs={{0,4},{4,8},{8,12},{12,0},{1,5},{5,9},{9,13},{13,1},{2,6},{6,10},{... | collective-permute-start | bytes 786440 | tf_op jit(solution)/shard_map/ppermute | solution.py:262
  91.3 4.0 %collective-permute-start.1 = (bf16[128,1024]{1,0:T(8,128)(2,1)}, bf16[128,1024]{1,0:T(8,128)(2,1)S(1)}, u32[]{:S(2)}, u32[]{:S(2)}) collective-permute-start(bf16[128,1024]{1,0:T(8,128)(2,1)} %get-tuple-element.33), channel_id=1, source_target_pairs={{0,8},{4,12},{8,0},{12,4},{1,9},{5,13},{9,1},{13,5},{2,10},{6,14},... | collective-permute-start | bytes 786440 | tf_op jit(solution)/shard_map/ppermute | solution.py:262
  95.3 2.5 %collective-permute-start.2 = (bf16[128,1024]{1,0:T(8,128)(2,1)}, bf16[128,1024]{1,0:T(8,128)(2,1)S(1)}, u32[]{:S(2)}, u32[]{:S(2)}) collective-permute-start(bf16[128,1024]{1,0:T(8,128)(2,1)} %get-tuple-element.35), channel_id=1, source_target_pairs={{0,12},{4,0},{8,4},{12,8},{1,13},{5,1},{9,5},{13,9},{2,14},{6,2},{... | collective-permute-start | bytes 786440 | tf_op jit(solution)/shard_map/ppermute | solution.py:262
  97.8 8.8 %collective-permute-done = bf16[128,1024]{1,0:T(8,128)(2,1)S(1)} collective-permute-done((bf16[128,1024]{1,0:T(8,128)(2,1)}, bf16[128,1024]{1,0:T(8,128)(2,1)S(1)}, u32[]{:S(2)}, u32[]{:S(2)}) %collective-permute-start) | collective-permute-done | bytes 262176 | tf_op jit(solution)/shard_map/ppermute | solution.py:262
  106.6 0.0 collective-permute-done.1
  106.6 2.5 %collective-permute-done.2 = bf16[128,1024]{1,0:T(8,128)(2,1)S(1)} collective-permute-done((bf16[128,1024]{1,0:T(8,128)(2,1)}, bf16[128,1024]{1,0:T(8,128)(2,1)S(1)}, u32[]{:S(2)}, u32[]{:S(2)}) %collective-permute-start.2) | collective-permute-done | bytes 262176 | tf_op jit(solution)/shard_map/ppermute | solution.py:262
  109.2 0.1 bitcast_dynamic-update-slice_fusion.3
  109.3 2.2 %collective-permute-start.3 = (bf16[128,512]{1,0:T(8,128)(2,1)S(1)}, bf16[128,512]{1,0:T(8,128)(2,1)S(1)}, u32[]{:S(2)}, u32[]{:S(2)}) collective-permute-start(bf16[128,512]{1,0:T(8,128)(2,1)S(1)} %get-tuple-element.39), channel_id=1, source_target_pairs={{0,4},{4,8},{8,12},{12,0},{1,5},{5,9},{9,13},{13,1},{2,6},{6,10},{... | collective-permute-start | bytes 393224 | tf_op jit(solution)/shard_map/ppermute | solution.py:262
  111.4 5.7 %collective-permute-start.4 = (bf16[128,512]{1,0:T(8,128)(2,1)S(1)}, bf16[128,512]{1,0:T(8,128)(2,1)S(1)}, u32[]{:S(2)}, u32[]{:S(2)}) collective-permute-start(bf16[128,512]{1,0:T(8,128)(2,1)S(1)} %get-tuple-element.39), channel_id=1, source_target_pairs={{0,8},{4,12},{8,0},{12,4},{1,9},{5,13},{9,1},{13,5},{2,10},{6,14},... | collective-permute-start | bytes 393224 | tf_op jit(solution)/shard_map/ppermute | solution.py:262
  117.2 1.9 %collective-permute-start.5 = (bf16[128,512]{1,0:T(8,128)(2,1)S(1)}, bf16[128,512]{1,0:T(8,128)(2,1)S(1)}, u32[]{:S(2)}, u32[]{:S(2)}) collective-permute-start(bf16[128,512]{1,0:T(8,128)(2,1)S(1)} %get-tuple-element.39), channel_id=1, source_target_pairs={{0,12},{4,0},{8,4},{12,8},{1,13},{5,1},{9,5},{13,9},{2,14},{6,2},{... | collective-permute-start | bytes 393224 | tf_op jit(solution)/shard_map/ppermute | solution.py:262
  119.1 0.0 all-to-all-done.1.came
  119.2 0.8 shard_map.97
  120.0 5.0 %all-to-all-start.2 = ((bf16[4,32,1024]{2,1,0:T(8,128)(2,1)}), bf16[4,32,1024]{2,1,0:T(8,128)(2,1)S(1)}, u32[]{:S(2)}, u32[]{:S(2)}) async-start(bf16[4,32,1024]{2,1,0:T(8,128)(2,1)} %bitcast.15), calls=%async_computation.2 | async-start | bytes 524288 | tf_op jit(solution)/shard_map/all_to_all | solution.py:359
  125.0 0.0 copy-start.1
  125.0 0.0 collective-permute-done.3
  125.0 0.0 collective-permute-done.4
  125.1 0.0 collective-permute-done.5
  125.1 0.0 copy-start.2
  125.1 18.5 %all-to-all-done.2 = bf16[4,32,1024]{2,1,0:T(8,128)(2,1)S(1)} async-done(((bf16[4,32,1024]{2,1,0:T(8,128)(2,1)}), bf16[4,32,1024]{2,1,0:T(8,128)(2,1)S(1)}, u32[]{:S(2)}, u32[]{:S(2)}) %all-to-all-start.2) | async-done | bytes 262176 | tf_op jit(solution)/shard_map/all_to_all | solution.py:359
  143.6 0.7 fusion.9
  144.3 0.0 copy-done.1
  144.3 0.0 copy-done.2
  (9 shorter events, 0.2 us)
Async XLA Ops:
  44.2 0.7 copy-start.3
  50.3 15.2 %all-to-all-start = ((bf16[4,144,512]{2,1,0:T(8,128)(2,1)}), bf16[4,144,512]{2,1,0:T(8,128)(2,1)S(1)}, u32[]{:S(2)}, u32[]{:S(2)}) async-start(bf16[4,144,512]{2,1,0:T(8,128)(2,1)} %get-tuple-element.16), calls=%async_computation | async-start | bytes 1179648 | tf_op jit(solution)/shard_map/all_to_all | solution.py:306
  72.0 8.5 %collective-permute-start.6 = (bf16[512,1024]{1,0:T(8,128)(2,1)S(1)}, bf16[512,1024]{1,0:T(8,128)(2,1)S(1)}, u32[]{:S(2)}, u32[]{:S(2)}) collective-permute-start(bf16[512,1024]{1,0:T(8,128)(2,1)S(1)} %get-tuple-element.27), channel_id=1, source_target_pairs={{0,16},{16,0},{32,48},{48,32},{64,80},{80,64},{96,112},{112,96},{1... | collective-permute-start | bytes 3145736 | tf_op jit(solution)/shard_map/ppermute | solution.py:329
  81.7 3.8 %copy-start = (bf16[1024,512]{1,0:T(8,128)(2,1)S(1)}, bf16[1024,512]{1,0:T(8,128)(2,1)}, u32[]{:S(2)}) copy-start(bf16[1024,512]{1,0:T(8,128)(2,1)} %get-tuple-element.17.keys_far) | copy-start | bytes 3145732
  81.7 37.5 %all-to-all-start.1 = ((bf16[4,128,1024]{2,1,0:T(8,128)(2,1)}), bf16[4,128,1024]{2,1,0:T(8,128)(2,1)S(1)}, u32[]{:S(2)}, u32[]{:S(2)}) async-start(bf16[4,128,1024]{2,1,0:T(8,128)(2,1)} %bitcast.34), calls=%async_computation.1 | async-start | bytes 2097152 | tf_op jit(solution)/shard_map/all_to_all | solution.py:337
  88.8 17.8 %collective-permute-start = (bf16[128,1024]{1,0:T(8,128)(2,1)}, bf16[128,1024]{1,0:T(8,128)(2,1)S(1)}, u32[]{:S(2)}, u32[]{:S(2)}) collective-permute-start(bf16[128,1024]{1,0:T(8,128)(2,1)} %get-tuple-element.31), channel_id=1, source_target_pairs={{0,4},{4,8},{8,12},{12,0},{1,5},{5,9},{9,13},{13,1},{2,6},{6,10},{... | collective-permute-start | bytes 786440 | tf_op jit(solution)/shard_map/ppermute | solution.py:262
  91.3 15.3 %collective-permute-start.1 = (bf16[128,1024]{1,0:T(8,128)(2,1)}, bf16[128,1024]{1,0:T(8,128)(2,1)S(1)}, u32[]{:S(2)}, u32[]{:S(2)}) collective-permute-start(bf16[128,1024]{1,0:T(8,128)(2,1)} %get-tuple-element.33), channel_id=1, source_target_pairs={{0,8},{4,12},{8,0},{12,4},{1,9},{5,13},{9,1},{13,5},{2,10},{6,14},... | collective-permute-start | bytes 786440 | tf_op jit(solution)/shard_map/ppermute | solution.py:262
  95.3 13.8 %collective-permute-start.2 = (bf16[128,1024]{1,0:T(8,128)(2,1)}, bf16[128,1024]{1,0:T(8,128)(2,1)S(1)}, u32[]{:S(2)}, u32[]{:S(2)}) collective-permute-start(bf16[128,1024]{1,0:T(8,128)(2,1)} %get-tuple-element.35), channel_id=1, source_target_pairs={{0,12},{4,0},{8,4},{12,8},{1,13},{5,1},{9,5},{13,9},{2,14},{6,2},{... | collective-permute-start | bytes 786440 | tf_op jit(solution)/shard_map/ppermute | solution.py:262
  109.3 15.7 %collective-permute-start.3 = (bf16[128,512]{1,0:T(8,128)(2,1)S(1)}, bf16[128,512]{1,0:T(8,128)(2,1)S(1)}, u32[]{:S(2)}, u32[]{:S(2)}) collective-permute-start(bf16[128,512]{1,0:T(8,128)(2,1)S(1)} %get-tuple-element.39), channel_id=1, source_target_pairs={{0,4},{4,8},{8,12},{12,0},{1,5},{5,9},{9,13},{13,1},{2,6},{6,10},{... | collective-permute-start | bytes 393224 | tf_op jit(solution)/shard_map/ppermute | solution.py:262
  111.4 13.6 %collective-permute-start.4 = (bf16[128,512]{1,0:T(8,128)(2,1)S(1)}, bf16[128,512]{1,0:T(8,128)(2,1)S(1)}, u32[]{:S(2)}, u32[]{:S(2)}) collective-permute-start(bf16[128,512]{1,0:T(8,128)(2,1)S(1)} %get-tuple-element.39), channel_id=1, source_target_pairs={{0,8},{4,12},{8,0},{12,4},{1,9},{5,13},{9,1},{13,5},{2,10},{6,14},... | collective-permute-start | bytes 393224 | tf_op jit(solution)/shard_map/ppermute | solution.py:262
  117.2 7.9 %collective-permute-start.5 = (bf16[128,512]{1,0:T(8,128)(2,1)S(1)}, bf16[128,512]{1,0:T(8,128)(2,1)S(1)}, u32[]{:S(2)}, u32[]{:S(2)}) collective-permute-start(bf16[128,512]{1,0:T(8,128)(2,1)S(1)} %get-tuple-element.39), channel_id=1, source_target_pairs={{0,12},{4,0},{8,4},{12,8},{1,13},{5,1},{9,5},{13,9},{2,14},{6,2},{... | collective-permute-start | bytes 393224 | tf_op jit(solution)/shard_map/ppermute | solution.py:262
  120.0 23.6 %all-to-all-start.2 = ((bf16[4,32,1024]{2,1,0:T(8,128)(2,1)}), bf16[4,32,1024]{2,1,0:T(8,128)(2,1)S(1)}, u32[]{:S(2)}, u32[]{:S(2)}) async-start(bf16[4,32,1024]{2,1,0:T(8,128)(2,1)} %bitcast.15), calls=%async_computation.2 | async-start | bytes 524288 | tf_op jit(solution)/shard_map/all_to_all | solution.py:359
  125.0 19.3 %copy-start.1 = (bf16[4,128,512]{2,1,0:T(8,128)(2,1)}, bf16[4,128,512]{2,1,0:T(8,128)(2,1)S(1)}, u32[]{:S(2)}) copy-start(bf16[4,128,512]{2,1,0:T(8,128)(2,1)S(1)} %fusion) | copy-start | bytes 1572868
  125.1 19.2 %copy-start.2 = (bf16[4,128,512]{2,1,0:T(8,128)(2,1)}, bf16[4,128,512]{2,1,0:T(8,128)(2,1)S(1)}, u32[]{:S(2)}) copy-start(bf16[4,128,512]{2,1,0:T(8,128)(2,1)S(1)} %bitcast_dynamic-update-slice_fusion) | copy-start | bytes 1572868

commit v4 on v3

--- a/solution.py
+++ b/solution.py
@@ -12,7 +12,7 @@
 NEG_FILL = -1e30
 FLOOR = -1e29
 LIFT = 4096.0
-CHUNK = 128
+CHUNK = 512
 NT = (((1,), (1,)), ((), ()))
 TN = (((0,), (0,)), ((), ()))
 F32, BF16 = jnp.float32, jnp.bfloat16
@@ -49,19 +49,6 @@
     )(*[pltpu.with_memory_space_constraint(a, HBM) if space == HBM else a for a, space in args])
 
 
-def pieces_of(x):
-    hi = x.astype(BF16)
-    rest = x - hi.astype(F32)
-    mid = rest.astype(BF16)
-    low = (rest - mid.astype(F32)).astype(BF16)
-    return [hi, mid, low]
-
-
-def joined(block, at):
-    rows = [block[3 * at + j : 3 * at + j + 1, :].astype(F32) for j in range(3)]
-    return rows[0] + (rows[1] + rows[2])
-
-
 def masked(scores, flags, first, own):
     return jnp.concatenate(
         [
@@ -73,8 +60,8 @@
 
 
 def forward_kernel(
-    flags, every, queries_far, cotangent_far, keys_far, values_far, parcel,
-    scores_at, expd, keys, values, queries, cotangent, sems,
+    flags, every, queries_far, cotangent_far, keys_far, values_far, features_far, stats,
+    scores_at, expd, keys, values, queries, cotangent, features, sems,
 ):
     block, width = keys.shape
     own = block // len(BLOCKS)
@@ -109,43 +96,39 @@
         e = jnp.exp(scores_at[here, :] - peak)
         expd[here, :] = e.astype(BF16)
         total += jnp.sum(e, axis=0, keepdims=True)
+    out = lax.dot_general(expd[...], values[...], TN, preferred_element_type=F32)
+    features[...] = out.astype(BF16)
+    store_f = pltpu.make_async_copy(features, features_far, sems.at[4])
+    store_f.start()
     fetch_g.wait()
-    ranks, deep = parcel.shape[0], parcel.shape[1]
-    quarter = rows // ranks
-    deltas = []
-    for r in range(ranks):
-        part = slice(quarter * r, quarter * (r + 1))
-        out = lax.dot_general(expd[:, part], values[...], TN, preferred_element_type=F32)
-        parcel[r, :quarter, :] = out.astype(BF16)
-        delta = jnp.sum(cotangent[part, :].astype(F32) * out, axis=1, keepdims=True)
-        deltas.append(jnp.transpose(jnp.broadcast_to(delta, (quarter, 128)))[0:1, :])
-    delta = jnp.concatenate(deltas, axis=1)
-    lines = pieces_of(peak) + pieces_of(total) + pieces_of(delta)
-    lines += [jnp.zeros((1, rows), BF16)] * (deep - quarter - len(lines))
-    lines = jnp.concatenate([x.astype(F32) for x in lines], axis=0).astype(BF16)
-    for r in range(ranks):
-        parcel[r, quarter:, :] = lines
+    delta = jnp.sum(cotangent[...].astype(F32) * out, axis=1, keepdims=True)
+    delta = jnp.transpose(jnp.broadcast_to(delta, (rows, 128)))[0:1, :]
+    for r in range(stats.shape[0]):
+        stats[r, 0:1, :] = peak
+        stats[r, 1:2, :] = total
+        stats[r, 2:3, :] = delta
     store_k.wait()
     store_v.wait()
-
-
-def merged(blocks):
-    peaks = [joined(b, 0) for b in blocks]
+    store_f.wait()
+
+
+def merged(stats):
+    peaks = [stats[i, 0:1, :] for i in range(stats.shape[0])]
     peak = peaks[0]
     for p in peaks[1:]:
         peak = jnp.maximum(peak, p)
     weights = [jnp.exp(p - peak) for p in peaks]
-    total = sum(w * joined(b, 1) for w, b in zip(weights, blocks))
-    return peak, total, weights
+    total = sum(w * stats[i, 1:2, :] for i, w in enumerate(weights))
+    delta = sum(w * stats[i, 2:3, :] for i, w in enumerate(weights))
+    return peak, total, delta
 
 
 def backward_kernel(
-    start, flags, parcels, keys_far, values_far, queries_far, cotangent_far, grads, ds_far,
+    start, flags, stats, keys_far, values_far, queries_far, cotangent_far, grads, ds_far,
     keys, values, queries, cotangent, ds_low, sems, key_sems, value_sems, store_sems,
 ):
     half, width = keys.shape
     scale = width ** (-0.5)
-    rows = queries.shape[0]
     own = 2 * half // len(BLOCKS)
     spots = range(0, half, CHUNK)
     there = [pl.ds(pl.multiple_of(start[0] + at, CHUNK), CHUNK) for at in spots]
@@ -167,10 +150,8 @@
     for k, v in zip(fetch_k[1:], fetch_v[1:]):
         k.start()
         v.start()
-    quarter = rows // parcels.shape[0]
-    blocks = [parcels[i, quarter:, :] for i in range(parcels.shape[0])]
-    peak, total, weights = merged(blocks)
-    delta = sum(w * joined(b, 2) for w, b in zip(weights, blocks)) / total
+    peak, total, delta = merged(stats)
+    delta = delta / total
     lse = peak + jnp.log(total)
     fetch_k[0].wait()
     fetch_q.wait()
@@ -203,41 +184,37 @@
 
 
 def outputs_kernel(
-    place, parcels, keys_far, keep_far, send_far, out, own_query, *rest
+    place, stats, own_stats, keys_far, features_far, keep_far, send_far, *rest
 ):
-    moved, (keys, low, sems) = rest[:3], rest[3:]
-    quarter, width = out.shape
-    half = low.shape[1]
-    phon, keep_at = place[0], place[1]
-    fetch_k = pltpu.make_async_copy(keys_far, keys, sems.at[0])
-    fetch_keep = pltpu.make_async_copy(keep_far, low.at[0], sems.at[1])
-    fetch_send = pltpu.make_async_copy(send_far, low.at[1], sems.at[2])
-    for f in (fetch_k, fetch_keep, fetch_send):
+    parts, (keys, features, low, gathered, sems) = rest[:4], rest[4:]
+    quarter = parts[0].shape[0]
+    half, rows = low.shape[1:]
+    width = keys.shape[1]
+    fetches = [
+        pltpu.make_async_copy(far, near, sems.at[i])
+        for i, (far, near) in enumerate(
+            ((keep_far, low.at[0]), (send_far, low.at[1]), (keys_far, keys),
+             (features_far, features))
+        )
+    ]
+    for f in fetches:
         f.start()
-    mine = pl.ds(pl.multiple_of(phon * quarter, quarter), quarter)
-    blocks = [parcels[i, quarter:, mine] for i in range(parcels.shape[0])]
-    _, total, weights = merged(blocks)
-    result = jnp.zeros((quarter, width), F32)
-    for i, w in enumerate(weights):
-        w = jnp.transpose(jnp.broadcast_to(w / total, (quarter, quarter)))
-        w = jnp.concatenate([w] * (width // quarter), axis=1)
-        result += w * parcels[i, :quarter, :].astype(F32)
-    result = result.astype(BF16)
-    out[...] = result
-    for f in (fetch_k, fetch_keep, fetch_send):
+    peak, total, _ = merged(stats)
+    share = jnp.exp(own_stats[0, 0:1, :] - peak) / total
+    for f in fetches[:3]:
         f.wait()
-    for d in range(4):
-        part = pl.ds(pl.multiple_of(((phon + d) & 3) * quarter, quarter), quarter)
-        query = jnp.zeros((quarter, width), F32)
-        for i, at in enumerate((keep_at, half - keep_at)):
-            right = keys[pl.ds(pl.multiple_of(at, half), half), :]
-            query += lax.dot_general(low[i, :, part], right, TN, preferred_element_type=F32)
-        query = (query * width ** (-0.5)).astype(BF16)
-        if d == 0:
-            own_query[...] = query
-        else:
-            moved[d - 1][:, :width] = query
-            moved[d - 1][:, width:] = result
+    query = jnp.zeros((rows, width), F32)
+    for i, at in enumerate((place[1], half - place[1])):
+        right = keys[pl.ds(pl.multiple_of(at, half), half), :]
+        query += lax.dot_general(low[i], right, TN, preferred_element_type=F32)
+    gathered[:, :width] = (query * width ** (-0.5)).astype(BF16)
+    fetches[3].wait()
+    share = jnp.transpose(jnp.broadcast_to(share, (128, rows)))
+    share = jnp.concatenate([share] * (width // 128), axis=1)
+    gathered[:, width:] = (features[...].astype(F32) * share).astype(BF16)
+    for d, part in enumerate(parts):
+        at = ((place[0] + d) & 3) * quarter
+        part[...] = gathered[pl.ds(pl.multiple_of(at, quarter), quarter), :]
 
 
 def add_kernel(keep, came, out, made, sems):
@@ -279,7 +256,6 @@
     half = block // 2
     ranks = lax.axis_size("phon")
     quarter = rows // ranks
-    deep = quarter + 16
     dma = pltpu.SemaphoreType.DMA
     near = [pltpu.VMEM((rows, width), BF16)] * 2
 
@@ -289,9 +265,10 @@
     tiles = phon * (block // TILE) + jnp.asarray(np.asarray(BLOCKS, np.int32) * own // TILE)
     flags = ((tiles >= band_first[0]) & (tiles < band_first[0] + NBAND)).astype(jnp.int32)
     work = 2 * block * rows * width
-    block_keys, block_values, parcel = call(
+    block_keys, block_values, features, stats = call(
         forward_kernel,
-        [((block, width), BF16, HBM)] * 2 + [((ranks, deep, width), BF16, VMEM)],
+        [((block, width), BF16, HBM)] * 2
+        + [((rows, width), BF16, HBM), ((ranks, 3, rows), F32, VMEM)],
         [(flags, SMEM), (every, VMEM), (queries, HBM), (cotangent, HBM)],
         [
             pltpu.VMEM((block, rows), F32),
@@ -299,11 +276,12 @@
             pltpu.VMEM((block, width), BF16),
             pltpu.VMEM((block, width), BF16),
             *near,
-            dma((4,)),
+            pltpu.VMEM((rows, width), BF16),
+            dma((5,)),
         ],
         2 * work,
     )
-    parcels = lax.all_to_all(parcel, "phon", 0, 0, tiled=True)
+    all_stats = lax.all_to_all(stats, "phon", 0, 0, tiled=True)
 
     def backward(start):
         return call(
@@ -312,7 +290,7 @@
             [
                 (jnp.reshape(start, (1,)).astype(jnp.int32), SMEM),
                 (flags, SMEM),
-                (parcels, VMEM),
+                (all_stats, VMEM),
                 (block_keys, HBM),
                 (block_values, HBM),
                 (queries, HBM),
@@ -340,28 +318,36 @@
     )
 
     place = jnp.stack([phon, core * half]).astype(jnp.int32)
-    mine_out, own_query, *parts = call(
+    parts = call(
         outputs_kernel,
-        [((quarter, width), BF16, VMEM)] * 2 + [((quarter, 2 * width), BF16, VMEM)] * 3,
+        [((quarter, 2 * width), BF16, VMEM)] * 4,
         [
             (place, SMEM),
-            (parcels, VMEM),
+            (all_stats, VMEM),
+            (stats, VMEM),
             (block_keys, HBM),
+            (features, HBM),
             (keep_ds, HBM),
             (send_ds, HBM),
         ],
-        [pltpu.VMEM((block, width), BF16), pltpu.VMEM((2, half, rows), BF16), dma((3,))],
+        [
+            pltpu.VMEM((block, width), BF16),
+            pltpu.VMEM((rows, width), BF16),
+            pltpu.VMEM((2, half, rows), BF16),
+            pltpu.VMEM((rows, 2 * width), BF16),
+            dma((4,)),
+        ],
         work,
     )
-    moved = [shifted(p, "phon", d) for d, p in zip((1, 2, 3), parts)]
+    moved = [parts[0]] + [shifted(p, "phon", d) for d, p in enumerate(parts) if d > 0]
 
     (second,) = call(sum_kernel, [((half // 4, 2 * width), BF16, VMEM)], [(first, VMEM)])
     second = lax.all_to_all(
         second.reshape(4, own, 2 * width), "frames", 0, 0, tiled=True,
         axis_index_groups=CROSSES,
     )
-    mine_query = f32_sum([own_query] + [m[:, :width] for m in moved]).astype(BF16)
-    spread = [mine_query] + [shifted(mine_query, "phon", d) for d in (1, 2, 3)]
+    mine = f32_sum(moved).astype(BF16)
+    spread = [mine] + [shifted(mine, "phon", d) for d in (1, 2, 3)]
 
     def placed(parts):
         whole = jnp.zeros((ranks, quarter, width), BF16)
@@ -369,8 +355,8 @@
             whole = lax.dynamic_update_index_in_dim(whole, p, (phon - d) & 3, 0)
         return whole.reshape(rows, width)
 
-    aligned = placed([mine_out] + [m[:, width:] for m in moved])
-    grad_query = placed(spread)
+    grad_query = placed([m[:, :width] for m in spread])
+    aligned = placed([m[:, width:] for m in spread])
     grad = f32_sum([second[i] for i in range(4)])
     return (aligned, grad_query, grad[:, :width], grad[:, width:])
 

time: 145 us -> 134 us (0.924)
  waiting for transfers between devices: 40.5 us -> 34.4 us
  local copies, waits for them, and re-layouts: 4.21 us -> 0.88 us
  Pallas kernels: 20.5 us -> 18.6 us
    all_to_all x1, waiting for transfers between devices: 10.7 us -> 5.45 us  [step(): all_stats = lax.all_to_all(stats, 'phon', 0, 0, tiled=True)]
    all_to_all x1, waiting for transfers between devices: 18.5 us -> 14.9 us  [step(): lax.all_to_all(second.reshape(4, own, 2 * width), 'frames', 0, 0, tiled=T...]
    pallas_call x1 -> x0, local copies, waits for them, and re-layouts: 3.34 us -> none  [call(): pl.pallas_call(kernel, out_shape=shapes, in_specs=[pl.BlockSpec(memory_sp...]
    ppermute x6, waiting for transfers between devices: 11.3 us -> 14 us  [shifted(): return lax.ppermute(value, axis, [(i, (i + d) % n) for i in range(n)])]
    pallas_call x5 -> x6, Pallas kernels: 20.5 us -> 18.6 us  [call(): pl.pallas_call(kernel, out_shape=shapes, in_specs=[pl.BlockSpec(memory_sp...]
  transfers between devices with their start and end apart: 10 -> 10, of which waited for: 4 -> 6; matrix products, arithmetic and copies ran while one was open for 3% -> 0% of each run, Pallas kernels for 5% -> 6%
where the time goes in v4:
time: 134 us; the launch traced here: 133 us
  blocking collectives  42.1 us (31%)
  waiting for transfers between devices  34.4 us (26%)
  starting transfers between devices  34.1 us (25%)
  Pallas kernels  18.6 us (14%)
  other arithmetic  1.69 us (1%)
  between operations  1.51 us (1%)
    all_gather x1, blocking collectives, step(): lax.all_gather(both.astype(jnp.float16), 'frames', axis=0, tiled=True)  42.1 us
    ppermute x6, starting transfers between devices, shifted(): return lax.ppermute(value, axis, [(i, (i + d) % n) for i in range(n)])  19.3 us
    pallas_call x6, Pallas kernels, call(): pl.pallas_call(kernel, out_shape=shapes, in_specs=[pl.BlockSpec(memory_sp...  18.6 us
    all_to_all x1, waiting for transfers between devices, step(): lax.all_to_all(second.reshape(4, own, 2 * width), 'frames', 0, 0, tiled=T...  14.9 us
    ppermute x6, waiting for transfers between devices, shifted(): return lax.ppermute(value, axis, [(i, (i + d) % n) for i in range(n)])  14 us
    all_to_all x1, waiting for transfers between devices, step(): all_stats = lax.all_to_all(stats, 'phon', 0, 0, tiled=True)  5.45 us
    all_to_all x1, starting transfers between devices, step(): lax.all_to_all(second.reshape(4, own, 2 * width), 'frames', 0, 0, tiled=T...  4.89 us
    all_to_all x1, starting transfers between devices, step(): all_stats = lax.all_to_all(stats, 'phon', 0, 0, tiled=True)  4.48 us
  transfers between devices with their start and end apart: 10, of which 6 were waited for; matrix products, arithmetic and copies ran while one was open for 0% of the time, Pallas kernels for 6%

profile of v4, /device:TPU:6, one launch (start us, length us, event | category | flops | bytes accessed | tf_op | source)
XLA Modules:
  0.0 133.2 jit_solution(3498212714427187554)
XLA Ops:
  1.3 0.8 multiply_convert_fusion.1
  2.1 42.1 %all-gather.1 = f16[1024,1024]{1,0:T(8,128)(2,1)S(1)} all-gather(f16[32,1024]{1,0:T(8,128)(2,1)S(1)} %multiply_convert_fusion.1), channel_id=1, replica_groups=mesh['frames'=32,'phon'=4,'chap'=4] {'frames'}, dimensions={0}, use_global_device_ids=true | all-gather | bytes 2162688 | tf_op jit(solution)/shard_map/all_gather | solution.py:263
  44.2 0.0 copy-start.2
  44.2 0.6 multiply_convert_fusion.every
  44.8 0.0 copy-done.2
  44.9 5.2 %shard_map.93 = (bf16[1024,512]{1,0:T(8,128)(2,1)}, bf16[1024,512]{1,0:T(8,128)(2,1)}, bf16[512,512]{1,0:T(8,128)(2,1)}, f32[4,3,512]{2,1,0:T(4,128)}) custom-call(s32[32]{0:T(128)S(1)} %and_convert_fusion.flags, bf16[1024,1024]{1,0:T(8,128)(2,1)S(1)} %multiply_convert_fusion.every, bf16[512,512]{1,0:T(8,128)(2,1)} %queries_far.5, bf16[512,512]{1,0:T(8,128)(2,1)} %cotangent_far.5), custom_call_target="tpu_custom_call" | custom-call | flops 1073741824 | bytes 5791872 | tf_op jit(solution)/shard_map/pallas_call | solution.py:41
  50.1 4.5 %all-to-all-start = ((f32[4,3,512]{2,1,0:T(4,128)}), f32[4,3,512]{2,1,0:T(4,128)S(1)}, u32[]{:S(2)}, u32[]{:S(2)}) async-start(f32[4,3,512]{2,1,0:T(4,128)} %get-tuple-element.16.own_stats), calls=%async_computation | async-start | bytes 65536 | tf_op jit(solution)/shard_map/all_to_all | solution.py:284
  54.6 5.5 %all-to-all-done.stats = f32[4,3,512]{2,1,0:T(4,128)S(1)} async-done(((f32[4,3,512]{2,1,0:T(4,128)}), f32[4,3,512]{2,1,0:T(4,128)S(1)}, u32[]{:S(2)}, u32[]{:S(2)}) %all-to-all-start) | async-done | bytes 24608 | tf_op jit(solution)/shard_map/all_to_all | solution.py:284
  60.0 4.1 %shard_map.95 = (bf16[512,1024]{1,0:T(8,128)(2,1)S(1)}, bf16[512,512]{1,0:T(8,128)(2,1)}) custom-call(s32[1]{0:T(128)} %bitcast.3.start, s32[32]{0:T(128)S(1)} %and_convert_fusion.flags, f32[4,3,512]{2,1,0:T(4,128)S(1)} %all-to-all-done.stats, bf16[1024,512]{1,0:T(8,128)(2,1)} %get-tuple-element.17.keys_far, bf16[1024,512]{1,0:T(8,128)(2,1)} %get-tuple-element.19.values_far, ...), custom_call_target="tpu_custom_call" | custom-call | flops 1073741824 | bytes 4743300 | tf_op jit(solution)/shard_map/pallas_call | solution.py:41
  64.1 1.9 %collective-permute-start.6 = (bf16[512,1024]{1,0:T(8,128)(2,1)S(1)}, bf16[512,1024]{1,0:T(8,128)(2,1)S(1)}, u32[]{:S(2)}, u32[]{:S(2)}) collective-permute-start(bf16[512,1024]{1,0:T(8,128)(2,1)S(1)} %get-tuple-element.27), channel_id=1, source_target_pairs={{0,16},{16,0},{32,48},{48,32},{64,80},{80,64},{96,112},{112,96},{1... | collective-permute-start | bytes 3145736 | tf_op jit(solution)/shard_map/ppermute | solution.py:307
  66.0 4.1 %shard_map.94 = (bf16[512,1024]{1,0:T(8,128)(2,1)S(1)}, bf16[512,512]{1,0:T(8,128)(2,1)}) custom-call(s32[1]{0:T(128)} %bitcast.1.start, s32[32]{0:T(128)S(1)} %and_convert_fusion.flags, f32[4,3,512]{2,1,0:T(4,128)S(1)} %all-to-all-done.stats, bf16[1024,512]{1,0:T(8,128)(2,1)} %get-tuple-element.17.keys_far, bf16[1024,512]{1,0:T(8,128)(2,1)} %get-tuple-element.19.values_far, ...), custom_call_target="tpu_custom_call" | custom-call | flops 1073741824 | bytes 4743300 | tf_op jit(solution)/shard_map/pallas_call | solution.py:41
  70.2 0.0 collective-permute-done.6.came
  70.2 1.1 shard_map.97
  71.2 3.5 %all-to-all-start.1 = ((bf16[4,128,1024]{2,1,0:T(8,128)(2,1)}), bf16[4,128,1024]{2,1,0:T(8,128)(2,1)S(1)}, u32[]{:S(2)}, u32[]{:S(2)}) async-start(bf16[4,128,1024]{2,1,0:T(8,128)(2,1)} %bitcast.44), calls=%async_computation.1 | async-start | bytes 2097152 | tf_op jit(solution)/shard_map/all_to_all | solution.py:315
  74.8 0.1 pad_add_fusion.place
  74.9 3.3 %shard_map.96 = (bf16[128,1024]{1,0:T(8,128)(2,1)S(1)}, bf16[128,1024]{1,0:T(8,128)(2,1)S(1)}, bf16[128,1024]{1,0:T(8,128)(2,1)S(1)}, bf16[128,1024]{1,0:T(8,128)(2,1)S(1)}) custom-call(s32[2]{0:T(128)S(1)} %pad_add_fusion.place, f32[4,3,512]{2,1,0:T(4,128)S(1)} %all-to-all-done.stats, f32[4,3,512]{2,1,0:T(4,128)} %get-tuple-element.16.own_stats, ...), custom_call_target="tpu_custom_call" | custom-call | flops 536870912 | bytes 3719176 | tf_op jit(solution)/shard_map/pallas_call | solution.py:41
  78.2 2.5 %collective-permute-start = (bf16[128,1024]{1,0:T(8,128)(2,1)S(1)}, bf16[128,1024]{1,0:T(8,128)(2,1)S(1)}, u32[]{:S(2)}, u32[]{:S(2)}) collective-permute-start(bf16[128,1024]{1,0:T(8,128)(2,1)S(1)} %get-tuple-element.23), channel_id=1, source_target_pairs={{0,4},{4,8},{8,12},{12,0},{1,5},{5,9},{9,13},{13,1},{2,6},{6,10},{... | collective-permute-start | bytes 786440 | tf_op jit(solution)/shard_map/ppermute | solution.py:239
  80.6 4.0 %collective-permute-start.1 = (bf16[128,1024]{1,0:T(8,128)(2,1)S(1)}, bf16[128,1024]{1,0:T(8,128)(2,1)S(1)}, u32[]{:S(2)}, u32[]{:S(2)}) collective-permute-start(bf16[128,1024]{1,0:T(8,128)(2,1)S(1)} %get-tuple-element.24), channel_id=1, source_target_pairs={{0,8},{4,12},{8,0},{12,4},{1,9},{5,13},{9,1},{13,5},{2,10},{6,14},... | collective-permute-start | bytes 786440 | tf_op jit(solution)/shard_map/ppermute | solution.py:239
  84.6 3.0 %collective-permute-start.2 = (bf16[128,1024]{1,0:T(8,128)(2,1)S(1)}, bf16[128,1024]{1,0:T(8,128)(2,1)S(1)}, u32[]{:S(2)}, u32[]{:S(2)}) collective-permute-start(bf16[128,1024]{1,0:T(8,128)(2,1)S(1)} %get-tuple-element.25), channel_id=1, source_target_pairs={{0,12},{4,0},{8,4},{12,8},{1,13},{5,1},{9,5},{13,9},{2,14},{6,2},{... | collective-permute-start | bytes 786440 | tf_op jit(solution)/shard_map/ppermute | solution.py:239
  87.6 8.1 %collective-permute-done = bf16[128,1024]{1,0:T(8,128)(2,1)S(1)} collective-permute-done((bf16[128,1024]{1,0:T(8,128)(2,1)S(1)}, bf16[128,1024]{1,0:T(8,128)(2,1)S(1)}, u32[]{:S(2)}, u32[]{:S(2)}) %collective-permute-start) | collective-permute-done | bytes 262176 | tf_op jit(solution)/shard_map/ppermute | solution.py:239
  95.7 0.0 collective-permute-done.1
  95.7 2.5 %collective-permute-done.2 = bf16[128,1024]{1,0:T(8,128)(2,1)S(1)} collective-permute-done((bf16[128,1024]{1,0:T(8,128)(2,1)S(1)}, bf16[128,1024]{1,0:T(8,128)(2,1)S(1)}, u32[]{:S(2)}, u32[]{:S(2)}) %collective-permute-start.2) | collective-permute-done | bytes 262176 | tf_op jit(solution)/shard_map/ppermute | solution.py:239
  98.2 0.2 add_convert_fusion
  98.4 2.3 %collective-permute-start.3 = (bf16[128,1024]{1,0:T(8,128)(2,1)S(1)}, bf16[128,1024]{1,0:T(8,128)(2,1)S(1)}, u32[]{:S(2)}, u32[]{:S(2)}) collective-permute-start(bf16[128,1024]{1,0:T(8,128)(2,1)S(1)} %add_convert_fusion), channel_id=1, source_target_pairs={{0,4},{4,8},{8,12},{12,0},{1,5},{5,9},{9,13},{13,1},{2,6},{6,10},{... | collective-permute-start | bytes 786440 | tf_op jit(solution)/shard_map/ppermute | solution.py:239
  100.8 5.6 %collective-permute-start.4 = (bf16[128,1024]{1,0:T(8,128)(2,1)S(1)}, bf16[128,1024]{1,0:T(8,128)(2,1)S(1)}, u32[]{:S(2)}, u32[]{:S(2)}) collective-permute-start(bf16[128,1024]{1,0:T(8,128)(2,1)S(1)} %add_convert_fusion), channel_id=1, source_target_pairs={{0,8},{4,12},{8,0},{12,4},{1,9},{5,13},{9,1},{13,5},{2,10},{6,14},... | collective-permute-start | bytes 786440 | tf_op jit(solution)/shard_map/ppermute | solution.py:239
  106.3 1.9 %collective-permute-start.5 = (bf16[128,1024]{1,0:T(8,128)(2,1)S(1)}, bf16[128,1024]{1,0:T(8,128)(2,1)S(1)}, u32[]{:S(2)}, u32[]{:S(2)}) collective-permute-start(bf16[128,1024]{1,0:T(8,128)(2,1)S(1)} %add_convert_fusion), channel_id=1, source_target_pairs={{0,12},{4,0},{8,4},{12,8},{1,13},{5,1},{9,5},{13,9},{2,14},{6,2},{... | collective-permute-start | bytes 786440 | tf_op jit(solution)/shard_map/ppermute | solution.py:239
  108.3 0.0 all-to-all-done.1.came
  108.4 0.8 shard_map.98
  109.2 4.9 %all-to-all-start.2 = ((bf16[4,32,1024]{2,1,0:T(8,128)(2,1)}), bf16[4,32,1024]{2,1,0:T(8,128)(2,1)S(1)}, u32[]{:S(2)}, u32[]{:S(2)}) async-start(bf16[4,32,1024]{2,1,0:T(8,128)(2,1)} %bitcast.15), calls=%async_computation.2 | async-start | bytes 524288 | tf_op jit(solution)/shard_map/all_to_all | solution.py:345
  114.1 0.0 collective-permute-done.3
  114.2 2.1 %collective-permute-done.4 = bf16[128,1024]{1,0:T(8,128)(2,1)S(1)} collective-permute-done((bf16[128,1024]{1,0:T(8,128)(2,1)S(1)}, bf16[128,1024]{1,0:T(8,128)(2,1)S(1)}, u32[]{:S(2)}, u32[]{:S(2)}) %collective-permute-start.4) | collective-permute-done | bytes 262176 | tf_op jit(solution)/shard_map/ppermute | solution.py:239
  116.3 1.3 collective-permute-done.5
  117.6 0.0 copy-start
  117.6 0.0 copy-start.1
  117.6 14.9 %all-to-all-done.2 = bf16[4,32,1024]{2,1,0:T(8,128)(2,1)S(1)} async-done(((bf16[4,32,1024]{2,1,0:T(8,128)(2,1)}), bf16[4,32,1024]{2,1,0:T(8,128)(2,1)S(1)}, u32[]{:S(2)}, u32[]{:S(2)}) %all-to-all-start.2) | async-done | bytes 262176 | tf_op jit(solution)/shard_map/all_to_all | solution.py:345
  132.6 0.7 fusion.8
  133.2 0.0 copy-done
  133.2 0.0 copy-done.1
  (9 shorter events, 0.2 us)
Async XLA Ops:
  44.2 0.7 copy-start.2
  50.1 9.9 %all-to-all-start = ((f32[4,3,512]{2,1,0:T(4,128)}), f32[4,3,512]{2,1,0:T(4,128)S(1)}, u32[]{:S(2)}, u32[]{:S(2)}) async-start(f32[4,3,512]{2,1,0:T(4,128)} %get-tuple-element.16.own_stats), calls=%async_computation | async-start | bytes 65536 | tf_op jit(solution)/shard_map/all_to_all | solution.py:284
  64.1 6.0 %collective-permute-start.6 = (bf16[512,1024]{1,0:T(8,128)(2,1)S(1)}, bf16[512,1024]{1,0:T(8,128)(2,1)S(1)}, u32[]{:S(2)}, u32[]{:S(2)}) collective-permute-start(bf16[512,1024]{1,0:T(8,128)(2,1)S(1)} %get-tuple-element.27), channel_id=1, source_target_pairs={{0,16},{16,0},{32,48},{48,32},{64,80},{80,64},{96,112},{112,96},{1... | collective-permute-start | bytes 3145736 | tf_op jit(solution)/shard_map/ppermute | solution.py:307
  71.2 37.1 %all-to-all-start.1 = ((bf16[4,128,1024]{2,1,0:T(8,128)(2,1)}), bf16[4,128,1024]{2,1,0:T(8,128)(2,1)S(1)}, u32[]{:S(2)}, u32[]{:S(2)}) async-start(bf16[4,128,1024]{2,1,0:T(8,128)(2,1)} %bitcast.44), calls=%async_computation.1 | async-start | bytes 2097152 | tf_op jit(solution)/shard_map/all_to_all | solution.py:315
  78.2 17.6 %collective-permute-start = (bf16[128,1024]{1,0:T(8,128)(2,1)S(1)}, bf16[128,1024]{1,0:T(8,128)(2,1)S(1)}, u32[]{:S(2)}, u32[]{:S(2)}) collective-permute-start(bf16[128,1024]{1,0:T(8,128)(2,1)S(1)} %get-tuple-element.23), channel_id=1, source_target_pairs={{0,4},{4,8},{8,12},{12,0},{1,5},{5,9},{9,13},{13,1},{2,6},{6,10},{... | collective-permute-start | bytes 786440 | tf_op jit(solution)/shard_map/ppermute | solution.py:239
  80.6 15.1 %collective-permute-start.1 = (bf16[128,1024]{1,0:T(8,128)(2,1)S(1)}, bf16[128,1024]{1,0:T(8,128)(2,1)S(1)}, u32[]{:S(2)}, u32[]{:S(2)}) collective-permute-start(bf16[128,1024]{1,0:T(8,128)(2,1)S(1)} %get-tuple-element.24), channel_id=1, source_target_pairs={{0,8},{4,12},{8,0},{12,4},{1,9},{5,13},{9,1},{13,5},{2,10},{6,14},... | collective-permute-start | bytes 786440 | tf_op jit(solution)/shard_map/ppermute | solution.py:239
  84.6 13.6 %collective-permute-start.2 = (bf16[128,1024]{1,0:T(8,128)(2,1)S(1)}, bf16[128,1024]{1,0:T(8,128)(2,1)S(1)}, u32[]{:S(2)}, u32[]{:S(2)}) collective-permute-start(bf16[128,1024]{1,0:T(8,128)(2,1)S(1)} %get-tuple-element.25), channel_id=1, source_target_pairs={{0,12},{4,0},{8,4},{12,8},{1,13},{5,1},{9,5},{13,9},{2,14},{6,2},{... | collective-permute-start | bytes 786440 | tf_op jit(solution)/shard_map/ppermute | solution.py:239
  98.4 15.7 %collective-permute-start.3 = (bf16[128,1024]{1,0:T(8,128)(2,1)S(1)}, bf16[128,1024]{1,0:T(8,128)(2,1)S(1)}, u32[]{:S(2)}, u32[]{:S(2)}) collective-permute-start(bf16[128,1024]{1,0:T(8,128)(2,1)S(1)} %add_convert_fusion), channel_id=1, source_target_pairs={{0,4},{4,8},{8,12},{12,0},{1,5},{5,9},{9,13},{13,1},{2,6},{6,10},{... | collective-permute-start | bytes 786440 | tf_op jit(solution)/shard_map/ppermute | solution.py:239
  100.8 15.5 %collective-permute-start.4 = (bf16[128,1024]{1,0:T(8,128)(2,1)S(1)}, bf16[128,1024]{1,0:T(8,128)(2,1)S(1)}, u32[]{:S(2)}, u32[]{:S(2)}) collective-permute-start(bf16[128,1024]{1,0:T(8,128)(2,1)S(1)} %add_convert_fusion), channel_id=1, source_target_pairs={{0,8},{4,12},{8,0},{12,4},{1,9},{5,13},{9,1},{13,5},{2,10},{6,14},... | collective-permute-start | bytes 786440 | tf_op jit(solution)/shard_map/ppermute | solution.py:239
  106.3 11.2 %collective-permute-start.5 = (bf16[128,1024]{1,0:T(8,128)(2,1)S(1)}, bf16[128,1024]{1,0:T(8,128)(2,1)S(1)}, u32[]{:S(2)}, u32[]{:S(2)}) collective-permute-start(bf16[128,1024]{1,0:T(8,128)(2,1)S(1)} %add_convert_fusion), channel_id=1, source_target_pairs={{0,12},{4,0},{8,4},{12,8},{1,13},{5,1},{9,5},{13,9},{2,14},{6,2},{... | collective-permute-start | bytes 786440 | tf_op jit(solution)/shard_map/ppermute | solution.py:239
  109.2 23.4 %all-to-all-start.2 = ((bf16[4,32,1024]{2,1,0:T(8,128)(2,1)}), bf16[4,32,1024]{2,1,0:T(8,128)(2,1)S(1)}, u32[]{:S(2)}, u32[]{:S(2)}) async-start(bf16[4,32,1024]{2,1,0:T(8,128)(2,1)} %bitcast.15), calls=%async_computation.2 | async-start | bytes 524288 | tf_op jit(solution)/shard_map/all_to_all | solution.py:345
  117.6 15.7 %copy-start = (bf16[4,128,512]{2,1,0:T(8,128)(2,1)}, bf16[4,128,512]{2,1,0:T(8,128)(2,1)S(1)}, u32[]{:S(2)}) copy-start(bf16[4,128,512]{2,1,0:T(8,128)(2,1)S(1)} %get-tuple-element.28) | copy-start | bytes 1572868
  117.6 15.6 %copy-start.1 = (bf16[4,128,512]{2,1,0:T(8,128)(2,1)}, bf16[4,128,512]{2,1,0:T(8,128)(2,1)S(1)}, u32[]{:S(2)}) copy-start(bf16[4,128,512]{2,1,0:T(8,128)(2,1)S(1)} %get-tuple-element.29) | copy-start | bytes 1572868

commit v5 on v4

--- a/solution.py
+++ b/solution.py
@@ -60,8 +60,8 @@
 
 
 def forward_kernel(
-    flags, every, queries_far, cotangent_far, keys_far, values_far, features_far, stats,
-    scores_at, expd, keys, values, queries, cotangent, features, sems,
+    flags, every, queries_far, cotangent_far, keys, values, features_far, stats,
+    scores_at, expd, queries, cotangent, features, sems,
 ):
     block, width = keys.shape
     own = block // len(BLOCKS)
@@ -86,10 +86,6 @@
         scores = masked(raw * scale + offset, flags, at // own, own)
         scores_at[here, :] = scores
         peak = jnp.maximum(peak, jnp.max(scores, axis=0, keepdims=True))
-    store_k = pltpu.make_async_copy(keys, keys_far, sems.at[2])
-    store_v = pltpu.make_async_copy(values, values_far, sems.at[3])
-    store_k.start()
-    store_v.start()
     total = jnp.zeros_like(peak)
     for at in range(0, block, CHUNK):
         here = slice(at, at + CHUNK)
@@ -98,134 +94,124 @@
         total += jnp.sum(e, axis=0, keepdims=True)
     out = lax.dot_general(expd[...], values[...], TN, preferred_element_type=F32)
     features[...] = out.astype(BF16)
-    store_f = pltpu.make_async_copy(features, features_far, sems.at[4])
+    store_f = pltpu.make_async_copy(features, features_far, sems.at[2])
     store_f.start()
     fetch_g.wait()
     delta = jnp.sum(cotangent[...].astype(F32) * out, axis=1, keepdims=True)
     delta = jnp.transpose(jnp.broadcast_to(delta, (rows, 128)))[0:1, :]
-    for r in range(stats.shape[0]):
-        stats[r, 0:1, :] = peak
-        stats[r, 1:2, :] = total
-        stats[r, 2:3, :] = delta
-    store_k.wait()
-    store_v.wait()
+    stats[0:1, :] = peak
+    stats[1:2, :] = total
+    stats[2:3, :] = delta
     store_f.wait()
 
 
-def merged(stats):
-    peaks = [stats[i, 0:1, :] for i in range(stats.shape[0])]
+def merged(heard):
+    peaks = [stats[0:1, :] for stats in heard]
     peak = peaks[0]
     for p in peaks[1:]:
         peak = jnp.maximum(peak, p)
     weights = [jnp.exp(p - peak) for p in peaks]
-    total = sum(w * stats[i, 1:2, :] for i, w in enumerate(weights))
-    delta = sum(w * stats[i, 2:3, :] for i, w in enumerate(weights))
-    return peak, total, delta
+    total = sum(w * stats[1:2, :] for w, stats in zip(weights, heard))
+    delta = sum(w * stats[2:3, :] for w, stats in zip(weights, heard))
+    return peak, jnp.maximum(total, 0.5), delta
 
 
 def backward_kernel(
-    start, flags, stats, keys_far, values_far, queries_far, cotangent_far, grads, ds_far,
-    keys, values, queries, cotangent, ds_low, sems, key_sems, value_sems, store_sems,
+    start, flags, stats, stats_up, stats_down, keys, values, queries_far, cotangent_far,
+    grads_out, ds_far, queries, cotangent, grads, ds_low, sems,
 ):
-    half, width = keys.shape
+    half, width = grads.shape[0], keys.shape[1]
     scale = width ** (-0.5)
     own = 2 * half // len(BLOCKS)
-    spots = range(0, half, CHUNK)
-    there = [pl.ds(pl.multiple_of(start[0] + at, CHUNK), CHUNK) for at in spots]
-    here = [pl.ds(at, CHUNK) for at in spots]
+    mine = pl.ds(pl.multiple_of(start[0], half), half)
     fetch_q = pltpu.make_async_copy(queries_far, queries, sems.at[0])
     fetch_g = pltpu.make_async_copy(cotangent_far, cotangent, sems.at[1])
-    fetch_k = [
-        pltpu.make_async_copy(keys_far.at[t], keys.at[h], key_sems.at[i])
-        for i, (t, h) in enumerate(zip(there, here))
-    ]
-    fetch_v = [
-        pltpu.make_async_copy(values_far.at[t], values.at[h], value_sems.at[i])
-        for i, (t, h) in enumerate(zip(there, here))
-    ]
-    fetch_k[0].start()
     fetch_q.start()
     fetch_g.start()
-    fetch_v[0].start()
-    for k, v in zip(fetch_k[1:], fetch_v[1:]):
-        k.start()
-        v.start()
-    peak, total, delta = merged(stats)
+    peak, total, delta = merged((stats, stats_up, stats_down))
     delta = delta / total
     lse = peak + jnp.log(total)
-    fetch_k[0].wait()
+    low_key = keys[mine, :]
+    key = low_key.astype(F32)
+    offset = jnp.sum(key * key, axis=1, keepdims=True) * (-0.5 * scale)
     fetch_q.wait()
-    stores = []
-    for i, spot in enumerate(here):
-        if i > 0:
-            fetch_k[i].wait()
-        low_key = keys[spot, :]
-        key = low_key.astype(F32)
-        offset = jnp.sum(key * key, axis=1, keepdims=True) * (-0.5 * scale)
-        raw = lax.dot_general(low_key, queries[...], NT, preferred_element_type=F32)
-        scores = masked(raw * scale + offset, flags, start[0] // own + i * CHUNK // own, own)
-        probs = jnp.exp(scores - lse)
-        if i == 0:
-            fetch_g.wait()
-        value = jnp.dot(probs.astype(BF16), cotangent[...], preferred_element_type=F32)
-        grads[spot, width:] = value.astype(BF16)
-        fetch_v[i].wait()
-        dp = lax.dot_general(values[spot, :], cotangent[...], NT, preferred_element_type=F32)
-        ds = probs * (dp - delta)
-        low = ds.astype(BF16)
-        ds_low[spot, :] = low
-        stores.append(pltpu.make_async_copy(ds_low.at[spot], ds_far.at[spot], store_sems.at[i]))
-        stores[-1].start()
-        column = jnp.sum(ds, axis=1, keepdims=True)
-        grad = jnp.dot(low, queries[...], preferred_element_type=F32)
-        grads[spot, :width] = ((grad - column * key) * scale).astype(BF16)
-    for store in stores:
-        store.wait()
+    raw = lax.dot_general(low_key, queries[...], NT, preferred_element_type=F32)
+    fetch_g.wait()
+    dp = lax.dot_general(values[mine, :], cotangent[...], NT, preferred_element_type=F32)
+    scores = masked(raw * scale + offset, flags, start[0] // own, own)
+    probs = jnp.exp(scores - lse)
+    value = jnp.dot(probs.astype(BF16), cotangent[...], preferred_element_type=F32)
+    grads[:, width:] = value.astype(BF16)
+    right = pl.ds(width, width)
+    store_value = pltpu.make_async_copy(grads.at[:, right], grads_out.at[:, right], sems.at[4])
+    store_value.start()
+    ds = probs * (dp - delta)
+    low = ds.astype(BF16)
+    ds_low[...] = low
+    store_ds = pltpu.make_async_copy(ds_low, ds_far, sems.at[2])
+    store_ds.start()
+    column = jnp.sum(ds, axis=1, keepdims=True)
+    grad = jnp.dot(low, queries[...], preferred_element_type=F32)
+    grads[:, :width] = ((grad - column * keys[mine, :].astype(F32)) * scale).astype(BF16)
+    left = pl.ds(0, width)
+    store_key = pltpu.make_async_copy(grads.at[:, left], grads_out.at[:, left], sems.at[3])
+    store_key.start()
+    store_ds.wait()
+    store_value.wait()
+    store_key.wait()
 
 
 def outputs_kernel(
-    place, stats, own_stats, keys_far, features_far, keep_far, send_far, *rest
+    place, stats, stats_up, stats_down, keys, features_far, keep_far, send_far, *rest
 ):
-    parts, (keys, features, low, gathered, sems) = rest[:4], rest[4:]
+    parts, (features, low, gathered, sems) = rest[:4], rest[4:]
     quarter = parts[0].shape[0]
     half, rows = low.shape[1:]
     width = keys.shape[1]
     fetches = [
         pltpu.make_async_copy(far, near, sems.at[i])
         for i, (far, near) in enumerate(
-            ((keep_far, low.at[0]), (send_far, low.at[1]), (keys_far, keys),
-             (features_far, features))
+            ((features_far, features), (keep_far, low.at[0]), (send_far, low.at[1]))
         )
     ]
     for f in fetches:
         f.start()
-    peak, total, _ = merged(stats)
-    share = jnp.exp(own_stats[0, 0:1, :] - peak) / total
-    for f in fetches[:3]:
-        f.wait()
+    peak, total, _ = merged((stats, stats_up, stats_down))
+    share = jnp.exp(stats[0:1, :] - peak) / total
+    share = jnp.transpose(jnp.broadcast_to(share, (128, rows)))
+    share = jnp.concatenate([share] * (width // 128), axis=1)
+    fetches[0].wait()
+    gathered[:, width:] = (features[...].astype(F32) * share).astype(BF16)
     query = jnp.zeros((rows, width), F32)
     for i, at in enumerate((place[1], half - place[1])):
+        fetches[i + 1].wait()
         right = keys[pl.ds(pl.multiple_of(at, half), half), :]
         query += lax.dot_general(low[i], right, TN, preferred_element_type=F32)
     gathered[:, :width] = (query * width ** (-0.5)).astype(BF16)
-    fetches[3].wait()
-    share = jnp.transpose(jnp.broadcast_to(share, (128, rows)))
-    share = jnp.concatenate([share] * (width // 128), axis=1)
-    gathered[:, width:] = (features[...].astype(F32) * share).astype(BF16)
     for d, part in enumerate(parts):
         at = ((place[0] + d) & 3) * quarter
         part[...] = gathered[pl.ds(pl.multiple_of(at, quarter), quarter), :]
 
 
-def add_kernel(keep, came, out, made, sems):
-    n = sems.shape[0]
+def add_kernel(keep_far, came_far, out, keep, came, sems):
+    n = sems.shape[1]
     size = keep.shape[0] // n
-    stores = []
-    for i in range(n):
-        part = pl.ds(size * i, size)
-        made[part, :] = (keep[part, :].astype(F32) + came[part, :].astype(F32)).astype(BF16)
-        stores.append(pltpu.make_async_copy(made.at[part], out.at[part], sems.at[i]))
-        stores[-1].start()
+    parts = [pl.ds(size * i, size) for i in range(n)]
+    copy = pltpu.make_async_copy
+    fetches = [
+        (copy(keep_far.at[p], keep.at[p], sems.at[0, i]),
+         copy(came_far.at[p], came.at[p], sems.at[1, i]))
+        for i, p in enumerate(parts)
+    ]
+    stores = [copy(keep.at[p], out.at[p], sems.at[2, i]) for i, p in enumerate(parts)]
+    for a, b in fetches:
+        a.start()
+        b.start()
+    for i, p in enumerate(parts):
+        for f in fetches[i]:
+            f.wait()
+        keep[p, :] = (keep[p, :].astype(F32) + came[p, :].astype(F32)).astype(BF16)
+        stores[i].start()
     for store in stores:
         store.wait()
 
@@ -267,39 +253,38 @@
     work = 2 * block * rows * width
     block_keys, block_values, features, stats = call(
         forward_kernel,
-        [((block, width), BF16, HBM)] * 2
-        + [((rows, width), BF16, HBM), ((ranks, 3, rows), F32, VMEM)],
+        [((block, width), BF16, VMEM)] * 2 + [((rows, width), BF16, HBM), ((3, rows), F32, VMEM)],
         [(flags, SMEM), (every, VMEM), (queries, HBM), (cotangent, HBM)],
         [
             pltpu.VMEM((block, rows), F32),
             pltpu.VMEM((block, rows), BF16),
-            pltpu.VMEM((block, width), BF16),
-            pltpu.VMEM((block, width), BF16),
             *near,
             pltpu.VMEM((rows, width), BF16),
-            dma((5,)),
+            dma((3,)),
         ],
         2 * work,
     )
-    all_stats = lax.all_to_all(stats, "phon", 0, 0, tiled=True)
+    heard = [(stats, VMEM), (shifted(stats, "phon", 1), VMEM), (shifted(stats, "phon", 3), VMEM)]
 
     def backward(start):
         return call(
             backward_kernel,
-            [((half, 2 * width), BF16, VMEM), ((half, rows), BF16, HBM)],
+            [((half, 2 * width), BF16, HBM), ((half, rows), BF16, HBM)],
             [
                 (jnp.reshape(start, (1,)).astype(jnp.int32), SMEM),
                 (flags, SMEM),
-                (all_stats, VMEM),
-                (block_keys, HBM),
-                (block_values, HBM),
+                *heard,
+                (block_keys, VMEM),
+                (block_values, VMEM),
                 (queries, HBM),
                 (cotangent, HBM),
             ],
-            [pltpu.VMEM((half, width), BF16)] * 2
-            + near
-            + [pltpu.VMEM((half, rows), BF16), dma((2,))]
-            + [dma((half // CHUNK,))] * 3,
+            near
+            + [
+                pltpu.VMEM((half, 2 * width), BF16),
+                pltpu.VMEM((half, rows), BF16),
+                dma((5,)),
+            ],
             2 * work,
         )
 
@@ -309,8 +294,8 @@
     (first,) = call(
         add_kernel,
         [((half, 2 * width), BF16, HBM)],
-        [(keep, VMEM), (came, VMEM)],
-        [pltpu.VMEM((half, 2 * width), BF16), dma((4,))],
+        [(keep, HBM), (came, HBM)],
+        [pltpu.VMEM((half, 2 * width), BF16)] * 2 + [dma((3, 4))],
     )
     first = lax.all_to_all(
         first.reshape(4, half // 4, 2 * width), "frames", 0, 0, tiled=True,
@@ -323,23 +308,21 @@
         [((quarter, 2 * width), BF16, VMEM)] * 4,
         [
             (place, SMEM),
-            (all_stats, VMEM),
-            (stats, VMEM),
-            (block_keys, HBM),
+            *heard,
+            (block_keys, VMEM),
             (features, HBM),
             (keep_ds, HBM),
             (send_ds, HBM),
         ],
         [
-            pltpu.VMEM((block, width), BF16),
             pltpu.VMEM((rows, width), BF16),
             pltpu.VMEM((2, half, rows), BF16),
             pltpu.VMEM((rows, 2 * width), BF16),
-            dma((4,)),
+            dma((3,)),
         ],
         work,
     )
-    moved = [parts[0]] + [shifted(p, "phon", d) for d, p in enumerate(parts) if d > 0]
+    moved = [parts[0]] + [shifted(parts[d], "phon", d) for d in (2, 1, 3)]
 
     (second,) = call(sum_kernel, [((half // 4, 2 * width), BF16, VMEM)], [(first, VMEM)])
     second = lax.all_to_all(

time: 134 us -> 133 us (level)
  waiting for transfers between devices: 34.4 us -> 26.9 us
  starting transfers between devices: 34.1 us -> 40 us
    ppermute x6 -> x8, starting transfers between devices: 19.3 us -> 30 us  [shifted(): return lax.ppermute(value, axis, [(i, (i + d) % n) for i in range(n)])]
    all_to_all x1 -> x0, waiting for transfers between devices: 5.45 us -> none  [step(): all_stats = lax.all_to_all(stats, 'phon', 0, 0, tiled=True)]
    all_to_all x1 -> x0, starting transfers between devices: 4.48 us -> none  [step(): all_stats = lax.all_to_all(stats, 'phon', 0, 0, tiled=True)]
    ppermute x6 -> x8, waiting for transfers between devices: 14 us -> 10.7 us  [shifted(): return lax.ppermute(value, axis, [(i, (i + d) % n) for i in range(n)])]
  transfers between devices with their start and end apart: 10 -> 11, of which waited for: 6 -> 7; matrix products, arithmetic and copies ran while one was open for 0% -> 0% of each run, Pallas kernels for 6% -> 6%
where the time goes in v5:
time: 133 us
  blocking collectives  42.1 us (32%)
  starting transfers between devices  40 us (30%)
  waiting for transfers between devices  26.9 us (20%)
  Pallas kernels  18.6 us (14%)
  local copies, waits for them, and re-layouts  1.87 us (1%)
  other arithmetic  1.69 us (1%)
  between operations  1.55 us (1%)
    all_gather x1, blocking collectives, step(): lax.all_gather(both.astype(jnp.float16), 'frames', axis=0, tiled=True)  42.1 us
    ppermute x8, starting transfers between devices, shifted(): return lax.ppermute(value, axis, [(i, (i + d) % n) for i in range(n)])  30 us
    pallas_call x6, Pallas kernels, call(): pl.pallas_call(kernel, out_shape=shapes, in_specs=[pl.BlockSpec(memory_sp...  18.6 us
    all_to_all x1, waiting for transfers between devices, step(): lax.all_to_all(second.reshape(4, own, 2 * width), 'frames', 0, 0, tiled=T...  16.2 us
    ppermute x8, waiting for transfers between devices, shifted(): return lax.ppermute(value, axis, [(i, (i + d) % n) for i in range(n)])  10.7 us
    all_to_all x1, starting transfers between devices, step(): lax.all_to_all(second.reshape(4, own, 2 * width), 'frames', 0, 0, tiled=T...  4.57 us
    all_to_all x1, starting transfers between devices, step(): lax.all_to_all(first.reshape(4, half // 4, 2 * width), 'frames', 0, 0, ti...  3.53 us
  transfers between devices with their start and end apart: 11, of which 7 were waited for; matrix products, arithmetic and copies ran while one was open for 0% of the time, Pallas kernels for 6%

profile of v5, /device:TPU:6, one launch (start us, length us, event | category | flops | bytes accessed | tf_op | source)
XLA Modules:
  0.0 132.7 jit_solution(6034272430922771129)
XLA Ops:
  1.3 0.8 multiply_convert_fusion.1
  2.1 42.1 %all-gather.1 = f16[1024,1024]{1,0:T(8,128)(2,1)S(1)} all-gather(f16[32,1024]{1,0:T(8,128)(2,1)S(1)} %multiply_convert_fusion.1), channel_id=1, replica_groups=mesh['frames'=32,'phon'=4,'chap'=4] {'frames'}, dimensions={0}, use_global_device_ids=true | all-gather | bytes 2162688 | tf_op jit(solution)/shard_map/all_gather | solution.py:249
  44.2 0.0 copy-start.3
  44.2 0.6 multiply_convert_fusion.every
  44.8 0.0 copy-done.3
  44.9 4.2 %shard_map.93 = (bf16[1024,512]{1,0:T(8,128)(2,1)S(1)}, bf16[1024,512]{1,0:T(8,128)(2,1)S(1)}, bf16[512,512]{1,0:T(8,128)(2,1)}, f32[3,512]{1,0:T(4,128)S(1)}) custom-call(s32[32]{0:T(128)S(1)} %and_convert_fusion.flags, bf16[1024,1024]{1,0:T(8,128)(2,1)S(1)} %multiply_convert_fusion.every, bf16[512,512]{1,0:T(8,128)(2,1)} %queries_far.5, ...), custom_call_target="tpu_custom_call" | custom-call | flops 1073741824 | bytes 5773440 | tf_op jit(solution)/shard_map/pallas_call | solution.py:41
  49.1 3.5 %collective-permute-start = (f32[3,512]{1,0:T(4,128)S(1)}, f32[3,512]{1,0:T(4,128)S(1)}, u32[]{:S(2)}, u32[]{:S(2)}) collective-permute-start(f32[3,512]{1,0:T(4,128)S(1)} %get-tuple-element.16.stats), channel_id=1, source_target_pairs={{0,4},{4,8},{8,12},{12,0},{1,5},{5,9},{9,13},{13,1},{2,6},{6,10},{... | collective-permute-start | bytes 18440 | tf_op jit(solution)/shard_map/ppermute | solution.py:225
  52.6 3.6 %collective-permute-start.1 = (f32[3,512]{1,0:T(4,128)S(1)}, f32[3,512]{1,0:T(4,128)S(1)}, u32[]{:S(2)}, u32[]{:S(2)}) collective-permute-start(f32[3,512]{1,0:T(4,128)S(1)} %get-tuple-element.16.stats), channel_id=1, source_target_pairs={{0,12},{4,0},{8,4},{12,8},{1,13},{5,1},{9,5},{13,9},{2,14},{6,2},{... | collective-permute-start | bytes 18440 | tf_op jit(solution)/shard_map/ppermute | solution.py:225
  56.2 0.0 collective-permute-done.stats_up
  56.2 2.0 %collective-permute-done.1.stats_down = f32[3,512]{1,0:T(4,128)S(1)} collective-permute-done((f32[3,512]{1,0:T(4,128)S(1)}, f32[3,512]{1,0:T(4,128)S(1)}, u32[]{:S(2)}, u32[]{:S(2)}) %collective-permute-start.1) | collective-permute-done | bytes 6176 | tf_op jit(solution)/shard_map/ppermute | solution.py:225
  58.2 4.2 %shard_map.95 = (bf16[512,1024]{1,0:T(8,128)(2,1)}, bf16[512,512]{1,0:T(8,128)(2,1)}) custom-call(s32[1]{0:T(128)} %bitcast.3.start, s32[32]{0:T(128)S(1)} %and_convert_fusion.flags, f32[3,512]{1,0:T(4,128)S(1)} %get-tuple-element.16.stats, f32[3,512]{1,0:T(4,128)S(1)} %collective-permute-done.stats_up, f32[3,512]{1,0:T(4,128)S(1)} %collective-permute-done.1.stats_down, ...), custom_call_target="tpu_custom_call" | custom-call | flops 1073741824 | bytes 4737156 | tf_op jit(solution)/shard_map/pallas_call | solution.py:41
  62.4 1.9 %collective-permute-start.8 = (bf16[512,1024]{1,0:T(8,128)(2,1)}, bf16[512,1024]{1,0:T(8,128)(2,1)S(1)}, u32[]{:S(2)}, u32[]{:S(2)}) collective-permute-start(bf16[512,1024]{1,0:T(8,128)(2,1)} %get-tuple-element.27), channel_id=1, source_target_pairs={{0,16},{16,0},{32,48},{48,32},{64,80},{80,64},{96,112},{112,96},{1... | collective-permute-start | bytes 3145736 | tf_op jit(solution)/shard_map/ppermute | solution.py:292
  64.3 4.2 %shard_map.94 = (bf16[512,1024]{1,0:T(8,128)(2,1)}, bf16[512,512]{1,0:T(8,128)(2,1)}) custom-call(s32[1]{0:T(128)} %bitcast.1.start, s32[32]{0:T(128)S(1)} %and_convert_fusion.flags, f32[3,512]{1,0:T(4,128)S(1)} %get-tuple-element.16.stats, f32[3,512]{1,0:T(4,128)S(1)} %collective-permute-done.stats_up, f32[3,512]{1,0:T(4,128)S(1)} %collective-permute-done.1.stats_down, ...), custom_call_target="tpu_custom_call" | custom-call | flops 1073741824 | bytes 4737156 | tf_op jit(solution)/shard_map/pallas_call | solution.py:41
  68.5 0.0 collective-permute-done.8.came_far
  68.5 0.0 copy-start
  68.5 1.0 copy-done
  69.5 2.4 %shard_map.97 = bf16[512,1024]{1,0:T(8,128)(2,1)} custom-call(bf16[512,1024]{1,0:T(8,128)(2,1)} %get-tuple-element.26.keep_far, bf16[512,1024]{1,0:T(8,128)(2,1)} %copy-done), custom_call_target="tpu_custom_call" | custom-call | bytes 3145728 | tf_op jit(solution)/shard_map/pallas_call | solution.py:41
  71.9 3.5 %all-to-all-start = ((bf16[4,128,1024]{2,1,0:T(8,128)(2,1)}), bf16[4,128,1024]{2,1,0:T(8,128)(2,1)S(1)}, u32[]{:S(2)}, u32[]{:S(2)}) async-start(bf16[4,128,1024]{2,1,0:T(8,128)(2,1)} %bitcast.44), calls=%async_computation | async-start | bytes 2097152 | tf_op jit(solution)/shard_map/all_to_all | solution.py:300
  75.4 0.1 pad_add_fusion.place
  75.5 2.7 %shard_map.96 = (bf16[128,1024]{1,0:T(8,128)(2,1)S(1)}, bf16[128,1024]{1,0:T(8,128)(2,1)S(1)}, bf16[128,1024]{1,0:T(8,128)(2,1)S(1)}, bf16[128,1024]{1,0:T(8,128)(2,1)S(1)}) custom-call(s32[2]{0:T(128)S(1)} %pad_add_fusion.place, f32[3,512]{1,0:T(4,128)S(1)} %get-tuple-element.16.stats, f32[3,512]{1,0:T(4,128)S(1)} %collective-permute-done.stats_up, ...), custom_call_target="tpu_custom_call" | custom-call | flops 536870912 | bytes 3688456 | tf_op jit(solution)/shard_map/pallas_call | solution.py:41
  78.3 4.8 %collective-permute-start.2 = (bf16[128,1024]{1,0:T(8,128)(2,1)S(1)}, bf16[128,1024]{1,0:T(8,128)(2,1)S(1)}, u32[]{:S(2)}, u32[]{:S(2)}) collective-permute-start(bf16[128,1024]{1,0:T(8,128)(2,1)S(1)} %get-tuple-element.23), channel_id=1, source_target_pairs={{0,8},{4,12},{8,0},{12,4},{1,9},{5,13},{9,1},{13,5},{2,10},{6,14},... | collective-permute-start | bytes 786440 | tf_op jit(solution)/shard_map/ppermute | solution.py:225
  83.1 2.7 %collective-permute-start.3 = (bf16[128,1024]{1,0:T(8,128)(2,1)S(1)}, bf16[128,1024]{1,0:T(8,128)(2,1)S(1)}, u32[]{:S(2)}, u32[]{:S(2)}) collective-permute-start(bf16[128,1024]{1,0:T(8,128)(2,1)S(1)} %get-tuple-element.24), channel_id=1, source_target_pairs={{0,4},{4,8},{8,12},{12,0},{1,5},{5,9},{9,13},{13,1},{2,6},{6,10},{... | collective-permute-start | bytes 786440 | tf_op jit(solution)/shard_map/ppermute | solution.py:225
  85.8 4.3 %collective-permute-start.4 = (bf16[128,1024]{1,0:T(8,128)(2,1)S(1)}, bf16[128,1024]{1,0:T(8,128)(2,1)S(1)}, u32[]{:S(2)}, u32[]{:S(2)}) collective-permute-start(bf16[128,1024]{1,0:T(8,128)(2,1)S(1)} %get-tuple-element.25), channel_id=1, source_target_pairs={{0,12},{4,0},{8,4},{12,8},{1,13},{5,1},{9,5},{13,9},{2,14},{6,2},{... | collective-permute-start | bytes 786440 | tf_op jit(solution)/shard_map/ppermute | solution.py:225
  90.2 0.7 collective-permute-done.2
  90.8 5.3 %collective-permute-done.3 = bf16[128,1024]{1,0:T(8,128)(2,1)S(1)} collective-permute-done((bf16[128,1024]{1,0:T(8,128)(2,1)S(1)}, bf16[128,1024]{1,0:T(8,128)(2,1)S(1)}, u32[]{:S(2)}, u32[]{:S(2)}) %collective-permute-start.3) | collective-permute-done | bytes 262176 | tf_op jit(solution)/shard_map/ppermute | solution.py:225
  96.1 0.2 collective-permute-done.4
  96.3 0.2 add_convert_fusion
  96.5 3.3 %collective-permute-start.5 = (bf16[128,1024]{1,0:T(8,128)(2,1)S(1)}, bf16[128,1024]{1,0:T(8,128)(2,1)S(1)}, u32[]{:S(2)}, u32[]{:S(2)}) collective-permute-start(bf16[128,1024]{1,0:T(8,128)(2,1)S(1)} %add_convert_fusion), channel_id=1, source_target_pairs={{0,4},{4,8},{8,12},{12,0},{1,5},{5,9},{9,13},{13,1},{2,6},{6,10},{... | collective-permute-start | bytes 786440 | tf_op jit(solution)/shard_map/ppermute | solution.py:225
  99.8 5.3 %collective-permute-start.6 = (bf16[128,1024]{1,0:T(8,128)(2,1)S(1)}, bf16[128,1024]{1,0:T(8,128)(2,1)S(1)}, u32[]{:S(2)}, u32[]{:S(2)}) collective-permute-start(bf16[128,1024]{1,0:T(8,128)(2,1)S(1)} %add_convert_fusion), channel_id=1, source_target_pairs={{0,8},{4,12},{8,0},{12,4},{1,9},{5,13},{9,1},{13,5},{2,10},{6,14},... | collective-permute-start | bytes 786440 | tf_op jit(solution)/shard_map/ppermute | solution.py:225
  105.1 2.5 %collective-permute-start.7 = (bf16[128,1024]{1,0:T(8,128)(2,1)S(1)}, bf16[128,1024]{1,0:T(8,128)(2,1)S(1)}, u32[]{:S(2)}, u32[]{:S(2)}) collective-permute-start(bf16[128,1024]{1,0:T(8,128)(2,1)S(1)} %add_convert_fusion), channel_id=1, source_target_pairs={{0,12},{4,0},{8,4},{12,8},{1,13},{5,1},{9,5},{13,9},{2,14},{6,2},{... | collective-permute-start | bytes 786440 | tf_op jit(solution)/shard_map/ppermute | solution.py:225
  107.6 0.0 all-to-all-done.came
  107.7 0.8 shard_map.98
  108.5 4.6 %all-to-all-start.1 = ((bf16[4,32,1024]{2,1,0:T(8,128)(2,1)}), bf16[4,32,1024]{2,1,0:T(8,128)(2,1)S(1)}, u32[]{:S(2)}, u32[]{:S(2)}) async-start(bf16[4,32,1024]{2,1,0:T(8,128)(2,1)} %bitcast.15), calls=%async_computation.1 | async-start | bytes 524288 | tf_op jit(solution)/shard_map/all_to_all | solution.py:328
  113.1 0.0 collective-permute-done.5
  113.2 1.0 collective-permute-done.6
  114.2 1.6 %collective-permute-done.7 = bf16[128,1024]{1,0:T(8,128)(2,1)S(1)} collective-permute-done((bf16[128,1024]{1,0:T(8,128)(2,1)S(1)}, bf16[128,1024]{1,0:T(8,128)(2,1)S(1)}, u32[]{:S(2)}, u32[]{:S(2)}) %collective-permute-start.7) | collective-permute-done | bytes 262176 | tf_op jit(solution)/shard_map/ppermute | solution.py:225
  115.8 0.0 copy-start.1
  115.8 0.0 copy-start.2
  115.8 16.2 %all-to-all-done.1 = bf16[4,32,1024]{2,1,0:T(8,128)(2,1)S(1)} async-done(((bf16[4,32,1024]{2,1,0:T(8,128)(2,1)}), bf16[4,32,1024]{2,1,0:T(8,128)(2,1)S(1)}, u32[]{:S(2)}, u32[]{:S(2)}) %all-to-all-start.1) | async-done | bytes 262176 | tf_op jit(solution)/shard_map/all_to_all | solution.py:328
  132.1 0.7 fusion.8
  132.7 0.0 copy-done.1
  132.7 0.0 copy-done.2
  (9 shorter events, 0.2 us)
Async XLA Ops:
  44.2 0.7 copy-start.3
  49.1 7.1 %collective-permute-start = (f32[3,512]{1,0:T(4,128)S(1)}, f32[3,512]{1,0:T(4,128)S(1)}, u32[]{:S(2)}, u32[]{:S(2)}) collective-permute-start(f32[3,512]{1,0:T(4,128)S(1)} %get-tuple-element.16.stats), channel_id=1, source_target_pairs={{0,4},{4,8},{8,12},{12,0},{1,5},{5,9},{9,13},{13,1},{2,6},{6,10},{... | collective-permute-start | bytes 18440 | tf_op jit(solution)/shard_map/ppermute | solution.py:225
  52.6 5.5 %collective-permute-start.1 = (f32[3,512]{1,0:T(4,128)S(1)}, f32[3,512]{1,0:T(4,128)S(1)}, u32[]{:S(2)}, u32[]{:S(2)}) collective-permute-start(f32[3,512]{1,0:T(4,128)S(1)} %get-tuple-element.16.stats), channel_id=1, source_target_pairs={{0,12},{4,0},{8,4},{12,8},{1,13},{5,1},{9,5},{13,9},{2,14},{6,2},{... | collective-permute-start | bytes 18440 | tf_op jit(solution)/shard_map/ppermute | solution.py:225
  62.4 6.2 %collective-permute-start.8 = (bf16[512,1024]{1,0:T(8,128)(2,1)}, bf16[512,1024]{1,0:T(8,128)(2,1)S(1)}, u32[]{:S(2)}, u32[]{:S(2)}) collective-permute-start(bf16[512,1024]{1,0:T(8,128)(2,1)} %get-tuple-element.27), channel_id=1, source_target_pairs={{0,16},{16,0},{32,48},{48,32},{64,80},{80,64},{96,112},{112,96},{1... | collective-permute-start | bytes 3145736 | tf_op jit(solution)/shard_map/ppermute | solution.py:292
  68.5 1.0 copy-start
  71.9 35.7 %all-to-all-start = ((bf16[4,128,1024]{2,1,0:T(8,128)(2,1)}), bf16[4,128,1024]{2,1,0:T(8,128)(2,1)S(1)}, u32[]{:S(2)}, u32[]{:S(2)}) async-start(bf16[4,128,1024]{2,1,0:T(8,128)(2,1)} %bitcast.44), calls=%async_computation | async-start | bytes 2097152 | tf_op jit(solution)/shard_map/all_to_all | solution.py:300
  78.3 12.6 %collective-permute-start.2 = (bf16[128,1024]{1,0:T(8,128)(2,1)S(1)}, bf16[128,1024]{1,0:T(8,128)(2,1)S(1)}, u32[]{:S(2)}, u32[]{:S(2)}) collective-permute-start(bf16[128,1024]{1,0:T(8,128)(2,1)S(1)} %get-tuple-element.23), channel_id=1, source_target_pairs={{0,8},{4,12},{8,0},{12,4},{1,9},{5,13},{9,1},{13,5},{2,10},{6,14},... | collective-permute-start | bytes 786440 | tf_op jit(solution)/shard_map/ppermute | solution.py:225
  83.1 13.0 %collective-permute-start.3 = (bf16[128,1024]{1,0:T(8,128)(2,1)S(1)}, bf16[128,1024]{1,0:T(8,128)(2,1)S(1)}, u32[]{:S(2)}, u32[]{:S(2)}) collective-permute-start(bf16[128,1024]{1,0:T(8,128)(2,1)S(1)} %get-tuple-element.24), channel_id=1, source_target_pairs={{0,4},{4,8},{8,12},{12,0},{1,5},{5,9},{9,13},{13,1},{2,6},{6,10},{... | collective-permute-start | bytes 786440 | tf_op jit(solution)/shard_map/ppermute | solution.py:225
  85.8 10.5 %collective-permute-start.4 = (bf16[128,1024]{1,0:T(8,128)(2,1)S(1)}, bf16[128,1024]{1,0:T(8,128)(2,1)S(1)}, u32[]{:S(2)}, u32[]{:S(2)}) collective-permute-start(bf16[128,1024]{1,0:T(8,128)(2,1)S(1)} %get-tuple-element.25), channel_id=1, source_target_pairs={{0,12},{4,0},{8,4},{12,8},{1,13},{5,1},{9,5},{13,9},{2,14},{6,2},{... | collective-permute-start | bytes 786440 | tf_op jit(solution)/shard_map/ppermute | solution.py:225
  96.5 16.7 %collective-permute-start.5 = (bf16[128,1024]{1,0:T(8,128)(2,1)S(1)}, bf16[128,1024]{1,0:T(8,128)(2,1)S(1)}, u32[]{:S(2)}, u32[]{:S(2)}) collective-permute-start(bf16[128,1024]{1,0:T(8,128)(2,1)S(1)} %add_convert_fusion), channel_id=1, source_target_pairs={{0,4},{4,8},{8,12},{12,0},{1,5},{5,9},{9,13},{13,1},{2,6},{6,10},{... | collective-permute-start | bytes 786440 | tf_op jit(solution)/shard_map/ppermute | solution.py:225
  99.8 14.4 %collective-permute-start.6 = (bf16[128,1024]{1,0:T(8,128)(2,1)S(1)}, bf16[128,1024]{1,0:T(8,128)(2,1)S(1)}, u32[]{:S(2)}, u32[]{:S(2)}) collective-permute-start(bf16[128,1024]{1,0:T(8,128)(2,1)S(1)} %add_convert_fusion), channel_id=1, source_target_pairs={{0,8},{4,12},{8,0},{12,4},{1,9},{5,13},{9,1},{13,5},{2,10},{6,14},... | collective-permute-start | bytes 786440 | tf_op jit(solution)/shard_map/ppermute | solution.py:225
  105.1 10.7 %collective-permute-start.7 = (bf16[128,1024]{1,0:T(8,128)(2,1)S(1)}, bf16[128,1024]{1,0:T(8,128)(2,1)S(1)}, u32[]{:S(2)}, u32[]{:S(2)}) collective-permute-start(bf16[128,1024]{1,0:T(8,128)(2,1)S(1)} %add_convert_fusion), channel_id=1, source_target_pairs={{0,12},{4,0},{8,4},{12,8},{1,13},{5,1},{9,5},{13,9},{2,14},{6,2},{... | collective-permute-start | bytes 786440 | tf_op jit(solution)/shard_map/ppermute | solution.py:225
  108.5 23.5 %all-to-all-start.1 = ((bf16[4,32,1024]{2,1,0:T(8,128)(2,1)}), bf16[4,32,1024]{2,1,0:T(8,128)(2,1)S(1)}, u32[]{:S(2)}, u32[]{:S(2)}) async-start(bf16[4,32,1024]{2,1,0:T(8,128)(2,1)} %bitcast.15), calls=%async_computation.1 | async-start | bytes 524288 | tf_op jit(solution)/shard_map/all_to_all | solution.py:328
  115.8 16.9 %copy-start.1 = (bf16[4,128,512]{2,1,0:T(8,128)(2,1)}, bf16[4,128,512]{2,1,0:T(8,128)(2,1)S(1)}, u32[]{:S(2)}) copy-start(bf16[4,128,512]{2,1,0:T(8,128)(2,1)S(1)} %get-tuple-element.28) | copy-start | bytes 1572868
  115.8 16.9 %copy-start.2 = (bf16[4,128,512]{2,1,0:T(8,128)(2,1)}, bf16[4,128,512]{2,1,0:T(8,128)(2,1)S(1)}, u32[]{:S(2)}) copy-start(bf16[4,128,512]{2,1,0:T(8,128)(2,1)S(1)} %get-tuple-element.29) | copy-start | bytes 1572868

commit v6 on v5

--- a/solution.py
+++ b/solution.py
@@ -23,9 +23,27 @@
 
 
 ORDERS = [chip_order(0), chip_order(2)]
-QUADS = [[2 * ORDERS[c][k][g] + c for k in range(4)] for c in range(2) for g in range(4)]
-CROSSES = [[2 * ORDERS[c][k][g] + c for g in range(4)] for c in range(2) for k in range(4)]
 BLOCKS = [2 * ORDERS[c][k][g] + c for c in range(2) for k in range(4) for g in range(4)]
+QUAD_STEPS = (2, 3, 1)
+CROSS_STEPS = (2, 1, 3)
+SPOTS = [(c, k, g) for c in range(2) for k in range(4) for g in range(4)]
+MEMBER = {2 * ORDERS[c][k][g] + c: (k, g) for c, k, g in SPOTS}
+
+
+def quad_mate(k, g, d):
+    return (((k + g) % 4) ^ d) - g & 3
+
+
+def quad_pairs(d):
+    return [(2 * ORDERS[c][k][g] + c, 2 * ORDERS[c][quad_mate(k, g, d)][g] + c) for c, k, g in SPOTS]
+
+
+def cross_pairs(d):
+    return [(2 * ORDERS[c][k][g] + c, 2 * ORDERS[c][k][(g + d) % 4] + c) for c, k, g in SPOTS]
+
+
+QUAD_ROWS = [[quad_mate(*MEMBER[f], d) for d in (0,) + QUAD_STEPS] for f in range(32)]
+CROSS_ROWS = [[(MEMBER[f][1] + d) % 4 for d in (0,) + CROSS_STEPS] for f in range(32)]
 
 
 VMEM, HBM, SMEM = pltpu.VMEM, pltpu.HBM, pltpu.SMEM
@@ -118,8 +136,9 @@
 
 def backward_kernel(
     start, flags, stats, stats_up, stats_down, keys, values, queries_far, cotangent_far,
-    grads_out, ds_far, queries, cotangent, grads, ds_low, sems,
+    grads_out, ds_far, queries, cotangent, ds_low, sems, *room,
 ):
+    grads = room[0] if room else grads_out
     half, width = grads.shape[0], keys.shape[1]
     scale = width ** (-0.5)
     own = 2 * half // len(BLOCKS)
@@ -143,29 +162,30 @@
     value = jnp.dot(probs.astype(BF16), cotangent[...], preferred_element_type=F32)
     grads[:, width:] = value.astype(BF16)
     right = pl.ds(width, width)
-    store_value = pltpu.make_async_copy(grads.at[:, right], grads_out.at[:, right], sems.at[4])
-    store_value.start()
+    stores = []
+    if room:
+        stores += [pltpu.make_async_copy(grads.at[:, right], grads_out.at[:, right], sems.at[4])]
+        stores[-1].start()
     ds = probs * (dp - delta)
     low = ds.astype(BF16)
     ds_low[...] = low
-    store_ds = pltpu.make_async_copy(ds_low, ds_far, sems.at[2])
-    store_ds.start()
+    stores += [pltpu.make_async_copy(ds_low, ds_far, sems.at[2])]
+    stores[-1].start()
     column = jnp.sum(ds, axis=1, keepdims=True)
     grad = jnp.dot(low, queries[...], preferred_element_type=F32)
     grads[:, :width] = ((grad - column * keys[mine, :].astype(F32)) * scale).astype(BF16)
     left = pl.ds(0, width)
-    store_key = pltpu.make_async_copy(grads.at[:, left], grads_out.at[:, left], sems.at[3])
-    store_key.start()
-    store_ds.wait()
-    store_value.wait()
-    store_key.wait()
+    if room:
+        stores += [pltpu.make_async_copy(grads.at[:, left], grads_out.at[:, left], sems.at[3])]
+        stores[-1].start()
+    for store in stores:
+        store.wait()
 
 
 def outputs_kernel(
-    place, stats, stats_up, stats_down, keys, features_far, keep_far, send_far, *rest
+    keep_at, stats, stats_up, stats_down, keys, features_far, keep_far, send_far, out,
+    features, low, sems,
 ):
-    parts, (features, low, gathered, sems) = rest[:4], rest[4:]
-    quarter = parts[0].shape[0]
     half, rows = low.shape[1:]
     width = keys.shape[1]
     fetches = [
@@ -181,43 +201,33 @@
     share = jnp.transpose(jnp.broadcast_to(share, (128, rows)))
     share = jnp.concatenate([share] * (width // 128), axis=1)
     fetches[0].wait()
-    gathered[:, width:] = (features[...].astype(F32) * share).astype(BF16)
+    out[:, width:] = (features[...].astype(F32) * share).astype(BF16)
     query = jnp.zeros((rows, width), F32)
-    for i, at in enumerate((place[1], half - place[1])):
+    for i, at in enumerate((keep_at[0], half - keep_at[0])):
         fetches[i + 1].wait()
         right = keys[pl.ds(pl.multiple_of(at, half), half), :]
         query += lax.dot_general(low[i], right, TN, preferred_element_type=F32)
-    gathered[:, :width] = (query * width ** (-0.5)).astype(BF16)
-    for d, part in enumerate(parts):
-        at = ((place[0] + d) & 3) * quarter
-        part[...] = gathered[pl.ds(pl.multiple_of(at, quarter), quarter), :]
-
-
-def add_kernel(keep_far, came_far, out, keep, came, sems):
-    n = sems.shape[1]
-    size = keep.shape[0] // n
-    parts = [pl.ds(size * i, size) for i in range(n)]
-    copy = pltpu.make_async_copy
-    fetches = [
-        (copy(keep_far.at[p], keep.at[p], sems.at[0, i]),
-         copy(came_far.at[p], came.at[p], sems.at[1, i]))
-        for i, p in enumerate(parts)
-    ]
-    stores = [copy(keep.at[p], out.at[p], sems.at[2, i]) for i, p in enumerate(parts)]
-    for a, b in fetches:
-        a.start()
-        b.start()
-    for i, p in enumerate(parts):
-        for f in fetches[i]:
-            f.wait()
-        keep[p, :] = (keep[p, :].astype(F32) + came[p, :].astype(F32)).astype(BF16)
-        stores[i].start()
-    for store in stores:
-        store.wait()
-
-
-def sum_kernel(came, out):
-    out[...] = f32_sum([came[j] for j in range(came.shape[0])]).astype(BF16)
+    out[:, :width] = (query * width ** (-0.5)).astype(BF16)
+
+
+def add_kernel(order, keep, came, *outs):
+    size = outs[0].shape[0]
+    for i, out in enumerate(outs):
+        part = pl.ds(pl.multiple_of(order[i] * size, size), size)
+        out[...] = (keep[part, :].astype(F32) + came[part, :].astype(F32)).astype(BF16)
+
+
+def sum_kernel(order, own, one, two, three, *outs):
+    size = outs[0].shape[0]
+    for i, out in enumerate(outs):
+        part = pl.ds(pl.multiple_of(order[i] * size, size), size)
+        out[...] = f32_sum([own[part, :], one[part, :], two[part, :], three[part, :]]).astype(BF16)
+
+
+def mine_kernel(came, out):
+    total = f32_sum([came[i] for i in range(came.shape[0])]).astype(BF16)
+    for i in range(out.shape[0]):
+        out[i] = total
 
 
 def shifted(value, axis, d):
@@ -266,10 +276,10 @@
     )
     heard = [(stats, VMEM), (shifted(stats, "phon", 1), VMEM), (shifted(stats, "phon", 3), VMEM)]
 
-    def backward(start):
+    def backward(start, space=HBM):
         return call(
             backward_kernel,
-            [((half, 2 * width), BF16, HBM), ((half, rows), BF16, HBM)],
+            [((half, 2 * width), BF16, space), ((half, rows), BF16, HBM)],
             [
                 (jnp.reshape(start, (1,)).astype(jnp.int32), SMEM),
                 (flags, SMEM),
@@ -280,68 +290,52 @@
                 (cotangent, HBM),
             ],
             near
-            + [
-                pltpu.VMEM((half, 2 * width), BF16),
-                pltpu.VMEM((half, rows), BF16),
-                dma((5,)),
-            ],
+            + [pltpu.VMEM((half, rows), BF16), dma((5,))]
+            + [pltpu.VMEM((half, 2 * width), BF16)] * (space == HBM),
             2 * work,
         )
 
     send, send_ds = backward((1 - core) * half)
     came = lax.ppermute(send, "frames", [(i, i ^ 1) for i in range(n)])
-    keep, keep_ds = backward(core * half)
-    (first,) = call(
+    keep, keep_ds = backward(core * half, VMEM)
+    frame = lax.axis_index("frames")
+    pick = lambda table: lax.dynamic_index_in_dim(jnp.asarray(table, jnp.int32), frame, 0, False)
+    part = half // 4
+    own_part, *parts = call(
         add_kernel,
-        [((half, 2 * width), BF16, HBM)],
-        [(keep, HBM), (came, HBM)],
-        [pltpu.VMEM((half, 2 * width), BF16)] * 2 + [dma((3, 4))],
-    )
-    first = lax.all_to_all(
-        first.reshape(4, half // 4, 2 * width), "frames", 0, 0, tiled=True,
-        axis_index_groups=QUADS,
-    )
-
-    place = jnp.stack([phon, core * half]).astype(jnp.int32)
-    parts = call(
+        [((part, 2 * width), BF16, VMEM)] * 4,
+        [(pick(QUAD_ROWS), SMEM), (keep, VMEM), (came, VMEM)],
+    )
+    parts = [lax.ppermute(p, "frames", quad_pairs(d)) for p, d in zip(parts, QUAD_STEPS)]
+
+    (outs,) = call(
         outputs_kernel,
-        [((quarter, 2 * width), BF16, VMEM)] * 4,
+        [((rows, 2 * width), BF16, VMEM)],
         [
-            (place, SMEM),
+            (jnp.reshape(core * half, (1,)).astype(jnp.int32), SMEM),
             *heard,
             (block_keys, VMEM),
             (features, HBM),
             (keep_ds, HBM),
             (send_ds, HBM),
         ],
-        [
-            pltpu.VMEM((rows, width), BF16),
-            pltpu.VMEM((2, half, rows), BF16),
-            pltpu.VMEM((rows, 2 * width), BF16),
-            dma((3,)),
-        ],
+        [pltpu.VMEM((rows, width), BF16), pltpu.VMEM((2, half, rows), BF16), dma((3,))],
         work,
     )
-    moved = [parts[0]] + [shifted(parts[d], "phon", d) for d in (2, 1, 3)]
-
-    (second,) = call(sum_kernel, [((half // 4, 2 * width), BF16, VMEM)], [(first, VMEM)])
-    second = lax.all_to_all(
-        second.reshape(4, own, 2 * width), "frames", 0, 0, tiled=True,
-        axis_index_groups=CROSSES,
-    )
-    mine = f32_sum(moved).astype(BF16)
-    spread = [mine] + [shifted(mine, "phon", d) for d in (1, 2, 3)]
-
-    def placed(parts):
-        whole = jnp.zeros((ranks, quarter, width), BF16)
-        for d, p in enumerate(parts):
-            whole = lax.dynamic_update_index_in_dim(whole, p, (phon - d) & 3, 0)
-        return whole.reshape(rows, width)
-
-    grad_query = placed([m[:, :width] for m in spread])
-    aligned = placed([m[:, width:] for m in spread])
-    grad = f32_sum([second[i] for i in range(4)])
-    return (aligned, grad_query, grad[:, :width], grad[:, width:])
+    outs = lax.all_to_all(
+        outs.reshape(ranks, quarter, 2 * width), "phon", 0, 0, tiled=True
+    )
+
+    own_grad, *grads = call(
+        sum_kernel,
+        [((own, 2 * width), BF16, VMEM)] * 4,
+        [(pick(CROSS_ROWS), SMEM), (own_part, VMEM)] + [(p, VMEM) for p in parts],
+    )
+    grads = [lax.ppermute(g, "frames", cross_pairs(d)) for g, d in zip(grads, CROSS_STEPS)]
+    (mine,) = call(mine_kernel, [((ranks, quarter, 2 * width), BF16, VMEM)], [(outs, VMEM)])
+    outs = lax.all_to_all(mine, "phon", 0, 0, tiled=True).reshape(rows, 2 * width)
+    grad = f32_sum([own_grad] + grads)
+    return (outs[:, width:], outs[:, :width], grad[:, :width], grad[:, width:])
 
 
 def solution(mesh):

time: 133 us -> 133 us (level); the launches traced: 133 us -> 131 us
  waiting for transfers between devices: 26.9 us -> 22.4 us
  local copies, waits for them, and re-layouts: 1.87 us -> 4.37 us
    ppermute x0 -> x6, starting transfers between devices: none -> 25.1 us  [the longest x3 15.9 us: step(): lax.ppermute(g, 'frames', cross_pairs(d))]
    ppermute x8 -> x2, starting transfers between devices: 30 us -> 6.84 us  [shifted(): return lax.ppermute(value, axis, [(i, (i + d) % n) for i in range(n)])]
    ppermute x0 -> x6, waiting for transfers between devices: none -> 13 us  [the longest x3 11.6 us: step(): lax.ppermute(g, 'frames', cross_pairs(d))]
    all_to_all x2, waiting for transfers between devices: 16.2 us -> 4.54 us  [the longest x1 4.53 us: step(): lax.all_to_all(outs.reshape(ranks, quarter, 2 * width), 'phon', 0, 0, til...]
    ppermute x8 -> x2, waiting for transfers between devices: 10.7 us -> 4.81 us  [shifted(): return lax.ppermute(value, axis, [(i, (i + d) % n) for i in range(n)])]
    squeeze x0 -> x2, local copies, waits for them, and re-layouts: none -> 1.4 us  [step(): lax.dynamic_index_in_dim(jnp.asarray(table, jnp.int32), frame, 0, False)]
    pallas_call x6 -> x7, Pallas kernels: 18.6 us -> 18.4 us  [call(): pl.pallas_call(kernel, out_shape=shapes, in_specs=[pl.BlockSpec(memory_sp...]
  transfers between devices with their start and end apart: 11 -> 11, of which waited for: 7 -> 6; matrix products, arithmetic and copies ran while one was open for 0% -> 2% of each run, Pallas kernels for 6% -> 8%
where the time goes in v6:
time: 133 us; the launch traced here: 131 us
  blocking collectives  42.1 us (32%)
  starting transfers between devices  40.9 us (31%)
  waiting for transfers between devices  22.4 us (17%)
  Pallas kernels  18.4 us (14%)
  local copies, waits for them, and re-layouts  4.37 us (3%)
  between operations  1.48 us (1%)
  other arithmetic  1.44 us (1%)
    all_gather x1, blocking collectives, step(): lax.all_gather(both.astype(jnp.float16), 'frames', axis=0, tiled=True)  42.1 us
    pallas_call x7, Pallas kernels, call(): pl.pallas_call(kernel, out_shape=shapes, in_specs=[pl.BlockSpec(memory_sp...  18.4 us
    ppermute x3, starting transfers between devices, step(): lax.ppermute(g, 'frames', cross_pairs(d))  15.9 us
    ppermute x3, waiting for transfers between devices, step(): lax.ppermute(g, 'frames', cross_pairs(d))  11.6 us
    ppermute x3, starting transfers between devices, step(): lax.ppermute(p, 'frames', quad_pairs(d))  9.2 us
    ppermute x2, starting transfers between devices, shifted(): return lax.ppermute(value, axis, [(i, (i + d) % n) for i in range(n)])  6.84 us
    ppermute x2, waiting for transfers between devices, shifted(): return lax.ppermute(value, axis, [(i, (i + d) % n) for i in range(n)])  4.81 us
    all_to_all x1, waiting for transfers between devices, step(): lax.all_to_all(outs.reshape(ranks, quarter, 2 * width), 'phon', 0, 0, til...  4.53 us
  transfers between devices with their start and end apart: 11, of which 6 were waited for; matrix products, arithmetic and copies ran while one was open for 2% of the time, Pallas kernels for 8%

profile of v6, /device:TPU:6, one launch (start us, length us, event | category | flops | bytes accessed | tf_op | source)
XLA Modules:
  0.0 131.1 jit_solution(7163082042432854424)
XLA Ops:
  1.3 0.8 multiply_convert_fusion.1
  2.1 42.1 %all-gather.1 = f16[1024,1024]{1,0:T(8,128)(2,1)S(1)} all-gather(f16[32,1024]{1,0:T(8,128)(2,1)S(1)} %multiply_convert_fusion.1), channel_id=1, replica_groups=mesh['frames'=32,'phon'=4,'chap'=4] {'frames'}, dimensions={0}, use_global_device_ids=true | all-gather | bytes 2162688 | tf_op jit(solution)/shard_map/all_gather | solution.py:259
  44.2 0.0 copy-start.2
  44.2 0.6 multiply_convert_fusion.every
  44.8 0.0 copy-done.2
  44.9 4.2 %shard_map.111 = (bf16[1024,512]{1,0:T(8,128)(2,1)S(1)}, bf16[1024,512]{1,0:T(8,128)(2,1)S(1)}, bf16[512,512]{1,0:T(8,128)(2,1)}, f32[3,512]{1,0:T(4,128)S(1)}) custom-call(s32[32]{0:T(128)S(1)} %and_convert_fusion.flags, bf16[1024,1024]{1,0:T(8,128)(2,1)S(1)} %multiply_convert_fusion.every, bf16[512,512]{1,0:T(8,128)(2,1)} %queries_far.5, ...), custom_call_target="tpu_custom_call" | custom-call | flops 1073741824 | bytes 5773440 | tf_op jit(solution)/shard_map/pallas_call | solution.py:59
  49.1 0.0 copy-start
  49.1 4.9 %collective-permute-start.1 = (f32[3,512]{1,0:T(4,128)S(1)}, f32[3,512]{1,0:T(4,128)S(1)}, u32[]{:S(2)}, u32[]{:S(2)}) collective-permute-start(f32[3,512]{1,0:T(4,128)S(1)} %get-tuple-element.20.stats), channel_id=1, source_target_pairs={{0,12},{4,0},{8,4},{12,8},{1,13},{5,1},{9,5},{13,9},{2,14},{6,2},{... | collective-permute-start | bytes 18440 | tf_op jit(solution)/shard_map/ppermute | solution.py:235
  54.1 1.9 %collective-permute-start = (f32[3,512]{1,0:T(4,128)S(1)}, f32[3,512]{1,0:T(4,128)S(1)}, u32[]{:S(2)}, u32[]{:S(2)}) collective-permute-start(f32[3,512]{1,0:T(4,128)S(1)} %get-tuple-element.20.stats), channel_id=1, source_target_pairs={{0,4},{4,8},{8,12},{12,0},{1,5},{5,9},{9,13},{13,1},{2,6},{6,10},{... | collective-permute-start | bytes 18440 | tf_op jit(solution)/shard_map/ppermute | solution.py:235
  56.0 0.0 collective-permute-done.1.stats_down
  56.0 4.8 %collective-permute-done.stats_up = f32[3,512]{1,0:T(4,128)S(1)} collective-permute-done((f32[3,512]{1,0:T(4,128)S(1)}, f32[3,512]{1,0:T(4,128)S(1)}, u32[]{:S(2)}, u32[]{:S(2)}) %collective-permute-start) | collective-permute-done | bytes 6176 | tf_op jit(solution)/shard_map/ppermute | solution.py:235
  60.8 4.2 %shard_map.113 = (bf16[512,1024]{1,0:T(8,128)(2,1)}, bf16[512,512]{1,0:T(8,128)(2,1)}) custom-call(s32[1]{0:T(128)} %bitcast.2.start, s32[32]{0:T(128)S(1)} %and_convert_fusion.flags, f32[3,512]{1,0:T(4,128)S(1)} %get-tuple-element.20.stats, f32[3,512]{1,0:T(4,128)S(1)} %collective-permute-done.stats_up, f32[3,512]{1,0:T(4,128)S(1)} %collective-permute-done.1.stats_down, ...), custom_call_target="tpu_custom_call" | custom-call | flops 1073741824 | bytes 4737156 | tf_op jit(solution)/shard_map/pallas_call | solution.py:59
  65.1 0.0 copy-done
  65.1 1.9 %collective-permute-start.2 = (bf16[512,1024]{1,0:T(8,128)(2,1)}, bf16[512,1024]{1,0:T(8,128)(2,1)S(1)}, u32[]{:S(2)}, u32[]{:S(2)}) collective-permute-start(bf16[512,1024]{1,0:T(8,128)(2,1)} %get-tuple-element.27), channel_id=1, source_target_pairs={{0,16},{16,0},{32,48},{48,32},{64,80},{80,64},{96,112},{112,96},{1... | collective-permute-start | bytes 3145736 | tf_op jit(solution)/shard_map/ppermute | solution.py:299
  67.0 0.0 copy-start.1
  67.0 1.2 copy-done.1
  68.2 3.5 %shard_map.112 = (bf16[512,1024]{1,0:T(8,128)(2,1)S(1)}, bf16[512,512]{1,0:T(8,128)(2,1)}) custom-call(s32[1]{0:T(128)} %bitcast.start.keep_at, s32[32]{0:T(128)S(1)} %and_convert_fusion.flags, f32[3,512]{1,0:T(4,128)S(1)} %get-tuple-element.20.stats, f32[3,512]{1,0:T(4,128)S(1)} %collective-permute-done.stats_up, ...), custom_call_target="tpu_custom_call" | custom-call | flops 1073741824 | bytes 4737156 | tf_op jit(solution)/shard_map/pallas_call | solution.py:59
  71.8 3.1 %shard_map.114 = bf16[512,1024]{1,0:T(8,128)(2,1)} custom-call(s32[1]{0:T(128)} %bitcast.start.keep_at, f32[3,512]{1,0:T(4,128)S(1)} %get-tuple-element.20.stats, f32[3,512]{1,0:T(4,128)S(1)} %collective-permute-done.stats_up, f32[3,512]{1,0:T(4,128)S(1)} %collective-permute-done.1.stats_down, bf16[1024,512]{1,0:T(8,128)(2,1)S(1)} %get-tuple-element.21.keys, ...), custom_call_target="tpu_custom_call" | custom-call | flops 536870912 | bytes 3688452 | tf_op jit(solution)/shard_map/pallas_call | solution.py:59
  74.9 3.5 %all-to-all-start = ((bf16[4,128,1024]{2,1,0:T(8,128)(2,1)}), bf16[4,128,1024]{2,1,0:T(8,128)(2,1)S(1)}, u32[]{:S(2)}, u32[]{:S(2)}) async-start(bf16[4,128,1024]{2,1,0:T(8,128)(2,1)} %bitcast.3), calls=%async_computation | async-start | bytes 2097152 | tf_op jit(solution)/shard_map/all_to_all | solution.py:325
  78.4 0.7 dynamic-slice_bitcast_fusion.order
  79.1 0.0 collective-permute-done.2.came
  79.1 1.5 %shard_map.116 = (bf16[128,1024]{1,0:T(8,128)(2,1)S(1)}, bf16[128,1024]{1,0:T(8,128)(2,1)}, bf16[128,1024]{1,0:T(8,128)(2,1)}, bf16[128,1024]{1,0:T(8,128)(2,1)}) custom-call(s32[4]{0:T(128)S(1)} %dynamic-slice_bitcast_fusion.order, bf16[512,1024]{1,0:T(8,128)(2,1)S(1)} %get-tuple-element.26.keep, bf16[512,1024]{1,0:T(8,128)(2,1)S(1)} %collective-permute-done.2.came), custom_call_target="tpu_custom_call" | custom-call | bytes 3145744 | tf_op jit(solution)/shard_map/pallas_call | solution.py:59
  80.6 2.2 %collective-permute-start.3 = (bf16[128,1024]{1,0:T(8,128)(2,1)}, bf16[128,1024]{1,0:T(8,128)(2,1)S(1)}, u32[]{:S(2)}, u32[]{:S(2)}) collective-permute-start(bf16[128,1024]{1,0:T(8,128)(2,1)} %get-tuple-element.29), channel_id=1, source_target_pairs={{0,64},{160,224},{320,256},{480,416},{32,96},{192,128},{352,288},{... | collective-permute-start | bytes 786440 | tf_op jit(solution)/shard_map/ppermute | solution.py:309
  82.8 3.8 %collective-permute-start.4 = (bf16[128,1024]{1,0:T(8,128)(2,1)}, bf16[128,1024]{1,0:T(8,128)(2,1)S(1)}, u32[]{:S(2)}, u32[]{:S(2)}) collective-permute-start(bf16[128,1024]{1,0:T(8,128)(2,1)} %get-tuple-element.30), channel_id=1, source_target_pairs={{0,96},{160,192},{320,288},{480,384},{32,64},{192,160},{352,256},{... | collective-permute-start | bytes 786440 | tf_op jit(solution)/shard_map/ppermute | solution.py:309
  86.6 3.3 %collective-permute-start.5 = (bf16[128,1024]{1,0:T(8,128)(2,1)}, bf16[128,1024]{1,0:T(8,128)(2,1)S(1)}, u32[]{:S(2)}, u32[]{:S(2)}) collective-permute-start(bf16[128,1024]{1,0:T(8,128)(2,1)} %get-tuple-element.31), channel_id=1, source_target_pairs={{0,32},{160,128},{320,352},{480,448},{32,0},{192,224},{352,320},{3... | collective-permute-start | bytes 786440 | tf_op jit(solution)/shard_map/ppermute | solution.py:309
  89.9 4.5 %all-to-all-done.came = bf16[4,128,1024]{2,1,0:T(8,128)(2,1)S(1)} async-done(((bf16[4,128,1024]{2,1,0:T(8,128)(2,1)}), bf16[4,128,1024]{2,1,0:T(8,128)(2,1)S(1)}, u32[]{:S(2)}, u32[]{:S(2)}) %all-to-all-start) | async-done | bytes 1048608 | tf_op jit(solution)/shard_map/all_to_all | solution.py:325
  94.4 1.1 shard_map.115
  95.5 3.5 %all-to-all-start.1 = ((bf16[4,128,1024]{2,1,0:T(8,128)(2,1)}), bf16[4,128,1024]{2,1,0:T(8,128)(2,1)S(1)}, u32[]{:S(2)}, u32[]{:S(2)}) async-start(bf16[4,128,1024]{2,1,0:T(8,128)(2,1)} %shard_map.115), calls=%async_computation.1 | async-start | bytes 2097152 | tf_op jit(solution)/shard_map/all_to_all | solution.py:336
  99.1 0.7 dynamic-slice_bitcast_fusion.1.order
  99.8 0.0 collective-permute-done.3.one
  99.8 0.2 collective-permute-done.4.two
  99.9 1.2 collective-permute-done.5.three
  101.2 0.7 shard_map.117
  101.8 8.9 %collective-permute-start.6 = (bf16[32,1024]{1,0:T(8,128)(2,1)S(1)}, bf16[32,1024]{1,0:T(8,128)(2,1)S(1)}, u32[]{:S(2)}, u32[]{:S(2)}) collective-permute-start(bf16[32,1024]{1,0:T(8,128)(2,1)S(1)} %get-tuple-element.33), channel_id=1, source_target_pairs={{0,320},{160,480},{320,0},{480,160},{32,352},{192,384},{352,32},{3... | collective-permute-start | bytes 196616 | tf_op jit(solution)/shard_map/ppermute | solution.py:334
  110.7 3.7 %collective-permute-start.7 = (bf16[32,1024]{1,0:T(8,128)(2,1)S(1)}, bf16[32,1024]{1,0:T(8,128)(2,1)S(1)}, u32[]{:S(2)}, u32[]{:S(2)}) collective-permute-start(bf16[32,1024]{1,0:T(8,128)(2,1)S(1)} %get-tuple-element.34), channel_id=1, source_target_pairs={{0,160},{160,320},{320,480},{480,0},{32,192},{192,352},{352,384},{... | collective-permute-start | bytes 196616 | tf_op jit(solution)/shard_map/ppermute | solution.py:334
  114.4 3.4 %collective-permute-start.8 = (bf16[32,1024]{1,0:T(8,128)(2,1)S(1)}, bf16[32,1024]{1,0:T(8,128)(2,1)S(1)}, u32[]{:S(2)}, u32[]{:S(2)}) collective-permute-start(bf16[32,1024]{1,0:T(8,128)(2,1)S(1)} %get-tuple-element.35), channel_id=1, source_target_pairs={{0,480},{160,0},{320,160},{480,320},{32,384},{192,32},{352,192},{3... | collective-permute-start | bytes 196616 | tf_op jit(solution)/shard_map/ppermute | solution.py:334
  117.8 0.0 collective-permute-done.6
  117.8 3.3 %collective-permute-done.7 = bf16[32,1024]{1,0:T(8,128)(2,1)S(1)} collective-permute-done((bf16[32,1024]{1,0:T(8,128)(2,1)S(1)}, bf16[32,1024]{1,0:T(8,128)(2,1)S(1)}, u32[]{:S(2)}, u32[]{:S(2)}) %collective-permute-start.7) | collective-permute-done | bytes 65568 | tf_op jit(solution)/shard_map/ppermute | solution.py:334
  121.1 8.3 %collective-permute-done.8 = bf16[32,1024]{1,0:T(8,128)(2,1)S(1)} collective-permute-done((bf16[32,1024]{1,0:T(8,128)(2,1)S(1)}, bf16[32,1024]{1,0:T(8,128)(2,1)S(1)}, u32[]{:S(2)}, u32[]{:S(2)}) %collective-permute-start.8) | collective-permute-done | bytes 65568 | tf_op jit(solution)/shard_map/ppermute | solution.py:334
  129.4 0.7 fusion.1
  130.1 0.0 all-to-all-done.1
  130.1 1.0 fusion
  (2 shorter events, 0.0 us)
Async XLA Ops:
  44.2 0.7 copy-start.2
  49.1 15.9 %copy-start = (bf16[1024,512]{1,0:T(8,128)(2,1)}, bf16[1024,512]{1,0:T(8,128)(2,1)S(1)}, u32[]{:S(2)}) copy-start(bf16[1024,512]{1,0:T(8,128)(2,1)S(1)} %get-tuple-element.23.values) | copy-start | bytes 3145732
  49.1 6.9 %collective-permute-start.1 = (f32[3,512]{1,0:T(4,128)S(1)}, f32[3,512]{1,0:T(4,128)S(1)}, u32[]{:S(2)}, u32[]{:S(2)}) collective-permute-start(f32[3,512]{1,0:T(4,128)S(1)} %get-tuple-element.20.stats), channel_id=1, source_target_pairs={{0,12},{4,0},{8,4},{12,8},{1,13},{5,1},{9,5},{13,9},{2,14},{6,2},{... | collective-permute-start | bytes 18440 | tf_op jit(solution)/shard_map/ppermute | solution.py:235
  54.1 6.8 %collective-permute-start = (f32[3,512]{1,0:T(4,128)S(1)}, f32[3,512]{1,0:T(4,128)S(1)}, u32[]{:S(2)}, u32[]{:S(2)}) collective-permute-start(f32[3,512]{1,0:T(4,128)S(1)} %get-tuple-element.20.stats), channel_id=1, source_target_pairs={{0,4},{4,8},{8,12},{12,0},{1,5},{5,9},{9,13},{13,1},{2,6},{6,10},{... | collective-permute-start | bytes 18440 | tf_op jit(solution)/shard_map/ppermute | solution.py:235
  65.1 14.0 %collective-permute-start.2 = (bf16[512,1024]{1,0:T(8,128)(2,1)}, bf16[512,1024]{1,0:T(8,128)(2,1)S(1)}, u32[]{:S(2)}, u32[]{:S(2)}) collective-permute-start(bf16[512,1024]{1,0:T(8,128)(2,1)} %get-tuple-element.27), channel_id=1, source_target_pairs={{0,16},{16,0},{32,48},{48,32},{64,80},{80,64},{96,112},{112,96},{1... | collective-permute-start | bytes 3145736 | tf_op jit(solution)/shard_map/ppermute | solution.py:299
  67.0 1.2 copy-start.1
  74.9 19.5 %all-to-all-start = ((bf16[4,128,1024]{2,1,0:T(8,128)(2,1)}), bf16[4,128,1024]{2,1,0:T(8,128)(2,1)S(1)}, u32[]{:S(2)}, u32[]{:S(2)}) async-start(bf16[4,128,1024]{2,1,0:T(8,128)(2,1)} %bitcast.3), calls=%async_computation | async-start | bytes 2097152 | tf_op jit(solution)/shard_map/all_to_all | solution.py:325
  80.6 19.1 %collective-permute-start.3 = (bf16[128,1024]{1,0:T(8,128)(2,1)}, bf16[128,1024]{1,0:T(8,128)(2,1)S(1)}, u32[]{:S(2)}, u32[]{:S(2)}) collective-permute-start(bf16[128,1024]{1,0:T(8,128)(2,1)} %get-tuple-element.29), channel_id=1, source_target_pairs={{0,64},{160,224},{320,256},{480,416},{32,96},{192,128},{352,288},{... | collective-permute-start | bytes 786440 | tf_op jit(solution)/shard_map/ppermute | solution.py:309
  82.8 17.1 %collective-permute-start.4 = (bf16[128,1024]{1,0:T(8,128)(2,1)}, bf16[128,1024]{1,0:T(8,128)(2,1)S(1)}, u32[]{:S(2)}, u32[]{:S(2)}) collective-permute-start(bf16[128,1024]{1,0:T(8,128)(2,1)} %get-tuple-element.30), channel_id=1, source_target_pairs={{0,96},{160,192},{320,288},{480,384},{32,64},{192,160},{352,256},{... | collective-permute-start | bytes 786440 | tf_op jit(solution)/shard_map/ppermute | solution.py:309
  86.6 14.6 %collective-permute-start.5 = (bf16[128,1024]{1,0:T(8,128)(2,1)}, bf16[128,1024]{1,0:T(8,128)(2,1)S(1)}, u32[]{:S(2)}, u32[]{:S(2)}) collective-permute-start(bf16[128,1024]{1,0:T(8,128)(2,1)} %get-tuple-element.31), channel_id=1, source_target_pairs={{0,32},{160,128},{320,352},{480,448},{32,0},{192,224},{352,320},{3... | collective-permute-start | bytes 786440 | tf_op jit(solution)/shard_map/ppermute | solution.py:309
  95.5 34.6 %all-to-all-start.1 = ((bf16[4,128,1024]{2,1,0:T(8,128)(2,1)}), bf16[4,128,1024]{2,1,0:T(8,128)(2,1)S(1)}, u32[]{:S(2)}, u32[]{:S(2)}) async-start(bf16[4,128,1024]{2,1,0:T(8,128)(2,1)} %shard_map.115), calls=%async_computation.1 | async-start | bytes 2097152 | tf_op jit(solution)/shard_map/all_to_all | solution.py:336
  101.8 16.0 %collective-permute-start.6 = (bf16[32,1024]{1,0:T(8,128)(2,1)S(1)}, bf16[32,1024]{1,0:T(8,128)(2,1)S(1)}, u32[]{:S(2)}, u32[]{:S(2)}) collective-permute-start(bf16[32,1024]{1,0:T(8,128)(2,1)S(1)} %get-tuple-element.33), channel_id=1, source_target_pairs={{0,320},{160,480},{320,0},{480,160},{32,352},{192,384},{352,32},{3... | collective-permute-start | bytes 196616 | tf_op jit(solution)/shard_map/ppermute | solution.py:334
  110.7 10.4 %collective-permute-start.7 = (bf16[32,1024]{1,0:T(8,128)(2,1)S(1)}, bf16[32,1024]{1,0:T(8,128)(2,1)S(1)}, u32[]{:S(2)}, u32[]{:S(2)}) collective-permute-start(bf16[32,1024]{1,0:T(8,128)(2,1)S(1)} %get-tuple-element.34), channel_id=1, source_target_pairs={{0,160},{160,320},{320,480},{480,0},{32,192},{192,352},{352,384},{... | collective-permute-start | bytes 196616 | tf_op jit(solution)/shard_map/ppermute | solution.py:334
  114.4 15.0 %collective-permute-start.8 = (bf16[32,1024]{1,0:T(8,128)(2,1)S(1)}, bf16[32,1024]{1,0:T(8,128)(2,1)S(1)}, u32[]{:S(2)}, u32[]{:S(2)}) collective-permute-start(bf16[32,1024]{1,0:T(8,128)(2,1)S(1)} %get-tuple-element.35), channel_id=1, source_target_pairs={{0,480},{160,0},{320,160},{480,320},{32,384},{192,32},{352,192},{3... | collective-permute-start | bytes 196616 | tf_op jit(solution)/shard_map/ppermute | solution.py:334

commit v7 on v5

--- a/solution.py
+++ b/solution.py
@@ -117,16 +117,15 @@
 
 
 def backward_kernel(
-    start, flags, stats, stats_up, stats_down, keys, values, queries_far, cotangent_far,
-    grads_out, ds_far, queries, cotangent, grads, ds_low, sems,
+    start, flags, stats, stats_up, stats_down, keys, values, queries, cotangent_far,
+    grads_out, ds_far, cotangent, ds_low, sems, *room,
 ):
+    grads = room[0] if room else grads_out
     half, width = grads.shape[0], keys.shape[1]
     scale = width ** (-0.5)
     own = 2 * half // len(BLOCKS)
     mine = pl.ds(pl.multiple_of(start[0], half), half)
-    fetch_q = pltpu.make_async_copy(queries_far, queries, sems.at[0])
     fetch_g = pltpu.make_async_copy(cotangent_far, cotangent, sems.at[1])
-    fetch_q.start()
     fetch_g.start()
     peak, total, delta = merged((stats, stats_up, stats_down))
     delta = delta / total
@@ -134,7 +133,6 @@
     low_key = keys[mine, :]
     key = low_key.astype(F32)
     offset = jnp.sum(key * key, axis=1, keepdims=True) * (-0.5 * scale)
-    fetch_q.wait()
     raw = lax.dot_general(low_key, queries[...], NT, preferred_element_type=F32)
     fetch_g.wait()
     dp = lax.dot_general(values[mine, :], cotangent[...], NT, preferred_element_type=F32)
@@ -143,22 +141,24 @@
     value = jnp.dot(probs.astype(BF16), cotangent[...], preferred_element_type=F32)
     grads[:, width:] = value.astype(BF16)
     right = pl.ds(width, width)
-    store_value = pltpu.make_async_copy(grads.at[:, right], grads_out.at[:, right], sems.at[4])
-    store_value.start()
+    stores = []
+    if room:
+        stores += [pltpu.make_async_copy(grads.at[:, right], grads_out.at[:, right], sems.at[4])]
+        stores[-1].start()
     ds = probs * (dp - delta)
     low = ds.astype(BF16)
     ds_low[...] = low
-    store_ds = pltpu.make_async_copy(ds_low, ds_far, sems.at[2])
-    store_ds.start()
+    stores += [pltpu.make_async_copy(ds_low, ds_far, sems.at[2])]
+    stores[-1].start()
     column = jnp.sum(ds, axis=1, keepdims=True)
     grad = jnp.dot(low, queries[...], preferred_element_type=F32)
     grads[:, :width] = ((grad - column * keys[mine, :].astype(F32)) * scale).astype(BF16)
     left = pl.ds(0, width)
-    store_key = pltpu.make_async_copy(grads.at[:, left], grads_out.at[:, left], sems.at[3])
-    store_key.start()
-    store_ds.wait()
-    store_value.wait()
-    store_key.wait()
+    if room:
+        stores += [pltpu.make_async_copy(grads.at[:, left], grads_out.at[:, left], sems.at[3])]
+        stores[-1].start()
+    for store in stores:
+        store.wait()
 
 
 def outputs_kernel(
@@ -193,24 +193,18 @@
         part[...] = gathered[pl.ds(pl.multiple_of(at, quarter), quarter), :]
 
 
-def add_kernel(keep_far, came_far, out, keep, came, sems):
+def add_kernel(keep, came_far, out, came, sems):
     n = sems.shape[1]
     size = keep.shape[0] // n
     parts = [pl.ds(size * i, size) for i in range(n)]
     copy = pltpu.make_async_copy
-    fetches = [
-        (copy(keep_far.at[p], keep.at[p], sems.at[0, i]),
-         copy(came_far.at[p], came.at[p], sems.at[1, i]))
-        for i, p in enumerate(parts)
-    ]
-    stores = [copy(keep.at[p], out.at[p], sems.at[2, i]) for i, p in enumerate(parts)]
-    for a, b in fetches:
-        a.start()
-        b.start()
+    fetches = [copy(came_far.at[p], came.at[p], sems.at[0, i]) for i, p in enumerate(parts)]
+    stores = [copy(came.at[p], out.at[p], sems.at[1, i]) for i, p in enumerate(parts)]
+    for fetch in fetches:
+        fetch.start()
     for i, p in enumerate(parts):
-        for f in fetches[i]:
-            f.wait()
-        keep[p, :] = (keep[p, :].astype(F32) + came[p, :].astype(F32)).astype(BF16)
+        fetches[i].wait()
+        came[p, :] = (keep[p, :].astype(F32) + came[p, :].astype(F32)).astype(BF16)
         stores[i].start()
     for store in stores:
         store.wait()
@@ -266,36 +260,33 @@
     )
     heard = [(stats, VMEM), (shifted(stats, "phon", 1), VMEM), (shifted(stats, "phon", 3), VMEM)]
 
-    def backward(start):
+    def backward(start, space=HBM):
         return call(
             backward_kernel,
-            [((half, 2 * width), BF16, HBM), ((half, rows), BF16, HBM)],
+            [((half, 2 * width), BF16, space), ((half, rows), BF16, HBM)],
             [
                 (jnp.reshape(start, (1,)).astype(jnp.int32), SMEM),
                 (flags, SMEM),
                 *heard,
                 (block_keys, VMEM),
                 (block_values, VMEM),
-                (queries, HBM),
+                (queries, VMEM),
                 (cotangent, HBM),
             ],
-            near
-            + [
-                pltpu.VMEM((half, 2 * width), BF16),
-                pltpu.VMEM((half, rows), BF16),
-                dma((5,)),
-            ],
+            near[1:]
+            + [pltpu.VMEM((half, rows), BF16), dma((5,))]
+            + [pltpu.VMEM((half, 2 * width), BF16)] * (space == HBM),
             2 * work,
         )
 
     send, send_ds = backward((1 - core) * half)
     came = lax.ppermute(send, "frames", [(i, i ^ 1) for i in range(n)])
-    keep, keep_ds = backward(core * half)
+    keep, keep_ds = backward(core * half, VMEM)
     (first,) = call(
         add_kernel,
         [((half, 2 * width), BF16, HBM)],
-        [(keep, HBM), (came, HBM)],
-        [pltpu.VMEM((half, 2 * width), BF16)] * 2 + [dma((3, 4))],
+        [(keep, VMEM), (came, HBM)],
+        [pltpu.VMEM((half, 2 * width), BF16), dma((2, 4))],
     )
     first = lax.all_to_all(
         first.reshape(4, half // 4, 2 * width), "frames", 0, 0, tiled=True,
@@ -330,11 +321,11 @@
         axis_index_groups=CROSSES,
     )
     mine = f32_sum(moved).astype(BF16)
-    spread = [mine] + [shifted(mine, "phon", d) for d in (1, 2, 3)]
+    spread = [mine] + [shifted(mine, "phon", d) for d in (2, 3, 1)]
 
     def placed(parts):
         whole = jnp.zeros((ranks, quarter, width), BF16)
-        for d, p in enumerate(parts):
+        for d, p in zip((0, 2, 3, 1), parts):
             whole = lax.dynamic_update_index_in_dim(whole, p, (phon - d) & 3, 0)
         return whole.reshape(rows, width)
 

time: 133 us -> 130 us (0.977)
  Pallas kernels: 18.6 us -> 16.9 us
    pallas_call x6, Pallas kernels: 18.6 us -> 16.9 us  [call(): pl.pallas_call(kernel, out_shape=shapes, in_specs=[pl.BlockSpec(memory_sp...]
  transfers between devices with their start and end apart: 11 -> 11, of which waited for: 7 -> 7; matrix products, arithmetic and copies ran while one was open for 0% -> 0% of each run, Pallas kernels for 6% -> 5%
where the time goes in v7:
time: 130 us; the launch traced here: 129 us
  blocking collectives  42.1 us (32%)
  starting transfers between devices  39.4 us (30%)
  waiting for transfers between devices  26.9 us (21%)
  Pallas kernels  16.9 us (13%)
  other arithmetic  1.69 us (1%)
  between operations  1.55 us (1%)
    all_gather x1, blocking collectives, step(): lax.all_gather(both.astype(jnp.float16), 'frames', axis=0, tiled=True)  42.1 us
    ppermute x8, starting transfers between devices, shifted(): return lax.ppermute(value, axis, [(i, (i + d) % n) for i in range(n)])  29.4 us
    pallas_call x6, Pallas kernels, call(): pl.pallas_call(kernel, out_shape=shapes, in_specs=[pl.BlockSpec(memory_sp...  16.9 us
    all_to_all x1, waiting for transfers between devices, step(): lax.all_to_all(second.reshape(4, own, 2 * width), 'frames', 0, 0, tiled=T...  16.2 us
    ppermute x8, waiting for transfers between devices, shifted(): return lax.ppermute(value, axis, [(i, (i + d) % n) for i in range(n)])  10.7 us
    all_to_all x1, starting transfers between devices, step(): lax.all_to_all(second.reshape(4, own, 2 * width), 'frames', 0, 0, tiled=T...  4.58 us
    all_to_all x1, starting transfers between devices, step(): lax.all_to_all(first.reshape(4, half // 4, 2 * width), 'frames', 0, 0, ti...  3.53 us
  transfers between devices with their start and end apart: 11, of which 7 were waited for; matrix products, arithmetic and copies ran while one was open for 0% of the time, Pallas kernels for 5%

profile of v7, /device:TPU:6, one launch (start us, length us, event | category | flops | bytes accessed | tf_op | source)
XLA Modules:
  0.0 129.5 jit_solution(6525197455807498388)
XLA Ops:
  1.3 0.8 multiply_convert_fusion.1
  2.1 42.1 %all-gather.1 = f16[1024,1024]{1,0:T(8,128)(2,1)S(1)} all-gather(f16[32,1024]{1,0:T(8,128)(2,1)S(1)} %multiply_convert_fusion.1), channel_id=1, replica_groups=mesh['frames'=32,'phon'=4,'chap'=4] {'frames'}, dimensions={0}, use_global_device_ids=true | all-gather | bytes 2162688 | tf_op jit(solution)/shard_map/all_gather | solution.py:243
  44.2 0.0 copy-start.3
  44.2 0.6 multiply_convert_fusion.every
  44.8 0.0 copy-start
  44.8 0.0 copy-done.3
  44.9 4.2 %shard_map.93 = (bf16[1024,512]{1,0:T(8,128)(2,1)S(1)}, bf16[1024,512]{1,0:T(8,128)(2,1)S(1)}, bf16[512,512]{1,0:T(8,128)(2,1)}, f32[3,512]{1,0:T(4,128)S(1)}) custom-call(s32[32]{0:T(128)S(1)} %and_convert_fusion.flags, bf16[1024,1024]{1,0:T(8,128)(2,1)S(1)} %multiply_convert_fusion.every, bf16[512,512]{1,0:T(8,128)(2,1)} %queries.3, ...), custom_call_target="tpu_custom_call" | custom-call | flops 1073741824 | bytes 5773440 | tf_op jit(solution)/shard_map/pallas_call | solution.py:41
  49.1 3.5 %collective-permute-start = (f32[3,512]{1,0:T(4,128)S(1)}, f32[3,512]{1,0:T(4,128)S(1)}, u32[]{:S(2)}, u32[]{:S(2)}) collective-permute-start(f32[3,512]{1,0:T(4,128)S(1)} %get-tuple-element.16.stats), channel_id=1, source_target_pairs={{0,4},{4,8},{8,12},{12,0},{1,5},{5,9},{9,13},{13,1},{2,6},{6,10},{... | collective-permute-start | bytes 18440 | tf_op jit(solution)/shard_map/ppermute | solution.py:219
  52.6 3.6 %collective-permute-start.1 = (f32[3,512]{1,0:T(4,128)S(1)}, f32[3,512]{1,0:T(4,128)S(1)}, u32[]{:S(2)}, u32[]{:S(2)}) collective-permute-start(f32[3,512]{1,0:T(4,128)S(1)} %get-tuple-element.16.stats), channel_id=1, source_target_pairs={{0,12},{4,0},{8,4},{12,8},{1,13},{5,1},{9,5},{13,9},{2,14},{6,2},{... | collective-permute-start | bytes 18440 | tf_op jit(solution)/shard_map/ppermute | solution.py:219
  56.2 0.0 collective-permute-done.stats_up
  56.2 2.0 %collective-permute-done.1.stats_down = f32[3,512]{1,0:T(4,128)S(1)} collective-permute-done((f32[3,512]{1,0:T(4,128)S(1)}, f32[3,512]{1,0:T(4,128)S(1)}, u32[]{:S(2)}, u32[]{:S(2)}) %collective-permute-start.1) | collective-permute-done | bytes 6176 | tf_op jit(solution)/shard_map/ppermute | solution.py:219
  58.2 0.0 copy-done
  58.2 3.8 %shard_map.95 = (bf16[512,1024]{1,0:T(8,128)(2,1)}, bf16[512,512]{1,0:T(8,128)(2,1)}) custom-call(s32[1]{0:T(128)} %bitcast.3.start, s32[32]{0:T(128)S(1)} %and_convert_fusion.flags, f32[3,512]{1,0:T(4,128)S(1)} %get-tuple-element.16.stats, f32[3,512]{1,0:T(4,128)S(1)} %collective-permute-done.stats_up, f32[3,512]{1,0:T(4,128)S(1)} %collective-permute-done.1.stats_down, ...), custom_call_target="tpu_custom_call" | custom-call | flops 1073741824 | bytes 4737156 | tf_op jit(solution)/shard_map/pallas_call | solution.py:41
  61.9 1.9 %collective-permute-start.8 = (bf16[512,1024]{1,0:T(8,128)(2,1)}, bf16[512,1024]{1,0:T(8,128)(2,1)}, u32[]{:S(2)}, u32[]{:S(2)}) collective-permute-start(bf16[512,1024]{1,0:T(8,128)(2,1)} %get-tuple-element.27), channel_id=1, source_target_pairs={{0,16},{16,0},{32,48},{48,32},{64,80},{80,64},{96,112},{112,96},{1... | collective-permute-start | bytes 3145736 | tf_op jit(solution)/shard_map/ppermute | solution.py:283
  63.9 3.3 %shard_map.94 = (bf16[512,1024]{1,0:T(8,128)(2,1)S(1)}, bf16[512,512]{1,0:T(8,128)(2,1)}) custom-call(s32[1]{0:T(128)} %bitcast.1.start, s32[32]{0:T(128)S(1)} %and_convert_fusion.flags, f32[3,512]{1,0:T(4,128)S(1)} %get-tuple-element.16.stats, f32[3,512]{1,0:T(4,128)S(1)} %collective-permute-done.stats_up, f32[3,512]{1,0:T(4,128)S(1)} %collective-permute-done.1.stats_down, ...), custom_call_target="tpu_custom_call" | custom-call | flops 1073741824 | bytes 4737156 | tf_op jit(solution)/shard_map/pallas_call | solution.py:41
  67.2 0.0 collective-permute-done.8.came_far
  67.2 2.1 %shard_map.97 = bf16[512,1024]{1,0:T(8,128)(2,1)} custom-call(bf16[512,1024]{1,0:T(8,128)(2,1)S(1)} %get-tuple-element.26.keep, bf16[512,1024]{1,0:T(8,128)(2,1)} %collective-permute-done.8.came_far), custom_call_target="tpu_custom_call" | custom-call | bytes 3145728 | tf_op jit(solution)/shard_map/pallas_call | solution.py:41
  69.3 3.5 %all-to-all-start = ((bf16[4,128,1024]{2,1,0:T(8,128)(2,1)}), bf16[4,128,1024]{2,1,0:T(8,128)(2,1)S(1)}, u32[]{:S(2)}, u32[]{:S(2)}) async-start(bf16[4,128,1024]{2,1,0:T(8,128)(2,1)} %bitcast.44), calls=%async_computation | async-start | bytes 2097152 | tf_op jit(solution)/shard_map/all_to_all | solution.py:291
  72.8 0.1 pad_add_fusion.place
  72.9 2.7 %shard_map.96 = (bf16[128,1024]{1,0:T(8,128)(2,1)S(1)}, bf16[128,1024]{1,0:T(8,128)(2,1)S(1)}, bf16[128,1024]{1,0:T(8,128)(2,1)S(1)}, bf16[128,1024]{1,0:T(8,128)(2,1)S(1)}) custom-call(s32[2]{0:T(128)S(1)} %pad_add_fusion.place, f32[3,512]{1,0:T(4,128)S(1)} %get-tuple-element.16.stats, f32[3,512]{1,0:T(4,128)S(1)} %collective-permute-done.stats_up, ...), custom_call_target="tpu_custom_call" | custom-call | flops 536870912 | bytes 3688456 | tf_op jit(solution)/shard_map/pallas_call | solution.py:41
  75.6 4.8 %collective-permute-start.2 = (bf16[128,1024]{1,0:T(8,128)(2,1)S(1)}, bf16[128,1024]{1,0:T(8,128)(2,1)S(1)}, u32[]{:S(2)}, u32[]{:S(2)}) collective-permute-start(bf16[128,1024]{1,0:T(8,128)(2,1)S(1)} %get-tuple-element.23), channel_id=1, source_target_pairs={{0,8},{4,12},{8,0},{12,4},{1,9},{5,13},{9,1},{13,5},{2,10},{6,14},... | collective-permute-start | bytes 786440 | tf_op jit(solution)/shard_map/ppermute | solution.py:219
  80.4 2.7 %collective-permute-start.3 = (bf16[128,1024]{1,0:T(8,128)(2,1)S(1)}, bf16[128,1024]{1,0:T(8,128)(2,1)S(1)}, u32[]{:S(2)}, u32[]{:S(2)}) collective-permute-start(bf16[128,1024]{1,0:T(8,128)(2,1)S(1)} %get-tuple-element.24), channel_id=1, source_target_pairs={{0,4},{4,8},{8,12},{12,0},{1,5},{5,9},{9,13},{13,1},{2,6},{6,10},{... | collective-permute-start | bytes 786440 | tf_op jit(solution)/shard_map/ppermute | solution.py:219
  83.2 4.3 %collective-permute-start.4 = (bf16[128,1024]{1,0:T(8,128)(2,1)S(1)}, bf16[128,1024]{1,0:T(8,128)(2,1)S(1)}, u32[]{:S(2)}, u32[]{:S(2)}) collective-permute-start(bf16[128,1024]{1,0:T(8,128)(2,1)S(1)} %get-tuple-element.25), channel_id=1, source_target_pairs={{0,12},{4,0},{8,4},{12,8},{1,13},{5,1},{9,5},{13,9},{2,14},{6,2},{... | collective-permute-start | bytes 786440 | tf_op jit(solution)/shard_map/ppermute | solution.py:219
  87.5 0.7 collective-permute-done.2
  88.2 5.3 %collective-permute-done.3 = bf16[128,1024]{1,0:T(8,128)(2,1)S(1)} collective-permute-done((bf16[128,1024]{1,0:T(8,128)(2,1)S(1)}, bf16[128,1024]{1,0:T(8,128)(2,1)S(1)}, u32[]{:S(2)}, u32[]{:S(2)}) %collective-permute-start.3) | collective-permute-done | bytes 262176 | tf_op jit(solution)/shard_map/ppermute | solution.py:219
  93.5 0.2 collective-permute-done.4
  93.7 0.2 add_convert_fusion
  93.8 4.6 %collective-permute-start.5 = (bf16[128,1024]{1,0:T(8,128)(2,1)S(1)}, bf16[128,1024]{1,0:T(8,128)(2,1)S(1)}, u32[]{:S(2)}, u32[]{:S(2)}) collective-permute-start(bf16[128,1024]{1,0:T(8,128)(2,1)S(1)} %add_convert_fusion), channel_id=1, source_target_pairs={{0,8},{4,12},{8,0},{12,4},{1,9},{5,13},{9,1},{13,5},{2,10},{6,14},... | collective-permute-start | bytes 786440 | tf_op jit(solution)/shard_map/ppermute | solution.py:219
  98.5 3.3 %collective-permute-start.6 = (bf16[128,1024]{1,0:T(8,128)(2,1)S(1)}, bf16[128,1024]{1,0:T(8,128)(2,1)S(1)}, u32[]{:S(2)}, u32[]{:S(2)}) collective-permute-start(bf16[128,1024]{1,0:T(8,128)(2,1)S(1)} %add_convert_fusion), channel_id=1, source_target_pairs={{0,12},{4,0},{8,4},{12,8},{1,13},{5,1},{9,5},{13,9},{2,14},{6,2},{... | collective-permute-start | bytes 786440 | tf_op jit(solution)/shard_map/ppermute | solution.py:219
  101.7 2.6 %collective-permute-start.7 = (bf16[128,1024]{1,0:T(8,128)(2,1)S(1)}, bf16[128,1024]{1,0:T(8,128)(2,1)S(1)}, u32[]{:S(2)}, u32[]{:S(2)}) collective-permute-start(bf16[128,1024]{1,0:T(8,128)(2,1)S(1)} %add_convert_fusion), channel_id=1, source_target_pairs={{0,4},{4,8},{8,12},{12,0},{1,5},{5,9},{9,13},{13,1},{2,6},{6,10},{... | collective-permute-start | bytes 786440 | tf_op jit(solution)/shard_map/ppermute | solution.py:219
  104.4 0.0 all-to-all-done.came
  104.4 0.8 shard_map.98
  105.3 4.6 %all-to-all-start.1 = ((bf16[4,32,1024]{2,1,0:T(8,128)(2,1)}), bf16[4,32,1024]{2,1,0:T(8,128)(2,1)S(1)}, u32[]{:S(2)}, u32[]{:S(2)}) async-start(bf16[4,32,1024]{2,1,0:T(8,128)(2,1)} %bitcast.15), calls=%async_computation.1 | async-start | bytes 524288 | tf_op jit(solution)/shard_map/all_to_all | solution.py:319
  109.9 0.0 collective-permute-done.5
  109.9 1.0 collective-permute-done.6
  110.9 1.6 %collective-permute-done.7 = bf16[128,1024]{1,0:T(8,128)(2,1)S(1)} collective-permute-done((bf16[128,1024]{1,0:T(8,128)(2,1)S(1)}, bf16[128,1024]{1,0:T(8,128)(2,1)S(1)}, u32[]{:S(2)}, u32[]{:S(2)}) %collective-permute-start.7) | collective-permute-done | bytes 262176 | tf_op jit(solution)/shard_map/ppermute | solution.py:219
  112.6 0.0 copy-start.1
  112.6 0.0 copy-start.2
  112.6 16.2 %all-to-all-done.1 = bf16[4,32,1024]{2,1,0:T(8,128)(2,1)S(1)} async-done(((bf16[4,32,1024]{2,1,0:T(8,128)(2,1)}), bf16[4,32,1024]{2,1,0:T(8,128)(2,1)S(1)}, u32[]{:S(2)}, u32[]{:S(2)}) %all-to-all-start.1) | async-done | bytes 262176 | tf_op jit(solution)/shard_map/all_to_all | solution.py:319
  128.8 0.7 fusion.8
  129.5 0.0 copy-done.1
  129.5 0.0 copy-done.2
  (9 shorter events, 0.2 us)
Async XLA Ops:
  44.2 0.7 copy-start.3
  44.8 13.3 %copy-start = (bf16[512,512]{1,0:T(8,128)(2,1)S(1)}, bf16[512,512]{1,0:T(8,128)(2,1)}, u32[]{:S(2)}) copy-start(bf16[512,512]{1,0:T(8,128)(2,1)} %queries.3) | copy-start | bytes 1572868
  49.1 7.1 %collective-permute-start = (f32[3,512]{1,0:T(4,128)S(1)}, f32[3,512]{1,0:T(4,128)S(1)}, u32[]{:S(2)}, u32[]{:S(2)}) collective-permute-start(f32[3,512]{1,0:T(4,128)S(1)} %get-tuple-element.16.stats), channel_id=1, source_target_pairs={{0,4},{4,8},{8,12},{12,0},{1,5},{5,9},{9,13},{13,1},{2,6},{6,10},{... | collective-permute-start | bytes 18440 | tf_op jit(solution)/shard_map/ppermute | solution.py:219
  52.6 5.5 %collective-permute-start.1 = (f32[3,512]{1,0:T(4,128)S(1)}, f32[3,512]{1,0:T(4,128)S(1)}, u32[]{:S(2)}, u32[]{:S(2)}) collective-permute-start(f32[3,512]{1,0:T(4,128)S(1)} %get-tuple-element.16.stats), channel_id=1, source_target_pairs={{0,12},{4,0},{8,4},{12,8},{1,13},{5,1},{9,5},{13,9},{2,14},{6,2},{... | collective-permute-start | bytes 18440 | tf_op jit(solution)/shard_map/ppermute | solution.py:219
  61.9 5.2 %collective-permute-start.8 = (bf16[512,1024]{1,0:T(8,128)(2,1)}, bf16[512,1024]{1,0:T(8,128)(2,1)}, u32[]{:S(2)}, u32[]{:S(2)}) collective-permute-start(bf16[512,1024]{1,0:T(8,128)(2,1)} %get-tuple-element.27), channel_id=1, source_target_pairs={{0,16},{16,0},{32,48},{48,32},{64,80},{80,64},{96,112},{112,96},{1... | collective-permute-start | bytes 3145736 | tf_op jit(solution)/shard_map/ppermute | solution.py:283
  69.3 35.1 %all-to-all-start = ((bf16[4,128,1024]{2,1,0:T(8,128)(2,1)}), bf16[4,128,1024]{2,1,0:T(8,128)(2,1)S(1)}, u32[]{:S(2)}, u32[]{:S(2)}) async-start(bf16[4,128,1024]{2,1,0:T(8,128)(2,1)} %bitcast.44), calls=%async_computation | async-start | bytes 2097152 | tf_op jit(solution)/shard_map/all_to_all | solution.py:291
  75.6 12.6 %collective-permute-start.2 = (bf16[128,1024]{1,0:T(8,128)(2,1)S(1)}, bf16[128,1024]{1,0:T(8,128)(2,1)S(1)}, u32[]{:S(2)}, u32[]{:S(2)}) collective-permute-start(bf16[128,1024]{1,0:T(8,128)(2,1)S(1)} %get-tuple-element.23), channel_id=1, source_target_pairs={{0,8},{4,12},{8,0},{12,4},{1,9},{5,13},{9,1},{13,5},{2,10},{6,14},... | collective-permute-start | bytes 786440 | tf_op jit(solution)/shard_map/ppermute | solution.py:219
  80.4 13.0 %collective-permute-start.3 = (bf16[128,1024]{1,0:T(8,128)(2,1)S(1)}, bf16[128,1024]{1,0:T(8,128)(2,1)S(1)}, u32[]{:S(2)}, u32[]{:S(2)}) collective-permute-start(bf16[128,1024]{1,0:T(8,128)(2,1)S(1)} %get-tuple-element.24), channel_id=1, source_target_pairs={{0,4},{4,8},{8,12},{12,0},{1,5},{5,9},{9,13},{13,1},{2,6},{6,10},{... | collective-permute-start | bytes 786440 | tf_op jit(solution)/shard_map/ppermute | solution.py:219
  83.2 10.5 %collective-permute-start.4 = (bf16[128,1024]{1,0:T(8,128)(2,1)S(1)}, bf16[128,1024]{1,0:T(8,128)(2,1)S(1)}, u32[]{:S(2)}, u32[]{:S(2)}) collective-permute-start(bf16[128,1024]{1,0:T(8,128)(2,1)S(1)} %get-tuple-element.25), channel_id=1, source_target_pairs={{0,12},{4,0},{8,4},{12,8},{1,13},{5,1},{9,5},{13,9},{2,14},{6,2},{... | collective-permute-start | bytes 786440 | tf_op jit(solution)/shard_map/ppermute | solution.py:219
  93.8 16.1 %collective-permute-start.5 = (bf16[128,1024]{1,0:T(8,128)(2,1)S(1)}, bf16[128,1024]{1,0:T(8,128)(2,1)S(1)}, u32[]{:S(2)}, u32[]{:S(2)}) collective-permute-start(bf16[128,1024]{1,0:T(8,128)(2,1)S(1)} %add_convert_fusion), channel_id=1, source_target_pairs={{0,8},{4,12},{8,0},{12,4},{1,9},{5,13},{9,1},{13,5},{2,10},{6,14},... | collective-permute-start | bytes 786440 | tf_op jit(solution)/shard_map/ppermute | solution.py:219
  98.5 12.4 %collective-permute-start.6 = (bf16[128,1024]{1,0:T(8,128)(2,1)S(1)}, bf16[128,1024]{1,0:T(8,128)(2,1)S(1)}, u32[]{:S(2)}, u32[]{:S(2)}) collective-permute-start(bf16[128,1024]{1,0:T(8,128)(2,1)S(1)} %add_convert_fusion), channel_id=1, source_target_pairs={{0,12},{4,0},{8,4},{12,8},{1,13},{5,1},{9,5},{13,9},{2,14},{6,2},{... | collective-permute-start | bytes 786440 | tf_op jit(solution)/shard_map/ppermute | solution.py:219
  101.7 10.8 %collective-permute-start.7 = (bf16[128,1024]{1,0:T(8,128)(2,1)S(1)}, bf16[128,1024]{1,0:T(8,128)(2,1)S(1)}, u32[]{:S(2)}, u32[]{:S(2)}) collective-permute-start(bf16[128,1024]{1,0:T(8,128)(2,1)S(1)} %add_convert_fusion), channel_id=1, source_target_pairs={{0,4},{4,8},{8,12},{12,0},{1,5},{5,9},{9,13},{13,1},{2,6},{6,10},{... | collective-permute-start | bytes 786440 | tf_op jit(solution)/shard_map/ppermute | solution.py:219
  105.3 23.5 %all-to-all-start.1 = ((bf16[4,32,1024]{2,1,0:T(8,128)(2,1)}), bf16[4,32,1024]{2,1,0:T(8,128)(2,1)S(1)}, u32[]{:S(2)}, u32[]{:S(2)}) async-start(bf16[4,32,1024]{2,1,0:T(8,128)(2,1)} %bitcast.15), calls=%async_computation.1 | async-start | bytes 524288 | tf_op jit(solution)/shard_map/all_to_all | solution.py:319
  112.6 16.9 %copy-start.1 = (bf16[4,128,512]{2,1,0:T(8,128)(2,1)}, bf16[4,128,512]{2,1,0:T(8,128)(2,1)S(1)}, u32[]{:S(2)}) copy-start(bf16[4,128,512]{2,1,0:T(8,128)(2,1)S(1)} %get-tuple-element.28) | copy-start | bytes 1572868
  112.6 16.9 %copy-start.2 = (bf16[4,128,512]{2,1,0:T(8,128)(2,1)}, bf16[4,128,512]{2,1,0:T(8,128)(2,1)S(1)}, u32[]{:S(2)}) copy-start(bf16[4,128,512]{2,1,0:T(8,128)(2,1)S(1)} %get-tuple-element.29) | copy-start | bytes 1572868

commit v8 on v7

--- a/solution.py
+++ b/solution.py
@@ -12,7 +12,6 @@
 NEG_FILL = -1e30
 FLOOR = -1e29
 LIFT = 4096.0
-CHUNK = 512
 NT = (((1,), (1,)), ((), ()))
 TN = (((0,), (0,)), ((), ()))
 F32, BF16 = jnp.float32, jnp.bfloat16
@@ -49,60 +48,69 @@
     )(*[pltpu.with_memory_space_constraint(a, HBM) if space == HBM else a for a, space in args])
 
 
-def masked(scores, flags, first, own):
-    return jnp.concatenate(
-        [
-            jnp.where(flags[first + j] > 0, scores[own * j : own * (j + 1)], NEG_FILL)
-            for j in range(scores.shape[0] // own)
-        ],
-        axis=0,
-    )
+def half_rows(every, core, own, columns):
+    count = len(BLOCKS) // 2
+    rows = []
+    for i in range(count):
+        at = ((BLOCKS[i] + 4 * core) & (2 * count - 1)) + core
+        rows.append(every[pl.ds(pl.multiple_of(at * own, own), own), columns])
+    return jnp.concatenate(rows, axis=0)
+
+
+def masked_half(scores, flags, core, own):
+    count = len(BLOCKS) // 2
+    parts = []
+    for i in range(count):
+        at = ((BLOCKS[i] + 4 * core) & (2 * count - 1)) + core
+        parts.append(
+            jnp.where(flags[at * own // TILE] > 0, scores[own * i : own * (i + 1)], NEG_FILL)
+        )
+    return jnp.concatenate(parts, axis=0)
 
 
 def forward_kernel(
-    flags, every, queries_far, cotangent_far, keys, values, features_far, stats,
-    scores_at, expd, queries, cotangent, features, sems,
+    flags, every, queries, cotangent_far, features_far, stats,
+    scores_at, expd, cotangent, features, sems,
 ):
-    block, width = keys.shape
-    own = block // len(BLOCKS)
+    block = every.shape[0]
+    rows, width = queries.shape
     scale = width ** (-0.5)
-    rows = queries.shape[0]
-    fetch_q = pltpu.make_async_copy(queries_far, queries, sems.at[0])
-    fetch_g = pltpu.make_async_copy(cotangent_far, cotangent, sems.at[1])
-    fetch_q.start()
+    fetch_g = pltpu.make_async_copy(cotangent_far, cotangent, sems.at[0])
     fetch_g.start()
     peak = jnp.full((1, rows), FLOOR, F32)
-    for at in range(0, block, CHUNK):
-        for i in range(at // own, (at + CHUNK) // own):
-            piece = every[own * BLOCKS[i] : own * (BLOCKS[i] + 1), :]
-            keys[own * i : own * (i + 1), :] = piece[:, :width]
-            values[own * i : own * (i + 1), :] = piece[:, width:]
-        if at == 0:
-            fetch_q.wait()
-        here = slice(at, at + CHUNK)
-        key = keys[here, :].astype(F32)
+    for tile in range(block // TILE):
+        here = slice(tile * TILE, (tile + 1) * TILE)
+        low_key = every[here, :width]
+        key = low_key.astype(F32)
         offset = jnp.sum(key * key, axis=1, keepdims=True) * (-0.5 * scale)
-        raw = lax.dot_general(keys[here, :], queries[...], NT, preferred_element_type=F32)
-        scores = masked(raw * scale + offset, flags, at // own, own)
+        raw = lax.dot_general(low_key, queries[...], NT, preferred_element_type=F32)
+        scores = jnp.where(flags[tile] > 0, raw * scale + offset, NEG_FILL)
         scores_at[here, :] = scores
         peak = jnp.maximum(peak, jnp.max(scores, axis=0, keepdims=True))
     total = jnp.zeros_like(peak)
-    for at in range(0, block, CHUNK):
-        here = slice(at, at + CHUNK)
+    for tile in range(block // TILE):
+        here = slice(tile * TILE, (tile + 1) * TILE)
         e = jnp.exp(scores_at[here, :] - peak)
         expd[here, :] = e.astype(BF16)
         total += jnp.sum(e, axis=0, keepdims=True)
-    out = lax.dot_general(expd[...], values[...], TN, preferred_element_type=F32)
-    features[...] = out.astype(BF16)
-    store_f = pltpu.make_async_copy(features, features_far, sems.at[2])
-    store_f.start()
-    fetch_g.wait()
-    delta = jnp.sum(cotangent[...].astype(F32) * out, axis=1, keepdims=True)
-    delta = jnp.transpose(jnp.broadcast_to(delta, (rows, 128)))[0:1, :]
+    deltas, stores = [], []
+    for i in range(2):
+        part = pl.ds(i * rows // 2, rows // 2)
+        out = lax.dot_general(expd[:, part], every[:, width:], TN, preferred_element_type=F32)
+        features[part, :] = out.astype(BF16)
+        copy = pltpu.make_async_copy(features.at[part], features_far.at[part], sems.at[1 + i])
+        copy.start()
+        stores.append(copy)
+        if i == 0:
+            fetch_g.wait()
+        delta = jnp.sum(cotangent[part, :].astype(F32) * out, axis=1, keepdims=True)
+        deltas.append(jnp.transpose(jnp.broadcast_to(delta, (rows // 2, 128)))[0:1, :])
+    delta = jnp.concatenate(deltas, axis=1)
     stats[0:1, :] = peak
     stats[1:2, :] = total
     stats[2:3, :] = delta
-    store_f.wait()
+    for copy in stores:
+        copy.wait()
 
 
 def merged(heard):
@@ -117,26 +125,27 @@
 
 
 def backward_kernel(
-    start, flags, stats, stats_up, stats_down, keys, values, queries, cotangent_far,
+    side, flags, stats, stats_up, stats_down, every, queries, cotangent_far,
     grads_out, ds_far, cotangent, ds_low, sems, *room,
 ):
     grads = room[0] if room else grads_out
-    half, width = grads.shape[0], keys.shape[1]
+    width = queries.shape[1]
     scale = width ** (-0.5)
-    own = 2 * half // len(BLOCKS)
-    mine = pl.ds(pl.multiple_of(start[0], half), half)
+    own = every.shape[0] // len(BLOCKS)
+    core = side[0]
     fetch_g = pltpu.make_async_copy(cotangent_far, cotangent, sems.at[1])
     fetch_g.start()
     peak, total, delta = merged((stats, stats_up, stats_down))
     delta = delta / total
     lse = peak + jnp.log(total)
-    low_key = keys[mine, :]
+    low_key = half_rows(every, core, own, slice(0, width))
     key = low_key.astype(F32)
     offset = jnp.sum(key * key, axis=1, keepdims=True) * (-0.5 * scale)
     raw = lax.dot_general(low_key, queries[...], NT, preferred_element_type=F32)
     fetch_g.wait()
-    dp = lax.dot_general(values[mine, :], cotangent[...], NT, preferred_element_type=F32)
-    scores = masked(raw * scale + offset, flags, start[0] // own, own)
+    low_value = half_rows(every, core, own, slice(width, 2 * width))
+    dp = lax.dot_general(low_value, cotangent[...], NT, preferred_element_type=F32)
+    scores = masked_half(raw * scale + offset, flags, core, own)
     probs = jnp.exp(scores - lse)
     value = jnp.dot(probs.astype(BF16), cotangent[...], preferred_element_type=F32)
     grads[:, width:] = value.astype(BF16)
@@ -152,7 +161,7 @@
     stores[-1].start()
     column = jnp.sum(ds, axis=1, keepdims=True)
     grad = jnp.dot(low, queries[...], preferred_element_type=F32)
-    grads[:, :width] = ((grad - column * keys[mine, :].astype(F32)) * scale).astype(BF16)
+    grads[:, :width] = ((grad - column * low_key.astype(F32)) * scale).astype(BF16)
     left = pl.ds(0, width)
     if room:
         stores += [pltpu.make_async_copy(grads.at[:, left], grads_out.at[:, left], sems.at[3])]
@@ -162,12 +171,12 @@
 
 
 def outputs_kernel(
-    place, stats, stats_up, stats_down, keys, features_far, keep_far, send_far, *rest
+    place, stats, stats_up, stats_down, every, features_far, keep_far, send_far, *rest
 ):
     parts, (features, low, gathered, sems) = rest[:4], rest[4:]
     quarter = parts[0].shape[0]
-    half, rows = low.shape[1:]
-    width = keys.shape[1]
+    rows, width = features.shape
+    own = every.shape[0] // len(BLOCKS)
     fetches = [
         pltpu.make_async_copy(far, near, sems.at[i])
         for i, (far, near) in enumerate(
@@ -183,9 +192,9 @@
     fetches[0].wait()
     gathered[:, width:] = (features[...].astype(F32) * share).astype(BF16)
     query = jnp.zeros((rows, width), F32)
-    for i, at in enumerate((place[1], half - place[1])):
+    for i, core in enumerate((place[1], 1 - place[1])):
         fetches[i + 1].wait()
-        right = keys[pl.ds(pl.multiple_of(at, half), half), :]
+        right = half_rows(every, core, own, slice(0, width))
         query += lax.dot_general(low[i], right, TN, preferred_element_type=F32)
     gathered[:, :width] = (query * width ** (-0.5)).astype(BF16)
     for d, part in enumerate(parts):
@@ -193,19 +202,15 @@
         part[...] = gathered[pl.ds(pl.multiple_of(at, quarter), quarter), :]
 
 
-def add_kernel(keep, came_far, out, came, sems):
-    n = sems.shape[1]
+def add_kernel(keep, came, out, made, sems):
+    n = sems.shape[0]
     size = keep.shape[0] // n
-    parts = [pl.ds(size * i, size) for i in range(n)]
-    copy = pltpu.make_async_copy
-    fetches = [copy(came_far.at[p], came.at[p], sems.at[0, i]) for i, p in enumerate(parts)]
-    stores = [copy(came.at[p], out.at[p], sems.at[1, i]) for i, p in enumerate(parts)]
-    for fetch in fetches:
-        fetch.start()
-    for i, p in enumerate(parts):
-        fetches[i].wait()
-        came[p, :] = (keep[p, :].astype(F32) + came[p, :].astype(F32)).astype(BF16)
-        stores[i].start()
+    stores = []
+    for i in range(n):
+        part = pl.ds(size * i, size)
+        made[part, :] = (keep[part, :].astype(F32) + came[part, :].astype(F32)).astype(BF16)
+        stores.append(pltpu.make_async_copy(made.at[part], out.at[part], sems.at[i]))
+        stores[-1].start()
     for store in stores:
         store.wait()
 
@@ -242,17 +247,17 @@
     both = jnp.concatenate([keys, values], axis=1).astype(F32) * LIFT
     every = lax.all_gather(both.astype(jnp.float16), "frames", axis=0, tiled=True)
     every = (every.astype(F32) * (1.0 / LIFT)).astype(BF16)
-    tiles = phon * (block // TILE) + jnp.asarray(np.asarray(BLOCKS, np.int32) * own // TILE)
+    tiles = phon * (block // TILE) + jnp.arange(block // TILE, dtype=jnp.int32)
     flags = ((tiles >= band_first[0]) & (tiles < band_first[0] + NBAND)).astype(jnp.int32)
     work = 2 * block * rows * width
-    block_keys, block_values, features, stats = call(
+    features, stats = call(
         forward_kernel,
-        [((block, width), BF16, VMEM)] * 2 + [((rows, width), BF16, HBM), ((3, rows), F32, VMEM)],
-        [(flags, SMEM), (every, VMEM), (queries, HBM), (cotangent, HBM)],
+        [((rows, width), BF16, HBM), ((3, rows), F32, VMEM)],
+        [(flags, SMEM), (every, VMEM), (queries, VMEM), (cotangent, HBM)],
         [
             pltpu.VMEM((block, rows), F32),
             pltpu.VMEM((block, rows), BF16),
-            *near,
+            near[0],
             pltpu.VMEM((rows, width), BF16),
             dma((3,)),
         ],
@@ -260,16 +265,15 @@
     )
     heard = [(stats, VMEM), (shifted(stats, "phon", 1), VMEM), (shifted(stats, "phon", 3), VMEM)]
 
-    def backward(start, space=HBM):
+    def backward(side, space=HBM):
         return call(
             backward_kernel,
             [((half, 2 * width), BF16, space), ((half, rows), BF16, HBM)],
             [
-                (jnp.reshape(start, (1,)).astype(jnp.int32), SMEM),
+                (jnp.reshape(side, (1,)).astype(jnp.int32), SMEM),
                 (flags, SMEM),
                 *heard,
-                (block_keys, VMEM),
-                (block_values, VMEM),
+                (every, VMEM),
                 (queries, VMEM),
                 (cotangent, HBM),
             ],
@@ -279,28 +283,28 @@
             2 * work,
         )
 
-    send, send_ds = backward((1 - core) * half)
+    send, send_ds = backward(1 - core)
     came = lax.ppermute(send, "frames", [(i, i ^ 1) for i in range(n)])
-    keep, keep_ds = backward(core * half, VMEM)
+    keep, keep_ds = backward(core, VMEM)
     (first,) = call(
         add_kernel,
         [((half, 2 * width), BF16, HBM)],
-        [(keep, VMEM), (came, HBM)],
-        [pltpu.VMEM((half, 2 * width), BF16), dma((2, 4))],
+        [(keep, VMEM), (came, VMEM)],
+        [pltpu.VMEM((half, 2 * width), BF16), dma((4,))],
     )
     first = lax.all_to_all(
         first.reshape(4, half // 4, 2 * width), "frames", 0, 0, tiled=True,
         axis_index_groups=QUADS,
     )
 
-    place = jnp.stack([phon, core * half]).astype(jnp.int32)
+    place = jnp.stack([phon, core]).astype(jnp.int32)
     parts = call(
         outputs_kernel,
         [((quarter, 2 * width), BF16, VMEM)] * 4,
         [
             (place, SMEM),
             *heard,
-            (block_keys, VMEM),
+            (every, VMEM),
             (features, HBM),
             (keep_ds, HBM),
             (send_ds, HBM),

time: 130 us -> 130 us (level)
  transfers between devices with their start and end apart: 11 -> 11, of which waited for: 7 -> 7; matrix products, arithmetic and copies ran while one was open for 0% -> 0% of each run, Pallas kernels for 5% -> 6%
where the time goes in v8:
time: 130 us; the launch traced here: 129 us
  blocking collectives  42.1 us (32%)
  starting transfers between devices  39.4 us (30%)
  waiting for transfers between devices  27.1 us (21%)
  Pallas kernels  16.3 us (13%)
  other arithmetic  1.68 us (1%)
  between operations  1.54 us (1%)
    all_gather x1, blocking collectives, step(): lax.all_gather(both.astype(jnp.float16), 'frames', axis=0, tiled=True)  42.1 us
    ppermute x8, starting transfers between devices, shifted(): return lax.ppermute(value, axis, [(i, (i + d) % n) for i in range(n)])  29.4 us
    pallas_call x6, Pallas kernels, call(): pl.pallas_call(kernel, out_shape=shapes, in_specs=[pl.BlockSpec(memory_sp...  16.3 us
    all_to_all x1, waiting for transfers between devices, step(): lax.all_to_all(second.reshape(4, own, 2 * width), 'frames', 0, 0, tiled=T...  16.2 us
    ppermute x8, waiting for transfers between devices, shifted(): return lax.ppermute(value, axis, [(i, (i + d) % n) for i in range(n)])  10.9 us
    all_to_all x1, starting transfers between devices, step(): lax.all_to_all(second.reshape(4, own, 2 * width), 'frames', 0, 0, tiled=T...  4.59 us
    all_to_all x1, starting transfers between devices, step(): lax.all_to_all(first.reshape(4, half // 4, 2 * width), 'frames', 0, 0, ti...  3.53 us
  transfers between devices with their start and end apart: 11, of which 7 were waited for; matrix products, arithmetic and copies ran while one was open for 0% of the time, Pallas kernels for 6%

profile of v8, /device:TPU:6, one launch (start us, length us, event | category | flops | bytes accessed | tf_op | source)
XLA Modules:
  0.0 129.5 jit_solution(2775724892962902880)
XLA Ops:
  1.3 0.8 multiply_convert_fusion.1
  2.1 42.1 %all-gather.1 = f16[1024,1024]{1,0:T(8,128)(2,1)S(1)} all-gather(f16[32,1024]{1,0:T(8,128)(2,1)S(1)} %multiply_convert_fusion.1), channel_id=1, replica_groups=mesh['frames'=32,'phon'=4,'chap'=4] {'frames'}, dimensions={0}, use_global_device_ids=true | all-gather | bytes 2162688 | tf_op jit(solution)/shard_map/all_gather | solution.py:248
  44.2 0.0 copy-start
  44.2 0.6 multiply_convert_fusion.every
  44.8 0.4 copy-done
  45.3 3.4 %shard_map.84 = (bf16[512,512]{1,0:T(8,128)(2,1)}, f32[3,512]{1,0:T(4,128)S(1)}) custom-call(s32[2]{0:T(128)S(1)} %and_convert_fusion.flags, bf16[1024,1024]{1,0:T(8,128)(2,1)S(1)} %multiply_convert_fusion.every, bf16[512,512]{1,0:T(8,128)(2,1)S(1)} %copy-done, bf16[512,512]{1,0:T(8,128)(2,1)} %cotangent_far.5), custom_call_target="tpu_custom_call" | custom-call | flops 1073741824 | bytes 3676168 | tf_op jit(solution)/shard_map/pallas_call | solution.py:40
  48.7 3.5 %collective-permute-start = (f32[3,512]{1,0:T(4,128)S(1)}, f32[3,512]{1,0:T(4,128)S(1)}, u32[]{:S(2)}, u32[]{:S(2)}) collective-permute-start(f32[3,512]{1,0:T(4,128)S(1)} %get-tuple-element.14.stats), channel_id=1, source_target_pairs={{0,4},{4,8},{8,12},{12,0},{1,5},{5,9},{9,13},{13,1},{2,6},{6,10},{... | collective-permute-start | bytes 18440 | tf_op jit(solution)/shard_map/ppermute | solution.py:224
  52.2 3.6 %collective-permute-start.1 = (f32[3,512]{1,0:T(4,128)S(1)}, f32[3,512]{1,0:T(4,128)S(1)}, u32[]{:S(2)}, u32[]{:S(2)}) collective-permute-start(f32[3,512]{1,0:T(4,128)S(1)} %get-tuple-element.14.stats), channel_id=1, source_target_pairs={{0,12},{4,0},{8,4},{12,8},{1,13},{5,1},{9,5},{13,9},{2,14},{6,2},{... | collective-permute-start | bytes 18440 | tf_op jit(solution)/shard_map/ppermute | solution.py:224
  55.8 0.0 collective-permute-done.stats_up
  55.8 1.9 %collective-permute-done.1.stats_down = f32[3,512]{1,0:T(4,128)S(1)} collective-permute-done((f32[3,512]{1,0:T(4,128)S(1)}, f32[3,512]{1,0:T(4,128)S(1)}, u32[]{:S(2)}, u32[]{:S(2)}) %collective-permute-start.1) | collective-permute-done | bytes 6176 | tf_op jit(solution)/shard_map/ppermute | solution.py:224
  57.7 4.0 %shard_map.86 = (bf16[512,1024]{1,0:T(8,128)(2,1)}, bf16[512,512]{1,0:T(8,128)(2,1)}) custom-call(s32[1]{0:T(128)} %bitcast.3.side, s32[2]{0:T(128)S(1)} %and_convert_fusion.flags, f32[3,512]{1,0:T(4,128)S(1)} %get-tuple-element.14.stats, f32[3,512]{1,0:T(4,128)S(1)} %collective-permute-done.stats_up, f32[3,512]{1,0:T(4,128)S(1)} %collective-permute-done.1.stats_down, ...), custom_call_target="tpu_custom_call" | custom-call | flops 1073741824 | bytes 4737036 | tf_op jit(solution)/shard_map/pallas_call | solution.py:40
  61.7 1.9 %collective-permute-start.8 = (bf16[512,1024]{1,0:T(8,128)(2,1)}, bf16[512,1024]{1,0:T(8,128)(2,1)S(1)}, u32[]{:S(2)}, u32[]{:S(2)}) collective-permute-start(bf16[512,1024]{1,0:T(8,128)(2,1)} %get-tuple-element.23), channel_id=1, source_target_pairs={{0,16},{16,0},{32,48},{48,32},{64,80},{80,64},{96,112},{112,96},{1... | collective-permute-start | bytes 3145736 | tf_op jit(solution)/shard_map/ppermute | solution.py:287
  63.7 3.4 %shard_map.85 = (bf16[512,1024]{1,0:T(8,128)(2,1)S(1)}, bf16[512,512]{1,0:T(8,128)(2,1)}) custom-call(s32[1]{0:T(128)} %bitcast.1.side, s32[2]{0:T(128)S(1)} %and_convert_fusion.flags, f32[3,512]{1,0:T(4,128)S(1)} %get-tuple-element.14.stats, f32[3,512]{1,0:T(4,128)S(1)} %collective-permute-done.stats_up, f32[3,512]{1,0:T(4,128)S(1)} %collective-permute-done.1.stats_down, ...), custom_call_target="tpu_custom_call" | custom-call | flops 1073741824 | bytes 4737036 | tf_op jit(solution)/shard_map/pallas_call | solution.py:40
  67.0 0.0 collective-permute-done.8.came
  67.0 1.1 shard_map.88
  68.1 3.5 %all-to-all-start = ((bf16[4,128,1024]{2,1,0:T(8,128)(2,1)}), bf16[4,128,1024]{2,1,0:T(8,128)(2,1)S(1)}, u32[]{:S(2)}, u32[]{:S(2)}) async-start(bf16[4,128,1024]{2,1,0:T(8,128)(2,1)} %bitcast.44), calls=%async_computation | async-start | bytes 2097152 | tf_op jit(solution)/shard_map/all_to_all | solution.py:295
  71.7 0.1 pad_add_fusion.place
  71.8 3.6 %shard_map.87 = (bf16[128,1024]{1,0:T(8,128)(2,1)S(1)}, bf16[128,1024]{1,0:T(8,128)(2,1)}, bf16[128,1024]{1,0:T(8,128)(2,1)}, bf16[128,1024]{1,0:T(8,128)(2,1)}) custom-call(s32[2]{0:T(128)S(1)} %pad_add_fusion.place, f32[3,512]{1,0:T(4,128)S(1)} %get-tuple-element.14.stats, f32[3,512]{1,0:T(4,128)S(1)} %collective-permute-done.stats_up, ...), custom_call_target="tpu_custom_call" | custom-call | flops 536870912 | bytes 4737032 | tf_op jit(solution)/shard_map/pallas_call | solution.py:40
  75.4 4.8 %collective-permute-start.2 = (bf16[128,1024]{1,0:T(8,128)(2,1)}, bf16[128,1024]{1,0:T(8,128)(2,1)S(1)}, u32[]{:S(2)}, u32[]{:S(2)}) collective-permute-start(bf16[128,1024]{1,0:T(8,128)(2,1)} %get-tuple-element.19), channel_id=1, source_target_pairs={{0,8},{4,12},{8,0},{12,4},{1,9},{5,13},{9,1},{13,5},{2,10},{6,14},... | collective-permute-start | bytes 786440 | tf_op jit(solution)/shard_map/ppermute | solution.py:224
  80.2 2.7 %collective-permute-start.3 = (bf16[128,1024]{1,0:T(8,128)(2,1)}, bf16[128,1024]{1,0:T(8,128)(2,1)S(1)}, u32[]{:S(2)}, u32[]{:S(2)}) collective-permute-start(bf16[128,1024]{1,0:T(8,128)(2,1)} %get-tuple-element.20), channel_id=1, source_target_pairs={{0,4},{4,8},{8,12},{12,0},{1,5},{5,9},{9,13},{13,1},{2,6},{6,10},{... | collective-permute-start | bytes 786440 | tf_op jit(solution)/shard_map/ppermute | solution.py:224
  83.0 4.3 %collective-permute-start.4 = (bf16[128,1024]{1,0:T(8,128)(2,1)}, bf16[128,1024]{1,0:T(8,128)(2,1)S(1)}, u32[]{:S(2)}, u32[]{:S(2)}) collective-permute-start(bf16[128,1024]{1,0:T(8,128)(2,1)} %get-tuple-element.21), channel_id=1, source_target_pairs={{0,12},{4,0},{8,4},{12,8},{1,13},{5,1},{9,5},{13,9},{2,14},{6,2},{... | collective-permute-start | bytes 786440 | tf_op jit(solution)/shard_map/ppermute | solution.py:224
  87.3 0.9 collective-permute-done.2
  88.2 5.3 %collective-permute-done.3 = bf16[128,1024]{1,0:T(8,128)(2,1)S(1)} collective-permute-done((bf16[128,1024]{1,0:T(8,128)(2,1)}, bf16[128,1024]{1,0:T(8,128)(2,1)S(1)}, u32[]{:S(2)}, u32[]{:S(2)}) %collective-permute-start.3) | collective-permute-done | bytes 262176 | tf_op jit(solution)/shard_map/ppermute | solution.py:224
  93.5 0.2 collective-permute-done.4
  93.7 0.2 add_convert_fusion
  93.8 4.6 %collective-permute-start.5 = (bf16[128,1024]{1,0:T(8,128)(2,1)S(1)}, bf16[128,1024]{1,0:T(8,128)(2,1)S(1)}, u32[]{:S(2)}, u32[]{:S(2)}) collective-permute-start(bf16[128,1024]{1,0:T(8,128)(2,1)S(1)} %add_convert_fusion), channel_id=1, source_target_pairs={{0,8},{4,12},{8,0},{12,4},{1,9},{5,13},{9,1},{13,5},{2,10},{6,14},... | collective-permute-start | bytes 786440 | tf_op jit(solution)/shard_map/ppermute | solution.py:224
  98.5 3.3 %collective-permute-start.6 = (bf16[128,1024]{1,0:T(8,128)(2,1)S(1)}, bf16[128,1024]{1,0:T(8,128)(2,1)S(1)}, u32[]{:S(2)}, u32[]{:S(2)}) collective-permute-start(bf16[128,1024]{1,0:T(8,128)(2,1)S(1)} %add_convert_fusion), channel_id=1, source_target_pairs={{0,12},{4,0},{8,4},{12,8},{1,13},{5,1},{9,5},{13,9},{2,14},{6,2},{... | collective-permute-start | bytes 786440 | tf_op jit(solution)/shard_map/ppermute | solution.py:224
  101.7 2.6 %collective-permute-start.7 = (bf16[128,1024]{1,0:T(8,128)(2,1)S(1)}, bf16[128,1024]{1,0:T(8,128)(2,1)S(1)}, u32[]{:S(2)}, u32[]{:S(2)}) collective-permute-start(bf16[128,1024]{1,0:T(8,128)(2,1)S(1)} %add_convert_fusion), channel_id=1, source_target_pairs={{0,4},{4,8},{8,12},{12,0},{1,5},{5,9},{9,13},{13,1},{2,6},{6,10},{... | collective-permute-start | bytes 786440 | tf_op jit(solution)/shard_map/ppermute | solution.py:224
  104.4 0.0 all-to-all-done.came
  104.4 0.8 shard_map.89
  105.2 4.6 %all-to-all-start.1 = ((bf16[4,32,1024]{2,1,0:T(8,128)(2,1)}), bf16[4,32,1024]{2,1,0:T(8,128)(2,1)S(1)}, u32[]{:S(2)}, u32[]{:S(2)}) async-start(bf16[4,32,1024]{2,1,0:T(8,128)(2,1)} %bitcast.15), calls=%async_computation.1 | async-start | bytes 524288 | tf_op jit(solution)/shard_map/all_to_all | solution.py:323
  109.9 0.0 collective-permute-done.5
  109.9 1.0 collective-permute-done.6
  110.9 1.6 %collective-permute-done.7 = bf16[128,1024]{1,0:T(8,128)(2,1)S(1)} collective-permute-done((bf16[128,1024]{1,0:T(8,128)(2,1)S(1)}, bf16[128,1024]{1,0:T(8,128)(2,1)S(1)}, u32[]{:S(2)}, u32[]{:S(2)}) %collective-permute-start.7) | collective-permute-done | bytes 262176 | tf_op jit(solution)/shard_map/ppermute | solution.py:224
  112.5 0.0 copy-start.1
  112.6 0.0 copy-start.2
  112.6 16.2 %all-to-all-done.1 = bf16[4,32,1024]{2,1,0:T(8,128)(2,1)S(1)} async-done(((bf16[4,32,1024]{2,1,0:T(8,128)(2,1)}), bf16[4,32,1024]{2,1,0:T(8,128)(2,1)S(1)}, u32[]{:S(2)}, u32[]{:S(2)}) %all-to-all-start.1) | async-done | bytes 262176 | tf_op jit(solution)/shard_map/all_to_all | solution.py:323
  128.8 0.7 fusion.8
  129.5 0.0 copy-done.1
  129.5 0.0 copy-done.2
  (9 shorter events, 0.2 us)
Async XLA Ops:
  44.2 1.0 copy-start
  48.7 7.1 %collective-permute-start = (f32[3,512]{1,0:T(4,128)S(1)}, f32[3,512]{1,0:T(4,128)S(1)}, u32[]{:S(2)}, u32[]{:S(2)}) collective-permute-start(f32[3,512]{1,0:T(4,128)S(1)} %get-tuple-element.14.stats), channel_id=1, source_target_pairs={{0,4},{4,8},{8,12},{12,0},{1,5},{5,9},{9,13},{13,1},{2,6},{6,10},{... | collective-permute-start | bytes 18440 | tf_op jit(solution)/shard_map/ppermute | solution.py:224
  52.2 5.5 %collective-permute-start.1 = (f32[3,512]{1,0:T(4,128)S(1)}, f32[3,512]{1,0:T(4,128)S(1)}, u32[]{:S(2)}, u32[]{:S(2)}) collective-permute-start(f32[3,512]{1,0:T(4,128)S(1)} %get-tuple-element.14.stats), channel_id=1, source_target_pairs={{0,12},{4,0},{8,4},{12,8},{1,13},{5,1},{9,5},{13,9},{2,14},{6,2},{... | collective-permute-start | bytes 18440 | tf_op jit(solution)/shard_map/ppermute | solution.py:224
  61.7 5.3 %collective-permute-start.8 = (bf16[512,1024]{1,0:T(8,128)(2,1)}, bf16[512,1024]{1,0:T(8,128)(2,1)S(1)}, u32[]{:S(2)}, u32[]{:S(2)}) collective-permute-start(bf16[512,1024]{1,0:T(8,128)(2,1)} %get-tuple-element.23), channel_id=1, source_target_pairs={{0,16},{16,0},{32,48},{48,32},{64,80},{80,64},{96,112},{112,96},{1... | collective-permute-start | bytes 3145736 | tf_op jit(solution)/shard_map/ppermute | solution.py:287
  68.1 36.2 %all-to-all-start = ((bf16[4,128,1024]{2,1,0:T(8,128)(2,1)}), bf16[4,128,1024]{2,1,0:T(8,128)(2,1)S(1)}, u32[]{:S(2)}, u32[]{:S(2)}) async-start(bf16[4,128,1024]{2,1,0:T(8,128)(2,1)} %bitcast.44), calls=%async_computation | async-start | bytes 2097152 | tf_op jit(solution)/shard_map/all_to_all | solution.py:295
  75.4 12.8 %collective-permute-start.2 = (bf16[128,1024]{1,0:T(8,128)(2,1)}, bf16[128,1024]{1,0:T(8,128)(2,1)S(1)}, u32[]{:S(2)}, u32[]{:S(2)}) collective-permute-start(bf16[128,1024]{1,0:T(8,128)(2,1)} %get-tuple-element.19), channel_id=1, source_target_pairs={{0,8},{4,12},{8,0},{12,4},{1,9},{5,13},{9,1},{13,5},{2,10},{6,14},... | collective-permute-start | bytes 786440 | tf_op jit(solution)/shard_map/ppermute | solution.py:224
  80.2 13.2 %collective-permute-start.3 = (bf16[128,1024]{1,0:T(8,128)(2,1)}, bf16[128,1024]{1,0:T(8,128)(2,1)S(1)}, u32[]{:S(2)}, u32[]{:S(2)}) collective-permute-start(bf16[128,1024]{1,0:T(8,128)(2,1)} %get-tuple-element.20), channel_id=1, source_target_pairs={{0,4},{4,8},{8,12},{12,0},{1,5},{5,9},{9,13},{13,1},{2,6},{6,10},{... | collective-permute-start | bytes 786440 | tf_op jit(solution)/shard_map/ppermute | solution.py:224
  83.0 10.7 %collective-permute-start.4 = (bf16[128,1024]{1,0:T(8,128)(2,1)}, bf16[128,1024]{1,0:T(8,128)(2,1)S(1)}, u32[]{:S(2)}, u32[]{:S(2)}) collective-permute-start(bf16[128,1024]{1,0:T(8,128)(2,1)} %get-tuple-element.21), channel_id=1, source_target_pairs={{0,12},{4,0},{8,4},{12,8},{1,13},{5,1},{9,5},{13,9},{2,14},{6,2},{... | collective-permute-start | bytes 786440 | tf_op jit(solution)/shard_map/ppermute | solution.py:224
  93.8 16.0 %collective-permute-start.5 = (bf16[128,1024]{1,0:T(8,128)(2,1)S(1)}, bf16[128,1024]{1,0:T(8,128)(2,1)S(1)}, u32[]{:S(2)}, u32[]{:S(2)}) collective-permute-start(bf16[128,1024]{1,0:T(8,128)(2,1)S(1)} %add_convert_fusion), channel_id=1, source_target_pairs={{0,8},{4,12},{8,0},{12,4},{1,9},{5,13},{9,1},{13,5},{2,10},{6,14},... | collective-permute-start | bytes 786440 | tf_op jit(solution)/shard_map/ppermute | solution.py:224
  98.5 12.4 %collective-permute-start.6 = (bf16[128,1024]{1,0:T(8,128)(2,1)S(1)}, bf16[128,1024]{1,0:T(8,128)(2,1)S(1)}, u32[]{:S(2)}, u32[]{:S(2)}) collective-permute-start(bf16[128,1024]{1,0:T(8,128)(2,1)S(1)} %add_convert_fusion), channel_id=1, source_target_pairs={{0,12},{4,0},{8,4},{12,8},{1,13},{5,1},{9,5},{13,9},{2,14},{6,2},{... | collective-permute-start | bytes 786440 | tf_op jit(solution)/shard_map/ppermute | solution.py:224
  101.7 10.8 %collective-permute-start.7 = (bf16[128,1024]{1,0:T(8,128)(2,1)S(1)}, bf16[128,1024]{1,0:T(8,128)(2,1)S(1)}, u32[]{:S(2)}, u32[]{:S(2)}) collective-permute-start(bf16[128,1024]{1,0:T(8,128)(2,1)S(1)} %add_convert_fusion), channel_id=1, source_target_pairs={{0,4},{4,8},{8,12},{12,0},{1,5},{5,9},{9,13},{13,1},{2,6},{6,10},{... | collective-permute-start | bytes 786440 | tf_op jit(solution)/shard_map/ppermute | solution.py:224
  105.2 23.6 %all-to-all-start.1 = ((bf16[4,32,1024]{2,1,0:T(8,128)(2,1)}), bf16[4,32,1024]{2,1,0:T(8,128)(2,1)S(1)}, u32[]{:S(2)}, u32[]{:S(2)}) async-start(bf16[4,32,1024]{2,1,0:T(8,128)(2,1)} %bitcast.15), calls=%async_computation.1 | async-start | bytes 524288 | tf_op jit(solution)/shard_map/all_to_all | solution.py:323
  112.5 16.9 %copy-start.1 = (bf16[4,128,512]{2,1,0:T(8,128)(2,1)}, bf16[4,128,512]{2,1,0:T(8,128)(2,1)S(1)}, u32[]{:S(2)}) copy-start(bf16[4,128,512]{2,1,0:T(8,128)(2,1)S(1)} %get-tuple-element.24) | copy-start | bytes 1572868
  112.6 16.9 %copy-start.2 = (bf16[4,128,512]{2,1,0:T(8,128)(2,1)}, bf16[4,128,512]{2,1,0:T(8,128)(2,1)S(1)}, u32[]{:S(2)}) copy-start(bf16[4,128,512]{2,1,0:T(8,128)(2,1)S(1)} %get-tuple-element.25) | copy-start | bytes 1572868

commit v9 on v8

--- a/solution.py
+++ b/solution.py
@@ -198,7 +198,7 @@
         query += lax.dot_general(low[i], right, TN, preferred_element_type=F32)
     gathered[:, :width] = (query * width ** (-0.5)).astype(BF16)
     for d, part in enumerate(parts):
-        at = ((place[0] + d) & 3) * quarter
+        at = (place[0] ^ d) * quarter
         part[...] = gathered[pl.ds(pl.multiple_of(at, quarter), quarter), :]
 
 
@@ -219,9 +219,8 @@
     out[...] = f32_sum([came[j] for j in range(came.shape[0])]).astype(BF16)
 
 
-def shifted(value, axis, d):
-    n = lax.axis_size(axis)
-    return lax.ppermute(value, axis, [(i, (i + d) % n) for i in range(n)])
+def swapped(value, d):
+    return lax.ppermute(value, "phon", [(i, i ^ d) for i in range(lax.axis_size("phon"))])
 
 
 def f32_sum(parts):
@@ -263,7 +262,7 @@
         ],
         2 * work,
     )
-    heard = [(stats, VMEM), (shifted(stats, "phon", 1), VMEM), (shifted(stats, "phon", 3), VMEM)]
+    heard = [(stats, VMEM), (swapped(stats, 1), VMEM), (swapped(stats, 3), VMEM)]
 
     def backward(side, space=HBM):
         return call(
@@ -317,7 +316,7 @@
         ],
         work,
     )
-    moved = [parts[0]] + [shifted(parts[d], "phon", d) for d in (2, 1, 3)]
+    moved = [parts[0]] + [swapped(parts[d], d) for d in (2, 1, 3)]
 
     (second,) = call(sum_kernel, [((half // 4, 2 * width), BF16, VMEM)], [(first, VMEM)])
     second = lax.all_to_all(
@@ -325,12 +324,12 @@
         axis_index_groups=CROSSES,
     )
     mine = f32_sum(moved).astype(BF16)
-    spread = [mine] + [shifted(mine, "phon", d) for d in (2, 3, 1)]
+    spread = [mine] + [swapped(mine, d) for d in (2, 3, 1)]
 
     def placed(parts):
         whole = jnp.zeros((ranks, quarter, width), BF16)
         for d, p in zip((0, 2, 3, 1), parts):
-            whole = lax.dynamic_update_index_in_dim(whole, p, (phon - d) & 3, 0)
+            whole = lax.dynamic_update_index_in_dim(whole, p, phon ^ d, 0)
         return whole.reshape(rows, width)
 
     grad_query = placed([m[:, :width] for m in spread])

time: 130 us -> 129 us (level)
  starting transfers between devices: 39.4 us -> 37.4 us
    ppermute x8, starting transfers between devices: 29.4 us -> 26.6 us  [swapped(): lax.ppermute(value, 'phon', [(i, i ^ d) for i in range(lax.axis_size('pho...]
  transfers between devices with their start and end apart: 11 -> 11, of which waited for: 7 -> 6; matrix products, arithmetic and copies ran while one was open for 0% -> 0% of each run, Pallas kernels for 6% -> 6%
where the time goes in v9:
time: 129 us
  blocking collectives  42.1 us (33%)
  starting transfers between devices  37.4 us (29%)
  waiting for transfers between devices  28.2 us (22%)
  Pallas kernels  16.3 us (13%)
  other arithmetic  1.67 us (1%)
  between operations  1.56 us (1%)
    all_gather x1, blocking collectives, step(): lax.all_gather(both.astype(jnp.float16), 'frames', axis=0, tiled=True)  42.1 us
    ppermute x8, starting transfers between devices, swapped(): lax.ppermute(value, 'phon', [(i, i ^ d) for i in range(lax.axis_size('pho...  26.6 us
    pallas_call x6, Pallas kernels, call(): pl.pallas_call(kernel, out_shape=shapes, in_specs=[pl.BlockSpec(memory_sp...  16.3 us
    all_to_all x1, waiting for transfers between devices, step(): lax.all_to_all(second.reshape(4, own, 2 * width), 'frames', 0, 0, tiled=T...  16.1 us
    ppermute x8, waiting for transfers between devices, swapped(): lax.ppermute(value, 'phon', [(i, i ^ d) for i in range(lax.axis_size('pho...  12 us
    all_to_all x1, starting transfers between devices, step(): lax.all_to_all(second.reshape(4, own, 2 * width), 'frames', 0, 0, tiled=T...  5.36 us
    all_to_all x1, starting transfers between devices, step(): lax.all_to_all(first.reshape(4, half // 4, 2 * width), 'frames', 0, 0, ti...  3.53 us
  transfers between devices with their start and end apart: 11, of which 6 were waited for; matrix products, arithmetic and copies ran while one was open for 0% of the time, Pallas kernels for 6%

profile of v9, /device:TPU:6, one launch (start us, length us, event | category | flops | bytes accessed | tf_op | source)
XLA Modules:
  0.0 128.5 jit_solution(13877691363576100436)
XLA Ops:
  1.3 0.8 multiply_convert_fusion.1
  2.1 42.1 %all-gather.1 = f16[1024,1024]{1,0:T(8,128)(2,1)S(1)} all-gather(f16[32,1024]{1,0:T(8,128)(2,1)S(1)} %multiply_convert_fusion.1), channel_id=1, replica_groups=mesh['frames'=32,'phon'=4,'chap'=4] {'frames'}, dimensions={0}, use_global_device_ids=true | all-gather | bytes 2162688 | tf_op jit(solution)/shard_map/all_gather | solution.py:247
  44.2 0.0 copy-start
  44.2 0.6 multiply_convert_fusion.every
  44.8 0.4 copy-done
  45.3 3.4 %shard_map.84 = (bf16[512,512]{1,0:T(8,128)(2,1)}, f32[3,512]{1,0:T(4,128)S(1)}) custom-call(s32[2]{0:T(128)S(1)} %and_convert_fusion.flags, bf16[1024,1024]{1,0:T(8,128)(2,1)S(1)} %multiply_convert_fusion.every, bf16[512,512]{1,0:T(8,128)(2,1)S(1)} %copy-done, bf16[512,512]{1,0:T(8,128)(2,1)} %cotangent_far.5), custom_call_target="tpu_custom_call" | custom-call | flops 1073741824 | bytes 3676168 | tf_op jit(solution)/shard_map/pallas_call | solution.py:40
  48.7 3.5 %collective-permute-start = (f32[3,512]{1,0:T(4,128)S(1)}, f32[3,512]{1,0:T(4,128)S(1)}, u32[]{:S(2)}, u32[]{:S(2)}) collective-permute-start(f32[3,512]{1,0:T(4,128)S(1)} %get-tuple-element.14.stats), channel_id=1, source_target_pairs={{0,4},{4,0},{8,12},{12,8},{1,5},{5,1},{9,13},{13,9},{2,6},{6,2},{1... | collective-permute-start | bytes 18440 | tf_op jit(solution)/shard_map/ppermute | solution.py:223
  52.2 4.1 %collective-permute-start.1 = (f32[3,512]{1,0:T(4,128)S(1)}, f32[3,512]{1,0:T(4,128)S(1)}, u32[]{:S(2)}, u32[]{:S(2)}) collective-permute-start(f32[3,512]{1,0:T(4,128)S(1)} %get-tuple-element.14.stats), channel_id=1, source_target_pairs={{0,12},{4,8},{8,4},{12,0},{1,13},{5,9},{9,5},{13,1},{2,14},{6,10},... | collective-permute-start | bytes 18440 | tf_op jit(solution)/shard_map/ppermute | solution.py:223
  56.3 0.0 collective-permute-done.stats_up
  56.3 2.6 %collective-permute-done.1.stats_down = f32[3,512]{1,0:T(4,128)S(1)} collective-permute-done((f32[3,512]{1,0:T(4,128)S(1)}, f32[3,512]{1,0:T(4,128)S(1)}, u32[]{:S(2)}, u32[]{:S(2)}) %collective-permute-start.1) | collective-permute-done | bytes 6176 | tf_op jit(solution)/shard_map/ppermute | solution.py:223
  58.9 4.0 %shard_map.86 = (bf16[512,1024]{1,0:T(8,128)(2,1)}, bf16[512,512]{1,0:T(8,128)(2,1)}) custom-call(s32[1]{0:T(128)} %bitcast.3.side, s32[2]{0:T(128)S(1)} %and_convert_fusion.flags, f32[3,512]{1,0:T(4,128)S(1)} %get-tuple-element.14.stats, f32[3,512]{1,0:T(4,128)S(1)} %collective-permute-done.stats_up, f32[3,512]{1,0:T(4,128)S(1)} %collective-permute-done.1.stats_down, ...), custom_call_target="tpu_custom_call" | custom-call | flops 1073741824 | bytes 4737036 | tf_op jit(solution)/shard_map/pallas_call | solution.py:40
  63.0 1.9 %collective-permute-start.8 = (bf16[512,1024]{1,0:T(8,128)(2,1)}, bf16[512,1024]{1,0:T(8,128)(2,1)S(1)}, u32[]{:S(2)}, u32[]{:S(2)}) collective-permute-start(bf16[512,1024]{1,0:T(8,128)(2,1)} %get-tuple-element.23), channel_id=1, source_target_pairs={{0,16},{16,0},{32,48},{48,32},{64,80},{80,64},{96,112},{112,96},{1... | collective-permute-start | bytes 3145736 | tf_op jit(solution)/shard_map/ppermute | solution.py:286
  64.9 3.4 %shard_map.85 = (bf16[512,1024]{1,0:T(8,128)(2,1)S(1)}, bf16[512,512]{1,0:T(8,128)(2,1)}) custom-call(s32[1]{0:T(128)} %bitcast.1.side, s32[2]{0:T(128)S(1)} %and_convert_fusion.flags, f32[3,512]{1,0:T(4,128)S(1)} %get-tuple-element.14.stats, f32[3,512]{1,0:T(4,128)S(1)} %collective-permute-done.stats_up, f32[3,512]{1,0:T(4,128)S(1)} %collective-permute-done.1.stats_down, ...), custom_call_target="tpu_custom_call" | custom-call | flops 1073741824 | bytes 4737036 | tf_op jit(solution)/shard_map/pallas_call | solution.py:40
  68.2 0.0 collective-permute-done.8.came
  68.3 1.1 shard_map.88
  69.4 3.5 %all-to-all-start = ((bf16[4,128,1024]{2,1,0:T(8,128)(2,1)}), bf16[4,128,1024]{2,1,0:T(8,128)(2,1)S(1)}, u32[]{:S(2)}, u32[]{:S(2)}) async-start(bf16[4,128,1024]{2,1,0:T(8,128)(2,1)} %bitcast.44), calls=%async_computation | async-start | bytes 2097152 | tf_op jit(solution)/shard_map/all_to_all | solution.py:294
  72.9 0.1 pad_add_fusion.place
  73.0 3.6 %shard_map.87 = (bf16[128,1024]{1,0:T(8,128)(2,1)S(1)}, bf16[128,1024]{1,0:T(8,128)(2,1)}, bf16[128,1024]{1,0:T(8,128)(2,1)}, bf16[128,1024]{1,0:T(8,128)(2,1)}) custom-call(s32[2]{0:T(128)S(1)} %pad_add_fusion.place, f32[3,512]{1,0:T(4,128)S(1)} %get-tuple-element.14.stats, f32[3,512]{1,0:T(4,128)S(1)} %collective-permute-done.stats_up, ...), custom_call_target="tpu_custom_call" | custom-call | flops 536870912 | bytes 4737032 | tf_op jit(solution)/shard_map/pallas_call | solution.py:40
  76.6 3.6 %collective-permute-start.2 = (bf16[128,1024]{1,0:T(8,128)(2,1)}, bf16[128,1024]{1,0:T(8,128)(2,1)S(1)}, u32[]{:S(2)}, u32[]{:S(2)}) collective-permute-start(bf16[128,1024]{1,0:T(8,128)(2,1)} %get-tuple-element.19), channel_id=1, source_target_pairs={{0,8},{4,12},{8,0},{12,4},{1,9},{5,13},{9,1},{13,5},{2,10},{6,14},... | collective-permute-start | bytes 786440 | tf_op jit(solution)/shard_map/ppermute | solution.py:223
  80.2 3.3 %collective-permute-start.3 = (bf16[128,1024]{1,0:T(8,128)(2,1)}, bf16[128,1024]{1,0:T(8,128)(2,1)S(1)}, u32[]{:S(2)}, u32[]{:S(2)}) collective-permute-start(bf16[128,1024]{1,0:T(8,128)(2,1)} %get-tuple-element.20), channel_id=1, source_target_pairs={{0,4},{4,0},{8,12},{12,8},{1,5},{5,1},{9,13},{13,9},{2,6},{6,2},{1... | collective-permute-start | bytes 786440 | tf_op jit(solution)/shard_map/ppermute | solution.py:223
  83.4 3.0 %collective-permute-start.4 = (bf16[128,1024]{1,0:T(8,128)(2,1)}, bf16[128,1024]{1,0:T(8,128)(2,1)S(1)}, u32[]{:S(2)}, u32[]{:S(2)}) collective-permute-start(bf16[128,1024]{1,0:T(8,128)(2,1)} %get-tuple-element.21), channel_id=1, source_target_pairs={{0,12},{4,8},{8,4},{12,0},{1,13},{5,9},{9,5},{13,1},{2,14},{6,10},... | collective-permute-start | bytes 786440 | tf_op jit(solution)/shard_map/ppermute | solution.py:223
  86.4 2.9 %collective-permute-done.2 = bf16[128,1024]{1,0:T(8,128)(2,1)S(1)} collective-permute-done((bf16[128,1024]{1,0:T(8,128)(2,1)}, bf16[128,1024]{1,0:T(8,128)(2,1)S(1)}, u32[]{:S(2)}, u32[]{:S(2)}) %collective-permute-start.2) | collective-permute-done | bytes 262176 | tf_op jit(solution)/shard_map/ppermute | solution.py:223
  89.4 4.8 %collective-permute-done.3 = bf16[128,1024]{1,0:T(8,128)(2,1)S(1)} collective-permute-done((bf16[128,1024]{1,0:T(8,128)(2,1)}, bf16[128,1024]{1,0:T(8,128)(2,1)S(1)}, u32[]{:S(2)}, u32[]{:S(2)}) %collective-permute-start.3) | collective-permute-done | bytes 262176 | tf_op jit(solution)/shard_map/ppermute | solution.py:223
  94.1 0.9 collective-permute-done.4
  95.0 0.2 add_convert_fusion
  95.2 3.2 %collective-permute-start.5 = (bf16[128,1024]{1,0:T(8,128)(2,1)S(1)}, bf16[128,1024]{1,0:T(8,128)(2,1)S(1)}, u32[]{:S(2)}, u32[]{:S(2)}) collective-permute-start(bf16[128,1024]{1,0:T(8,128)(2,1)S(1)} %add_convert_fusion), channel_id=1, source_target_pairs={{0,8},{4,12},{8,0},{12,4},{1,9},{5,13},{9,1},{13,5},{2,10},{6,14},... | collective-permute-start | bytes 786440 | tf_op jit(solution)/shard_map/ppermute | solution.py:223
  98.4 3.1 %collective-permute-start.6 = (bf16[128,1024]{1,0:T(8,128)(2,1)S(1)}, bf16[128,1024]{1,0:T(8,128)(2,1)S(1)}, u32[]{:S(2)}, u32[]{:S(2)}) collective-permute-start(bf16[128,1024]{1,0:T(8,128)(2,1)S(1)} %add_convert_fusion), channel_id=1, source_target_pairs={{0,12},{4,8},{8,4},{12,0},{1,13},{5,9},{9,5},{13,1},{2,14},{6,10},... | collective-permute-start | bytes 786440 | tf_op jit(solution)/shard_map/ppermute | solution.py:223
  101.5 2.9 %collective-permute-start.7 = (bf16[128,1024]{1,0:T(8,128)(2,1)S(1)}, bf16[128,1024]{1,0:T(8,128)(2,1)S(1)}, u32[]{:S(2)}, u32[]{:S(2)}) collective-permute-start(bf16[128,1024]{1,0:T(8,128)(2,1)S(1)} %add_convert_fusion), channel_id=1, source_target_pairs={{0,4},{4,0},{8,12},{12,8},{1,5},{5,1},{9,13},{13,9},{2,6},{6,2},{1... | collective-permute-start | bytes 786440 | tf_op jit(solution)/shard_map/ppermute | solution.py:223
  104.5 0.0 all-to-all-done.came
  104.5 0.8 shard_map.89
  105.3 5.4 %all-to-all-start.1 = ((bf16[4,32,1024]{2,1,0:T(8,128)(2,1)}), bf16[4,32,1024]{2,1,0:T(8,128)(2,1)S(1)}, u32[]{:S(2)}, u32[]{:S(2)}) async-start(bf16[4,32,1024]{2,1,0:T(8,128)(2,1)} %bitcast.15), calls=%async_computation.1 | async-start | bytes 524288 | tf_op jit(solution)/shard_map/all_to_all | solution.py:322
  110.8 0.0 collective-permute-done.5
  110.8 0.8 collective-permute-done.6
  111.6 0.0 collective-permute-done.7
  111.7 0.0 copy-start.1
  111.7 0.0 copy-start.2
  111.7 16.1 %all-to-all-done.1 = bf16[4,32,1024]{2,1,0:T(8,128)(2,1)S(1)} async-done(((bf16[4,32,1024]{2,1,0:T(8,128)(2,1)}), bf16[4,32,1024]{2,1,0:T(8,128)(2,1)S(1)}, u32[]{:S(2)}, u32[]{:S(2)}) %all-to-all-start.1) | async-done | bytes 262176 | tf_op jit(solution)/shard_map/all_to_all | solution.py:322
  127.9 0.7 fusion.8
  128.5 0.0 copy-done.1
  128.5 0.0 copy-done.2
  (9 shorter events, 0.2 us)
Async XLA Ops:
  44.2 1.0 copy-start
  48.7 7.6 %collective-permute-start = (f32[3,512]{1,0:T(4,128)S(1)}, f32[3,512]{1,0:T(4,128)S(1)}, u32[]{:S(2)}, u32[]{:S(2)}) collective-permute-start(f32[3,512]{1,0:T(4,128)S(1)} %get-tuple-element.14.stats), channel_id=1, source_target_pairs={{0,4},{4,0},{8,12},{12,8},{1,5},{5,1},{9,13},{13,9},{2,6},{6,2},{1... | collective-permute-start | bytes 18440 | tf_op jit(solution)/shard_map/ppermute | solution.py:223
  52.2 6.8 %collective-permute-start.1 = (f32[3,512]{1,0:T(4,128)S(1)}, f32[3,512]{1,0:T(4,128)S(1)}, u32[]{:S(2)}, u32[]{:S(2)}) collective-permute-start(f32[3,512]{1,0:T(4,128)S(1)} %get-tuple-element.14.stats), channel_id=1, source_target_pairs={{0,12},{4,8},{8,4},{12,0},{1,13},{5,9},{9,5},{13,1},{2,14},{6,10},... | collective-permute-start | bytes 18440 | tf_op jit(solution)/shard_map/ppermute | solution.py:223
  63.0 5.3 %collective-permute-start.8 = (bf16[512,1024]{1,0:T(8,128)(2,1)}, bf16[512,1024]{1,0:T(8,128)(2,1)S(1)}, u32[]{:S(2)}, u32[]{:S(2)}) collective-permute-start(bf16[512,1024]{1,0:T(8,128)(2,1)} %get-tuple-element.23), channel_id=1, source_target_pairs={{0,16},{16,0},{32,48},{48,32},{64,80},{80,64},{96,112},{112,96},{1... | collective-permute-start | bytes 3145736 | tf_op jit(solution)/shard_map/ppermute | solution.py:286
  69.4 35.1 %all-to-all-start = ((bf16[4,128,1024]{2,1,0:T(8,128)(2,1)}), bf16[4,128,1024]{2,1,0:T(8,128)(2,1)S(1)}, u32[]{:S(2)}, u32[]{:S(2)}) async-start(bf16[4,128,1024]{2,1,0:T(8,128)(2,1)} %bitcast.44), calls=%async_computation | async-start | bytes 2097152 | tf_op jit(solution)/shard_map/all_to_all | solution.py:294
  76.6 12.8 %collective-permute-start.2 = (bf16[128,1024]{1,0:T(8,128)(2,1)}, bf16[128,1024]{1,0:T(8,128)(2,1)S(1)}, u32[]{:S(2)}, u32[]{:S(2)}) collective-permute-start(bf16[128,1024]{1,0:T(8,128)(2,1)} %get-tuple-element.19), channel_id=1, source_target_pairs={{0,8},{4,12},{8,0},{12,4},{1,9},{5,13},{9,1},{13,5},{2,10},{6,14},... | collective-permute-start | bytes 786440 | tf_op jit(solution)/shard_map/ppermute | solution.py:223
  80.2 14.0 %collective-permute-start.3 = (bf16[128,1024]{1,0:T(8,128)(2,1)}, bf16[128,1024]{1,0:T(8,128)(2,1)S(1)}, u32[]{:S(2)}, u32[]{:S(2)}) collective-permute-start(bf16[128,1024]{1,0:T(8,128)(2,1)} %get-tuple-element.20), channel_id=1, source_target_pairs={{0,4},{4,0},{8,12},{12,8},{1,5},{5,1},{9,13},{13,9},{2,6},{6,2},{1... | collective-permute-start | bytes 786440 | tf_op jit(solution)/shard_map/ppermute | solution.py:223
  83.4 11.6 %collective-permute-start.4 = (bf16[128,1024]{1,0:T(8,128)(2,1)}, bf16[128,1024]{1,0:T(8,128)(2,1)S(1)}, u32[]{:S(2)}, u32[]{:S(2)}) collective-permute-start(bf16[128,1024]{1,0:T(8,128)(2,1)} %get-tuple-element.21), channel_id=1, source_target_pairs={{0,12},{4,8},{8,4},{12,0},{1,13},{5,9},{9,5},{13,1},{2,14},{6,10},... | collective-permute-start | bytes 786440 | tf_op jit(solution)/shard_map/ppermute | solution.py:223
  95.2 15.6 %collective-permute-start.5 = (bf16[128,1024]{1,0:T(8,128)(2,1)S(1)}, bf16[128,1024]{1,0:T(8,128)(2,1)S(1)}, u32[]{:S(2)}, u32[]{:S(2)}) collective-permute-start(bf16[128,1024]{1,0:T(8,128)(2,1)S(1)} %add_convert_fusion), channel_id=1, source_target_pairs={{0,8},{4,12},{8,0},{12,4},{1,9},{5,13},{9,1},{13,5},{2,10},{6,14},... | collective-permute-start | bytes 786440 | tf_op jit(solution)/shard_map/ppermute | solution.py:223
  98.4 13.2 %collective-permute-start.6 = (bf16[128,1024]{1,0:T(8,128)(2,1)S(1)}, bf16[128,1024]{1,0:T(8,128)(2,1)S(1)}, u32[]{:S(2)}, u32[]{:S(2)}) collective-permute-start(bf16[128,1024]{1,0:T(8,128)(2,1)S(1)} %add_convert_fusion), channel_id=1, source_target_pairs={{0,12},{4,8},{8,4},{12,0},{1,13},{5,9},{9,5},{13,1},{2,14},{6,10},... | collective-permute-start | bytes 786440 | tf_op jit(solution)/shard_map/ppermute | solution.py:223
  101.5 10.2 %collective-permute-start.7 = (bf16[128,1024]{1,0:T(8,128)(2,1)S(1)}, bf16[128,1024]{1,0:T(8,128)(2,1)S(1)}, u32[]{:S(2)}, u32[]{:S(2)}) collective-permute-start(bf16[128,1024]{1,0:T(8,128)(2,1)S(1)} %add_convert_fusion), channel_id=1, source_target_pairs={{0,4},{4,0},{8,12},{12,8},{1,5},{5,1},{9,13},{13,9},{2,6},{6,2},{1... | collective-permute-start | bytes 786440 | tf_op jit(solution)/shard_map/ppermute | solution.py:223
  105.3 22.5 %all-to-all-start.1 = ((bf16[4,32,1024]{2,1,0:T(8,128)(2,1)}), bf16[4,32,1024]{2,1,0:T(8,128)(2,1)S(1)}, u32[]{:S(2)}, u32[]{:S(2)}) async-start(bf16[4,32,1024]{2,1,0:T(8,128)(2,1)} %bitcast.15), calls=%async_computation.1 | async-start | bytes 524288 | tf_op jit(solution)/shard_map/all_to_all | solution.py:322
  111.7 16.9 %copy-start.1 = (bf16[4,128,512]{2,1,0:T(8,128)(2,1)}, bf16[4,128,512]{2,1,0:T(8,128)(2,1)S(1)}, u32[]{:S(2)}) copy-start(bf16[4,128,512]{2,1,0:T(8,128)(2,1)S(1)} %get-tuple-element.24) | copy-start | bytes 1572868
  111.7 16.9 %copy-start.2 = (bf16[4,128,512]{2,1,0:T(8,128)(2,1)}, bf16[4,128,512]{2,1,0:T(8,128)(2,1)S(1)}, u32[]{:S(2)}) copy-start(bf16[4,128,512]{2,1,0:T(8,128)(2,1)S(1)} %get-tuple-element.25) | copy-start | bytes 1572868

commit v10 on v9

--- a/solution.py
+++ b/solution.py
@@ -262,7 +262,12 @@
         ],
         2 * work,
     )
-    heard = [(stats, VMEM), (swapped(stats, 1), VMEM), (swapped(stats, 3), VMEM)]
+    n_phon = lax.axis_size("phon")
+    passed = [
+        lax.ppermute(stats, "phon", [(i, (i + d) % n_phon) for i in range(n_phon)])
+        for d in (1, n_phon - 1)
+    ]
+    heard = [(stats, VMEM)] + [(p, VMEM) for p in passed]
 
     def backward(side, space=HBM):
         return call(

time: 129 us -> 129 us (level)
    ppermute x8 -> x6, starting transfers between devices: 26.6 us -> 19.2 us  [swapped(): lax.ppermute(value, 'phon', [(i, i ^ d) for i in range(lax.axis_size('pho...]
    ppermute x0 -> x2, starting transfers between devices: none -> 7.05 us  [step(): lax.ppermute(stats, 'phon', [(i, (i + d) % n_phon) for i in range(n_phon)])]
    ppermute x0 -> x2, waiting for transfers between devices: none -> 1.95 us  [step(): lax.ppermute(stats, 'phon', [(i, (i + d) % n_phon) for i in range(n_phon)])]
    ppermute x8 -> x6, waiting for transfers between devices: 12 us -> 10.1 us  [swapped(): lax.ppermute(value, 'phon', [(i, i ^ d) for i in range(lax.axis_size('pho...]
where the time goes in v10:
time: 129 us; the launch traced here: 128 us
  blocking collectives  42.1 us (33%)
  starting transfers between devices  36.9 us (29%)
  waiting for transfers between devices  28.7 us (22%)
  Pallas kernels  16.3 us (13%)
  other arithmetic  1.67 us (1%)
  between operations  1.56 us (1%)
    all_gather x1, blocking collectives, step(): lax.all_gather(both.astype(jnp.float16), 'frames', axis=0, tiled=True)  42.1 us
    ppermute x6, starting transfers between devices, swapped(): lax.ppermute(value, 'phon', [(i, i ^ d) for i in range(lax.axis_size('pho...  19.2 us
    all_to_all x1, waiting for transfers between devices, step(): lax.all_to_all(second.reshape(4, own, 2 * width), 'frames', 0, 0, tiled=T...  16.6 us
    pallas_call x6, Pallas kernels, call(): pl.pallas_call(kernel, out_shape=shapes, in_specs=[pl.BlockSpec(memory_sp...  16.3 us
    ppermute x6, waiting for transfers between devices, swapped(): lax.ppermute(value, 'phon', [(i, i ^ d) for i in range(lax.axis_size('pho...  10.1 us
    ppermute x2, starting transfers between devices, step(): lax.ppermute(stats, 'phon', [(i, (i + d) % n_phon) for i in range(n_phon)])  7.05 us
    all_to_all x1, starting transfers between devices, step(): lax.all_to_all(second.reshape(4, own, 2 * width), 'frames', 0, 0, tiled=T...  5.18 us
    all_to_all x1, starting transfers between devices, step(): lax.all_to_all(first.reshape(4, half // 4, 2 * width), 'frames', 0, 0, ti...  3.53 us
  transfers between devices with their start and end apart: 11, of which 6 were waited for; matrix products, arithmetic and copies ran while one was open for 0% of the time, Pallas kernels for 6%

profile of v10, /device:TPU:6, one launch (start us, length us, event | category | flops | bytes accessed | tf_op | source)
XLA Modules:
  0.0 128.5 jit_solution(17251499679472860331)
XLA Ops:
  1.3 0.8 multiply_convert_fusion.1
  2.1 42.1 %all-gather.1 = f16[1024,1024]{1,0:T(8,128)(2,1)S(1)} all-gather(f16[32,1024]{1,0:T(8,128)(2,1)S(1)} %multiply_convert_fusion.1), channel_id=1, replica_groups=mesh['frames'=32,'phon'=4,'chap'=4] {'frames'}, dimensions={0}, use_global_device_ids=true | all-gather | bytes 2162688 | tf_op jit(solution)/shard_map/all_gather | solution.py:247
  44.2 0.0 copy-start
  44.2 0.6 multiply_convert_fusion.every
  44.8 0.4 copy-done
  45.3 3.4 %shard_map.84 = (bf16[512,512]{1,0:T(8,128)(2,1)}, f32[3,512]{1,0:T(4,128)S(1)}) custom-call(s32[2]{0:T(128)S(1)} %and_convert_fusion.flags, bf16[1024,1024]{1,0:T(8,128)(2,1)S(1)} %multiply_convert_fusion.every, bf16[512,512]{1,0:T(8,128)(2,1)S(1)} %copy-done, bf16[512,512]{1,0:T(8,128)(2,1)} %cotangent_far.5), custom_call_target="tpu_custom_call" | custom-call | flops 1073741824 | bytes 3676168 | tf_op jit(solution)/shard_map/pallas_call | solution.py:40
  48.7 3.5 %collective-permute-start = (f32[3,512]{1,0:T(4,128)S(1)}, f32[3,512]{1,0:T(4,128)S(1)}, u32[]{:S(2)}, u32[]{:S(2)}) collective-permute-start(f32[3,512]{1,0:T(4,128)S(1)} %get-tuple-element.14.stats), channel_id=1, source_target_pairs={{0,4},{4,8},{8,12},{12,0},{1,5},{5,9},{9,13},{13,1},{2,6},{6,10},{... | collective-permute-start | bytes 18440 | tf_op jit(solution)/shard_map/ppermute | solution.py:267
  52.2 3.6 %collective-permute-start.1 = (f32[3,512]{1,0:T(4,128)S(1)}, f32[3,512]{1,0:T(4,128)S(1)}, u32[]{:S(2)}, u32[]{:S(2)}) collective-permute-start(f32[3,512]{1,0:T(4,128)S(1)} %get-tuple-element.14.stats), channel_id=1, source_target_pairs={{0,12},{4,0},{8,4},{12,8},{1,13},{5,1},{9,5},{13,9},{2,14},{6,2},{... | collective-permute-start | bytes 18440 | tf_op jit(solution)/shard_map/ppermute | solution.py:267
  55.8 0.0 collective-permute-done.stats_up
  55.8 1.9 %collective-permute-done.1.stats_down = f32[3,512]{1,0:T(4,128)S(1)} collective-permute-done((f32[3,512]{1,0:T(4,128)S(1)}, f32[3,512]{1,0:T(4,128)S(1)}, u32[]{:S(2)}, u32[]{:S(2)}) %collective-permute-start.1) | collective-permute-done | bytes 6176 | tf_op jit(solution)/shard_map/ppermute | solution.py:267
  57.7 4.0 %shard_map.86 = (bf16[512,1024]{1,0:T(8,128)(2,1)}, bf16[512,512]{1,0:T(8,128)(2,1)}) custom-call(s32[1]{0:T(128)} %bitcast.3.side, s32[2]{0:T(128)S(1)} %and_convert_fusion.flags, f32[3,512]{1,0:T(4,128)S(1)} %get-tuple-element.14.stats, f32[3,512]{1,0:T(4,128)S(1)} %collective-permute-done.stats_up, f32[3,512]{1,0:T(4,128)S(1)} %collective-permute-done.1.stats_down, ...), custom_call_target="tpu_custom_call" | custom-call | flops 1073741824 | bytes 4737036 | tf_op jit(solution)/shard_map/pallas_call | solution.py:40
  61.7 1.9 %collective-permute-start.8 = (bf16[512,1024]{1,0:T(8,128)(2,1)}, bf16[512,1024]{1,0:T(8,128)(2,1)S(1)}, u32[]{:S(2)}, u32[]{:S(2)}) collective-permute-start(bf16[512,1024]{1,0:T(8,128)(2,1)} %get-tuple-element.23), channel_id=1, source_target_pairs={{0,16},{16,0},{32,48},{48,32},{64,80},{80,64},{96,112},{112,96},{1... | collective-permute-start | bytes 3145736 | tf_op jit(solution)/shard_map/ppermute | solution.py:291
  63.7 3.4 %shard_map.85 = (bf16[512,1024]{1,0:T(8,128)(2,1)S(1)}, bf16[512,512]{1,0:T(8,128)(2,1)}) custom-call(s32[1]{0:T(128)} %bitcast.1.side, s32[2]{0:T(128)S(1)} %and_convert_fusion.flags, f32[3,512]{1,0:T(4,128)S(1)} %get-tuple-element.14.stats, f32[3,512]{1,0:T(4,128)S(1)} %collective-permute-done.stats_up, f32[3,512]{1,0:T(4,128)S(1)} %collective-permute-done.1.stats_down, ...), custom_call_target="tpu_custom_call" | custom-call | flops 1073741824 | bytes 4737036 | tf_op jit(solution)/shard_map/pallas_call | solution.py:40
  67.0 0.0 collective-permute-done.8.came
  67.0 1.1 shard_map.88
  68.1 3.5 %all-to-all-start = ((bf16[4,128,1024]{2,1,0:T(8,128)(2,1)}), bf16[4,128,1024]{2,1,0:T(8,128)(2,1)S(1)}, u32[]{:S(2)}, u32[]{:S(2)}) async-start(bf16[4,128,1024]{2,1,0:T(8,128)(2,1)} %bitcast.44), calls=%async_computation | async-start | bytes 2097152 | tf_op jit(solution)/shard_map/all_to_all | solution.py:299
  71.7 0.1 pad_add_fusion.place
  71.8 3.6 %shard_map.87 = (bf16[128,1024]{1,0:T(8,128)(2,1)S(1)}, bf16[128,1024]{1,0:T(8,128)(2,1)}, bf16[128,1024]{1,0:T(8,128)(2,1)}, bf16[128,1024]{1,0:T(8,128)(2,1)}) custom-call(s32[2]{0:T(128)S(1)} %pad_add_fusion.place, f32[3,512]{1,0:T(4,128)S(1)} %get-tuple-element.14.stats, f32[3,512]{1,0:T(4,128)S(1)} %collective-permute-done.stats_up, ...), custom_call_target="tpu_custom_call" | custom-call | flops 536870912 | bytes 4737032 | tf_op jit(solution)/shard_map/pallas_call | solution.py:40
  75.4 4.8 %collective-permute-start.2 = (bf16[128,1024]{1,0:T(8,128)(2,1)}, bf16[128,1024]{1,0:T(8,128)(2,1)S(1)}, u32[]{:S(2)}, u32[]{:S(2)}) collective-permute-start(bf16[128,1024]{1,0:T(8,128)(2,1)} %get-tuple-element.19), channel_id=1, source_target_pairs={{0,8},{4,12},{8,0},{12,4},{1,9},{5,13},{9,1},{13,5},{2,10},{6,14},... | collective-permute-start | bytes 786440 | tf_op jit(solution)/shard_map/ppermute | solution.py:223
  80.2 2.7 %collective-permute-start.3 = (bf16[128,1024]{1,0:T(8,128)(2,1)}, bf16[128,1024]{1,0:T(8,128)(2,1)S(1)}, u32[]{:S(2)}, u32[]{:S(2)}) collective-permute-start(bf16[128,1024]{1,0:T(8,128)(2,1)} %get-tuple-element.20), channel_id=1, source_target_pairs={{0,4},{4,0},{8,12},{12,8},{1,5},{5,1},{9,13},{13,9},{2,6},{6,2},{1... | collective-permute-start | bytes 786440 | tf_op jit(solution)/shard_map/ppermute | solution.py:223
  82.9 2.4 %collective-permute-start.4 = (bf16[128,1024]{1,0:T(8,128)(2,1)}, bf16[128,1024]{1,0:T(8,128)(2,1)S(1)}, u32[]{:S(2)}, u32[]{:S(2)}) collective-permute-start(bf16[128,1024]{1,0:T(8,128)(2,1)} %get-tuple-element.21), channel_id=1, source_target_pairs={{0,12},{4,8},{8,4},{12,0},{1,13},{5,9},{9,5},{13,1},{2,14},{6,10},... | collective-permute-start | bytes 786440 | tf_op jit(solution)/shard_map/ppermute | solution.py:223
  85.4 2.8 %collective-permute-done.2 = bf16[128,1024]{1,0:T(8,128)(2,1)S(1)} collective-permute-done((bf16[128,1024]{1,0:T(8,128)(2,1)}, bf16[128,1024]{1,0:T(8,128)(2,1)S(1)}, u32[]{:S(2)}, u32[]{:S(2)}) %collective-permute-start.2) | collective-permute-done | bytes 262176 | tf_op jit(solution)/shard_map/ppermute | solution.py:223
  88.1 5.5 %collective-permute-done.3 = bf16[128,1024]{1,0:T(8,128)(2,1)S(1)} collective-permute-done((bf16[128,1024]{1,0:T(8,128)(2,1)}, bf16[128,1024]{1,0:T(8,128)(2,1)S(1)}, u32[]{:S(2)}, u32[]{:S(2)}) %collective-permute-start.3) | collective-permute-done | bytes 262176 | tf_op jit(solution)/shard_map/ppermute | solution.py:223
  93.6 0.9 collective-permute-done.4
  94.5 0.2 add_convert_fusion
  94.7 3.7 %collective-permute-start.5 = (bf16[128,1024]{1,0:T(8,128)(2,1)S(1)}, bf16[128,1024]{1,0:T(8,128)(2,1)S(1)}, u32[]{:S(2)}, u32[]{:S(2)}) collective-permute-start(bf16[128,1024]{1,0:T(8,128)(2,1)S(1)} %add_convert_fusion), channel_id=1, source_target_pairs={{0,8},{4,12},{8,0},{12,4},{1,9},{5,13},{9,1},{13,5},{2,10},{6,14},... | collective-permute-start | bytes 786440 | tf_op jit(solution)/shard_map/ppermute | solution.py:223
  98.4 3.3 %collective-permute-start.6 = (bf16[128,1024]{1,0:T(8,128)(2,1)S(1)}, bf16[128,1024]{1,0:T(8,128)(2,1)S(1)}, u32[]{:S(2)}, u32[]{:S(2)}) collective-permute-start(bf16[128,1024]{1,0:T(8,128)(2,1)S(1)} %add_convert_fusion), channel_id=1, source_target_pairs={{0,12},{4,8},{8,4},{12,0},{1,13},{5,9},{9,5},{13,1},{2,14},{6,10},... | collective-permute-start | bytes 786440 | tf_op jit(solution)/shard_map/ppermute | solution.py:223
  101.7 2.2 %collective-permute-start.7 = (bf16[128,1024]{1,0:T(8,128)(2,1)S(1)}, bf16[128,1024]{1,0:T(8,128)(2,1)S(1)}, u32[]{:S(2)}, u32[]{:S(2)}) collective-permute-start(bf16[128,1024]{1,0:T(8,128)(2,1)S(1)} %add_convert_fusion), channel_id=1, source_target_pairs={{0,4},{4,0},{8,12},{12,8},{1,5},{5,1},{9,13},{13,9},{2,6},{6,2},{1... | collective-permute-start | bytes 786440 | tf_op jit(solution)/shard_map/ppermute | solution.py:223
  104.0 0.0 all-to-all-done.came
  104.0 0.8 shard_map.89
  104.8 5.2 %all-to-all-start.1 = ((bf16[4,32,1024]{2,1,0:T(8,128)(2,1)}), bf16[4,32,1024]{2,1,0:T(8,128)(2,1)S(1)}, u32[]{:S(2)}, u32[]{:S(2)}) async-start(bf16[4,32,1024]{2,1,0:T(8,128)(2,1)} %bitcast.15), calls=%async_computation.1 | async-start | bytes 524288 | tf_op jit(solution)/shard_map/all_to_all | solution.py:327
  110.1 0.0 collective-permute-done.5
  110.1 1.0 collective-permute-done.6
  111.1 0.0 collective-permute-done.7
  111.2 0.0 copy-start.1
  111.2 0.0 copy-start.2
  111.2 16.6 %all-to-all-done.1 = bf16[4,32,1024]{2,1,0:T(8,128)(2,1)S(1)} async-done(((bf16[4,32,1024]{2,1,0:T(8,128)(2,1)}), bf16[4,32,1024]{2,1,0:T(8,128)(2,1)S(1)}, u32[]{:S(2)}, u32[]{:S(2)}) %all-to-all-start.1) | async-done | bytes 262176 | tf_op jit(solution)/shard_map/all_to_all | solution.py:327
  127.8 0.7 fusion.8
  128.5 0.0 copy-done.1
  128.5 0.0 copy-done.2
  (9 shorter events, 0.2 us)
Async XLA Ops:
  44.2 1.0 copy-start
  48.7 7.1 %collective-permute-start = (f32[3,512]{1,0:T(4,128)S(1)}, f32[3,512]{1,0:T(4,128)S(1)}, u32[]{:S(2)}, u32[]{:S(2)}) collective-permute-start(f32[3,512]{1,0:T(4,128)S(1)} %get-tuple-element.14.stats), channel_id=1, source_target_pairs={{0,4},{4,8},{8,12},{12,0},{1,5},{5,9},{9,13},{13,1},{2,6},{6,10},{... | collective-permute-start | bytes 18440 | tf_op jit(solution)/shard_map/ppermute | solution.py:267
  52.2 5.5 %collective-permute-start.1 = (f32[3,512]{1,0:T(4,128)S(1)}, f32[3,512]{1,0:T(4,128)S(1)}, u32[]{:S(2)}, u32[]{:S(2)}) collective-permute-start(f32[3,512]{1,0:T(4,128)S(1)} %get-tuple-element.14.stats), channel_id=1, source_target_pairs={{0,12},{4,0},{8,4},{12,8},{1,13},{5,1},{9,5},{13,9},{2,14},{6,2},{... | collective-permute-start | bytes 18440 | tf_op jit(solution)/shard_map/ppermute | solution.py:267
  61.7 5.3 %collective-permute-start.8 = (bf16[512,1024]{1,0:T(8,128)(2,1)}, bf16[512,1024]{1,0:T(8,128)(2,1)S(1)}, u32[]{:S(2)}, u32[]{:S(2)}) collective-permute-start(bf16[512,1024]{1,0:T(8,128)(2,1)} %get-tuple-element.23), channel_id=1, source_target_pairs={{0,16},{16,0},{32,48},{48,32},{64,80},{80,64},{96,112},{112,96},{1... | collective-permute-start | bytes 3145736 | tf_op jit(solution)/shard_map/ppermute | solution.py:291
  68.1 35.8 %all-to-all-start = ((bf16[4,128,1024]{2,1,0:T(8,128)(2,1)}), bf16[4,128,1024]{2,1,0:T(8,128)(2,1)S(1)}, u32[]{:S(2)}, u32[]{:S(2)}) async-start(bf16[4,128,1024]{2,1,0:T(8,128)(2,1)} %bitcast.44), calls=%async_computation | async-start | bytes 2097152 | tf_op jit(solution)/shard_map/all_to_all | solution.py:299
  75.4 12.8 %collective-permute-start.2 = (bf16[128,1024]{1,0:T(8,128)(2,1)}, bf16[128,1024]{1,0:T(8,128)(2,1)S(1)}, u32[]{:S(2)}, u32[]{:S(2)}) collective-permute-start(bf16[128,1024]{1,0:T(8,128)(2,1)} %get-tuple-element.19), channel_id=1, source_target_pairs={{0,8},{4,12},{8,0},{12,4},{1,9},{5,13},{9,1},{13,5},{2,10},{6,14},... | collective-permute-start | bytes 786440 | tf_op jit(solution)/shard_map/ppermute | solution.py:223
  80.2 13.4 %collective-permute-start.3 = (bf16[128,1024]{1,0:T(8,128)(2,1)}, bf16[128,1024]{1,0:T(8,128)(2,1)S(1)}, u32[]{:S(2)}, u32[]{:S(2)}) collective-permute-start(bf16[128,1024]{1,0:T(8,128)(2,1)} %get-tuple-element.20), channel_id=1, source_target_pairs={{0,4},{4,0},{8,12},{12,8},{1,5},{5,1},{9,13},{13,9},{2,6},{6,2},{1... | collective-permute-start | bytes 786440 | tf_op jit(solution)/shard_map/ppermute | solution.py:223
  82.9 11.6 %collective-permute-start.4 = (bf16[128,1024]{1,0:T(8,128)(2,1)}, bf16[128,1024]{1,0:T(8,128)(2,1)S(1)}, u32[]{:S(2)}, u32[]{:S(2)}) collective-permute-start(bf16[128,1024]{1,0:T(8,128)(2,1)} %get-tuple-element.21), channel_id=1, source_target_pairs={{0,12},{4,8},{8,4},{12,0},{1,13},{5,9},{9,5},{13,1},{2,14},{6,10},... | collective-permute-start | bytes 786440 | tf_op jit(solution)/shard_map/ppermute | solution.py:223
  94.7 15.4 %collective-permute-start.5 = (bf16[128,1024]{1,0:T(8,128)(2,1)S(1)}, bf16[128,1024]{1,0:T(8,128)(2,1)S(1)}, u32[]{:S(2)}, u32[]{:S(2)}) collective-permute-start(bf16[128,1024]{1,0:T(8,128)(2,1)S(1)} %add_convert_fusion), channel_id=1, source_target_pairs={{0,8},{4,12},{8,0},{12,4},{1,9},{5,13},{9,1},{13,5},{2,10},{6,14},... | collective-permute-start | bytes 786440 | tf_op jit(solution)/shard_map/ppermute | solution.py:223
  98.4 12.7 %collective-permute-start.6 = (bf16[128,1024]{1,0:T(8,128)(2,1)S(1)}, bf16[128,1024]{1,0:T(8,128)(2,1)S(1)}, u32[]{:S(2)}, u32[]{:S(2)}) collective-permute-start(bf16[128,1024]{1,0:T(8,128)(2,1)S(1)} %add_convert_fusion), channel_id=1, source_target_pairs={{0,12},{4,8},{8,4},{12,0},{1,13},{5,9},{9,5},{13,1},{2,14},{6,10},... | collective-permute-start | bytes 786440 | tf_op jit(solution)/shard_map/ppermute | solution.py:223
  101.7 9.5 %collective-permute-start.7 = (bf16[128,1024]{1,0:T(8,128)(2,1)S(1)}, bf16[128,1024]{1,0:T(8,128)(2,1)S(1)}, u32[]{:S(2)}, u32[]{:S(2)}) collective-permute-start(bf16[128,1024]{1,0:T(8,128)(2,1)S(1)} %add_convert_fusion), channel_id=1, source_target_pairs={{0,4},{4,0},{8,12},{12,8},{1,5},{5,1},{9,13},{13,9},{2,6},{6,2},{1... | collective-permute-start | bytes 786440 | tf_op jit(solution)/shard_map/ppermute | solution.py:223
  104.8 23.0 %all-to-all-start.1 = ((bf16[4,32,1024]{2,1,0:T(8,128)(2,1)}), bf16[4,32,1024]{2,1,0:T(8,128)(2,1)S(1)}, u32[]{:S(2)}, u32[]{:S(2)}) async-start(bf16[4,32,1024]{2,1,0:T(8,128)(2,1)} %bitcast.15), calls=%async_computation.1 | async-start | bytes 524288 | tf_op jit(solution)/shard_map/all_to_all | solution.py:327
  111.2 17.3 %copy-start.1 = (bf16[4,128,512]{2,1,0:T(8,128)(2,1)}, bf16[4,128,512]{2,1,0:T(8,128)(2,1)S(1)}, u32[]{:S(2)}) copy-start(bf16[4,128,512]{2,1,0:T(8,128)(2,1)S(1)} %get-tuple-element.24) | copy-start | bytes 1572868
  111.2 17.3 %copy-start.2 = (bf16[4,128,512]{2,1,0:T(8,128)(2,1)}, bf16[4,128,512]{2,1,0:T(8,128)(2,1)S(1)}, u32[]{:S(2)}) copy-start(bf16[4,128,512]{2,1,0:T(8,128)(2,1)S(1)} %get-tuple-element.25) | copy-start | bytes 1572868
